TPU v7x, 32 devices: a whole 2x2x4 slice. The times are simulated.
32 devices in a mesh: lat: 8 (over y, x, core), lon: 4 (over z).
Axes of the slice: x: 2, y: 2, z: 4, core: 2. Of those that a mesh axis runs over, the one named last changes fastest.
Arguments:
- level_fields: float32 [2, 2, 640, 2560], P(None, None, 'lat', 'lon'), may hold values from -6 to 6
- wind_field: float32 [2, 2, 640, 2560], P(None, None, 'lat', 'lon'), may hold values from -6 to 6
- zonal_step: float32 [640], P('lat'), may hold values from 0.1 to 1
- quad_weight: float32 [640], P('lat'), may hold values from 0.005 to 0.05
- legendre: bfloat16 [640, 640, 640], P('lon', 'lat'), may hold values from -6 to 6
- wave_table: int32 [640], replicated, may hold values from 0 to 639, as said below
- damping: float32 [2], replicated, may hold values from 0.5 to 20
- vertical: float32 [2, 2], replicated, may hold values from -4 to 4
Outputs:
- new_fields: float32 [2, 2, 640, 2560], P(None, None, 'lat', 'lon')
- spectrum: float32 [640, 640, 2, 2], P('lat', 'lon')
Inputs may be any that keep to these rules, and one draw needn't show every extreme that they name: `wave_table`: slots 2k and 2k+1 hold wavenumbers p and 639 - p; every wavenumber appears in exactly one slot.
All inputs are finite; a program needn't handle non-finite values.
Results may differ from a plain program's by a relative error of at most 0.0038.
Values may be sent and summed in bfloat16 or wider, within the bound.
No kernel may reach another device: no remote copies, remote signals or barrier semaphores. Data moves between devices by JAX's collectives and lax.ppermute only.
A program may use at most 64 MiB of HBM per device.

v0:
```python
import math

import jax
import jax.numpy as jnp
from jax import lax
from jax.experimental import pallas as pl
from jax.experimental.pallas import tpu as pltpu
from jax.sharding import PartitionSpec as P

NLON = 2560
M = 640


HIGHEST_PRECISION = lax.Precision.HIGHEST


def padded(cells, sides, width):
    for axis, dim in sides:
        count = lax.axis_size(axis)
        head = lax.slice_in_dim(cells, 0, width, axis=dim)
        tail = lax.slice_in_dim(cells, cells.shape[dim] - width, cells.shape[dim], axis=dim)
        cells = jnp.concatenate(
            [
                lax.ppermute(tail, axis, [(i, (i + 1) % count) for i in range(count)]),
                cells,
                lax.ppermute(head, axis, [((i + 1) % count, i) for i in range(count)]),
            ],
            axis=dim,
        )
    return cells


def angle_table(waves, columns):
    return (waves[:, None] * columns[None, :] % NLON).astype(jnp.float32) * (2.0 * math.pi / NLON)


def correct(spectrum, degrees, damping, vertical):
    modal = jnp.einsum("kl,nmcl->nmck", vertical, spectrum, precision=HIGHEST_PRECISION)
    divisor = 1.0 + damping[None, :] * (degrees * (degrees + 1)).astype(jnp.float32)[
        :, None
    ] / float(M * M)
    modal = modal / divisor[:, None, None, :]
    return jnp.einsum("kl,nmck->nmcl", vertical, modal, precision=HIGHEST_PRECISION)


def untiled(
    level_fields, wind_field, zonal_step, quad_weight, legendre, wave_table, damping, vertical
):
    levels, hemis, rows_half, lon_dev = level_fields.shape
    slots_dev = legendre.shape[0]
    lat_count = lax.axis_size("lat")
    lat_index = lax.axis_index("lat")
    lon_index = lax.axis_index("lon")
    degree_dev = M // lat_count
    grid_count = levels * hemis * rows_half
    contract_last = (((1,), (1,)), ((), ()))
    contract_first = (((0,), (0,)), ((), ()))
    batch_slots = (((2,), (1,)), ((0,), (0,)))
    extended = padded(level_fields, (("lat", 2), ("lon", 3)), 1)
    eastward = extended[:, :, 1:-1, 2:]
    westward = extended[:, :, 1:-1, :-2]
    toward = extended[:, :, 2:, 1:-1]
    poleward = extended[:, :, :-2, 1:-1]
    row_number = jnp.arange(rows_half)
    at_equator = (row_number == rows_half - 1) & (lat_index == lat_count - 1)
    toward = jnp.where(at_equator[:, None], level_fields[:, ::-1, -1:, :], toward)
    at_pole = (row_number == 0) & (lat_index == 0)
    poleward = jnp.where(at_pole[:, None], 0.0, poleward)
    tendency = wind_field[0] * zonal_step[:, None] * (eastward - westward) + 0.25 * wind_field[
        1
    ] * (toward - poleward)
    stepped = level_fields - tendency
    my_waves = lax.dynamic_slice_in_dim(wave_table, lon_index * slots_dev, slots_dev)
    portion = lax.all_gather(stepped, "lon", axis=3, tiled=True)
    lon_width = portion.shape[3]
    columns = jnp.arange(lon_width, dtype=jnp.int32)
    angles = angle_table(my_waves, columns)
    values = portion.reshape(grid_count, lon_width)
    cosine_sum = lax.dot_general(
        jnp.cos(angles), values, contract_last, precision=HIGHEST_PRECISION
    )
    sine_sum = lax.dot_general(jnp.sin(angles), values, contract_last, precision=HIGHEST_PRECISION)
    cosine_sum, sine_sum = (cosine_sum, sine_sum)
    fourier = jnp.stack([cosine_sum, -sine_sum], axis=1) / math.sqrt(NLON)
    weighted = (fourier.reshape(slots_dev, 2, levels, hemis, rows_half) * quad_weight).astype(
        jnp.bfloat16
    )
    weighted = weighted.reshape(slots_dev, 2 * levels * hemis, rows_half)
    table_part = legendre
    summed = lax.dot_general(weighted, table_part, batch_slots, preferred_element_type=jnp.float32)
    summed = summed.reshape(slots_dev, 2, levels, hemis, degree_dev * lax.axis_size("lat"))
    degrees = jnp.arange(degree_dev * lax.axis_size("lat"), dtype=jnp.int32)
    parity = jnp.where((degrees[None, :] - my_waves[:, None]) % 2 == 0, 1.0, -1.0)
    kept_mask = degrees[None, :] >= my_waves[:, None]
    combined = summed[:, :, :, 0] + parity[:, None, None, :] * summed[:, :, :, 1]
    combined = jnp.where(kept_mask[:, None, None, :], combined, 0.0)
    raw = lax.psum_scatter(combined.transpose(3, 0, 1, 2), "lat", scatter_dimension=0, tiled=True)
    my_degrees = lat_index * degree_dev + jnp.arange(degree_dev, dtype=jnp.int32)
    spectrum = correct(raw, my_degrees, damping, vertical)
    portion = lax.all_gather(spectrum.astype(jnp.bfloat16), "lat", axis=0, tiled=True)
    row_count = portion.shape[0]
    table_part = legendre
    degrees = jnp.arange(row_count, dtype=jnp.int32)
    even_mask = ((degrees[None, :] - my_waves[:, None]) % 2 == 0)[:, :, None]
    arranged = portion.transpose(1, 0, 2, 3).reshape(slots_dev, row_count, 2 * levels)
    even_sum = lax.dot_general(
        table_part,
        jnp.where(even_mask, arranged, 0),
        batch_slots,
        preferred_element_type=jnp.float32,
    )
    odd_sum = lax.dot_general(
        table_part,
        jnp.where(even_mask, 0, arranged),
        batch_slots,
        preferred_element_type=jnp.float32,
    )
    even_sum, odd_sum = (even_sum, odd_sum)
    coefs = jnp.stack([even_sum + odd_sum, even_sum - odd_sum], axis=1) / math.sqrt(M)
    coefs = (
        coefs.reshape(slots_dev, 2, rows_half, 2, levels)
        .transpose(0, 3, 4, 1, 2)
        .reshape(slots_dev, 2, grid_count)
    )
    my_columns = lon_index * lon_dev + jnp.arange(lon_dev, dtype=jnp.int32)
    portion = lax.all_gather(coefs, "lon", axis=0, tiled=True)
    factor = jnp.where(wave_table == 0, 1.0, 2.0)[:, None]
    angles = angle_table(wave_table, my_columns)
    totals = lax.dot_general(
        portion[:, 0], jnp.cos(angles) * factor, contract_first, precision=HIGHEST_PRECISION
    )
    grid_out = totals - lax.dot_general(
        portion[:, 1], jnp.sin(angles) * factor, contract_first, precision=HIGHEST_PRECISION
    )
    new_fields = (grid_out / math.sqrt(NLON)).reshape(level_fields.shape)
    return (new_fields, spectrum)


UNIT = 32
CUTS = (64, 96)
GROUP = 16
LANES = 128
F32 = jnp.float32
BF16 = jnp.bfloat16


def split_halves(value):
    high = value.astype(BF16)
    return high, (value - high.astype(F32)).astype(BF16)


def dot_rows(left, right):
    return lax.dot_general(left, right, (((1,), (1,)), ((), ())), preferred_element_type=F32)


def dot_columns(left, right):
    return lax.dot_general(left, right, (((0,), (0,)), ((), ())), preferred_element_type=F32)


def pairs(count, step):
    return [(i, i ^ step) for i in range(count)]


def edges_kernel(fields_ref, first_row, last_row, first_column, last_column):
    count, rows, columns = fields_ref.shape
    for p in range(count):
        first_row[p : p + 1, :] = fields_ref[p, 0:1, :]
        last_row[p : p + 1, :] = fields_ref[p, rows - 1 : rows, :]
        first_column[:, p : p + 1] = fields_ref[p, :, 0:1]
        last_column[:, p : p + 1] = fields_ref[p, :, columns - 1 : columns]


def advance(flags, fields_ref, wind_ref, step_ref, above, below, before, after, stepped_ref):
    count, rows, columns = fields_ref.shape
    lane = lax.broadcasted_iota(jnp.int32, (rows, columns), 1)
    row = lax.broadcasted_iota(jnp.int32, (rows, columns), 0)
    for p in range(count):
        h = p % 2
        field = fields_ref[p]
        eastward = jnp.where(
            lane == columns - 1, after[:, p : p + 1], pltpu.roll(field, columns - 1, 1)
        )
        westward = jnp.where(lane == 0, before[:, p : p + 1], pltpu.roll(field, 1, 1))
        other = fields_ref[p ^ 1, rows - 1 : rows, :]
        low_edge = jnp.where(flags[1] == 1, other, below[p : p + 1, :])
        high_edge = jnp.where(flags[0] == 1, 0.0, above[p : p + 1, :])
        toward = jnp.where(row == rows - 1, low_edge, pltpu.roll(field, rows - 1, 0))
        poleward = jnp.where(row == 0, high_edge, pltpu.roll(field, 1, 0))
        tendency = wind_ref[h] * step_ref[...] * (eastward - westward) + 0.25 * wind_ref[
            2 + h
        ] * (toward - poleward)
        stepped_ref[p * rows : (p + 1) * rows, :] = field - tendency


def table_rows(near, far, first, share, blocks, part):
    per_block = near.shape[0] // blocks
    half = far.shape[1] // 2
    out = []
    for k in range(blocks):
        at = pl.ds(k * per_block + first, share)
        near_cos, near_sin = near[at, :LANES], near[at, LANES:]
        far_cos, far_sin = far[at, :half], far[at, half:]
        columns = []
        for j in range(half):
            c, s = far_cos[:, j : j + 1], far_sin[:, j : j + 1]
            if part:
                columns.append(-(s * near_cos + c * near_sin))
            else:
                columns.append(c * near_cos - s * near_sin)
        out.append(jnp.concatenate(columns, axis=1))
    return jnp.concatenate(out, axis=0)


def zonal_sums(blocks, share, first, stepped_ref, near, far, outs):
    high, low = split_halves(stepped_ref[...])
    count = stepped_ref.shape[0]
    for part in range(2):
        rows_high, rows_low = split_halves(table_rows(near, far, first, share, blocks, part))
        sums = dot_rows(rows_high, high) + (dot_rows(rows_high, low) + dot_rows(rows_low, high))
        for k, out in enumerate(outs):
            out[:, part * count : (part + 1) * count] = sums[
                k * share : (k + 1) * share, :
            ].astype(out.dtype)


def forward_kernel(
    blocks, sections, rows, degree_dev, last, waves_ref, place_ref, *refs
):
    received = refs[:blocks]
    weight_ref, table_ref = refs[blocks : blocks + 2]
    rest = refs[blocks + 2 :]
    spread_ref, kept_ref, turned_ref = rest[-3:]
    step = pl.program_id(0)
    half = sections // 2
    levels = half // 2
    group = table_ref.shape[0]
    columns = table_ref.shape[2]
    share = spread_ref.shape[0]

    @pl.when(step == 0)
    def _():
        total = received[0][...].astype(F32)
        for other in received[1:]:
            total = total + other[...].astype(F32)
        total = total * weight_ref[...]
        for c in range(2):
            for level in range(levels):
                for h in range(2):
                    at = ((c * levels + level) * 2 + h) * rows
                    spread_ref[:, h * half + level * 2 + c, 0:rows] = total[:, at : at + rows]

    degree = lax.broadcasted_iota(jnp.int32, (2 * half, columns), 1)
    row = lax.broadcasted_iota(jnp.int32, (2 * half, 1), 0)
    for u in range(0, group, 2):
        sums = []
        for v in (u, u + 1):
            high, low = split_halves(spread_ref[step * group + v, :, 0:rows])
            both = jnp.concatenate([high.astype(F32), low.astype(F32)], axis=0).astype(BF16)
            total = jnp.dot(both, table_ref[v], preferred_element_type=F32)
            sums.append(total[:sections] + total[sections:])
        north = jnp.concatenate([sums[0][:half], sums[1][:half]], axis=0)
        south = jnp.concatenate([sums[0][half:], sums[1][half:]], axis=0)
        slot = step * group + u
        past = degree - jnp.where(row < half, waves_ref[slot], waves_ref[slot + 1])
        combined = north + jnp.where(past & 1 == 0, south, -south)
        combined = jnp.where(past >= 0, combined, 0.0)
        at = pl.ds(pl.multiple_of(slot * half, 2 * half), 2 * half)
        for t in range(columns // LANES):
            kept_ref[t, at, :] = combined[:, t * LANES : (t + 1) * LANES]

    @pl.when(step == pl.num_programs(0) - 1)
    def _():
        target = turned_ref if last else rest[0]
        for t in range(columns // LANES):
            tile = jnp.concatenate(
                [kept_ref[t, pl.ds(j, share, stride=half), :] for j in range(half)], axis=0
            )
            target[t * LANES : (t + 1) * LANES, :] = tile.T
        if not last:
            return
        earlier, (own_ref, other_ref) = rest[:-5], rest[-5:-3]
        for j in range(own_ref.shape[0]):
            for out, k in ((own_ref, 2 * j), (other_ref, 2 * j + 1)):
                at = pl.ds(pl.multiple_of((place_ref[0] ^ k) * degree_dev, 8), degree_dev)
                done = 0
                for source in (*earlier, turned_ref):
                    wide = source.shape[1]
                    out[j, :, done : done + wide] = source[at, :]
                    done += wide


def correct_kernel(
    cuts, levels, place_ref, damping_ref, vertical_ref, sum_ref, *refs
):
    others, (rounded_ref, spectrum_ref) = refs[:-2], refs[-2:]
    total = sum_ref[...]
    for other in others:
        total = total + other[...].astype(F32)
    count = total.shape[0]
    degree = place_ref[0] * count + lax.broadcasted_iota(jnp.int32, (count, 1), 0)
    growth = (degree * (degree + 1)).astype(F32) / float(M * M)
    scale = [1.0 / (1.0 + damping_ref[k] * growth) for k in range(levels)]
    at, slot = 0, 0
    for share in cuts:
        wide = 2 * share
        raw = [total[:, at + l * wide : at + (l + 1) * wide] for l in range(levels)]
        modal = [
            sum(vertical_ref[k, l] * raw[l] for l in range(levels)) * scale[k]
            for k in range(levels)
        ]
        for l in range(levels):
            value = sum(vertical_ref[k, l] * modal[k] for k in range(levels))
            rounded_ref[:, at + l * wide : at + (l + 1) * wide] = value.astype(BF16)
            for c in range(2):
                spectrum_ref[c * levels + l, :, slot : slot + share] = value[
                    :, c * share : (c + 1) * share
                ]
        at, slot = at + levels * wide, slot + share


def inverse_kernel(sections, rows, first, waves_ref, joined_ref, table_ref, out_ref, kept_ref, spread_ref):
    step = pl.program_id(0)
    half = sections // 2
    levels = half // 2
    group = table_ref.shape[0]
    columns = table_ref.shape[2]
    share = spread_ref.shape[0]

    @pl.when(step == 0)
    def _():
        for t in range(columns // LANES):
            tile = joined_ref[t * LANES : (t + 1) * LANES, half * first : half * (first + share)]
            turned = tile.astype(F32).T
            for j in range(half):
                kept_ref[t, pl.ds(j, share, stride=half), :] = turned[
                    j * share : (j + 1) * share, :
                ]

    degree = lax.broadcasted_iota(jnp.int32, (2 * half, columns), 1)
    row = lax.broadcasted_iota(jnp.int32, (2 * half, 1), 0)
    upper = row < half
    for u in range(0, group, 2):
        slot = step * group + u
        at = pl.ds(pl.multiple_of(slot * half, 2 * half), 2 * half)
        values = jnp.concatenate(
            [kept_ref[t, at, :] for t in range(columns // LANES)], axis=1
        )
        even = (degree - jnp.where(upper, waves_ref[slot], waves_ref[slot + 1])) & 1 == 0
        evens = jnp.where(even, values, 0.0)
        odds = pltpu.roll(jnp.where(even, 0.0, values), half, 0)
        for v in range(2):
            both = jnp.where(upper, odds, evens) if v else jnp.where(upper, evens, odds)
            sums = dot_rows(both.astype(BF16), table_ref[u + v])
            factor = jnp.where(waves_ref[slot + v] == 0, 1.0, 2.0) / math.sqrt(M)
            sums = sums * factor
            swapped = pltpu.roll(sums, half, 0)
            less = sums - swapped if v else swapped - sums
            spread_ref[slot + v, :, 0:rows] = jnp.where(upper, sums + swapped, less)

    @pl.when(step == pl.num_programs(0) - 1)
    def _():
        for c in range(2):
            for level in range(levels):
                for h in range(2):
                    at = ((c * levels + level) * 2 + h) * rows
                    out_ref[:, at : at + rows] = spread_ref[
                        :, h * half + level * 2 + c, 0:rows
                    ].astype(out_ref.dtype)


def zonal_values(blocks, share, first, near, far, received, total):
    for part in range(2):
        count = received[0].shape[1] // 2
        rows_high, rows_low = split_halves(table_rows(near, far, first, share, blocks, part))
        coefs = jnp.concatenate(
            [other[:, part * count : (part + 1) * count] for other in received], axis=0
        )
        term = dot_columns(coefs, rows_high) + dot_columns(coefs, rows_low)
        total = term if total is None else total + term
    return total


VMEM = pl.BlockSpec(memory_space=pltpu.VMEM)
SMEM = pl.BlockSpec(memory_space=pltpu.SMEM)


def grant(size):
    return pltpu.CompilerParams(vmem_limit_bytes=size << 20)


def like(shape, dtype):
    return jax.ShapeDtypeStruct(shape, dtype)


def whole_block(shape):
    return pl.BlockSpec(shape, lambda *_: (0,) * len(shape))


def shards(
    level_fields, wind_field, zonal_step, quad_weight, legendre, wave_table, damping, vertical
):
    levels, hemis, rows_half, lon_dev = level_fields.shape
    slots_dev, _, columns = legendre.shape
    lat_count = lax.axis_size("lat")
    lon_count = lax.axis_size("lon")
    degree_dev = columns // lat_count
    if (
        rows_half % 16
        or degree_dev % 16
        or lon_dev % LANES
        or slots_dev != sum(CUTS)
        or levels != 2
        or lat_count & (lat_count - 1)
        or lat_count < 4
        or lon_count & (lon_count - 1)
    ):
        return untiled(
            level_fields,
            wind_field,
            zonal_step,
            quad_weight,
            legendre,
            wave_table,
            damping,
            vertical,
        )
    lat_index = lax.axis_index("lat")
    lon_index = lax.axis_index("lon")
    planes = levels * hemis
    grid_count = planes * rows_half
    sections = 2 * planes
    half = sections // 2
    width = 2 * grid_count
    fields = level_fields.reshape(planes, rows_half, lon_dev)
    winds = wind_field.reshape(2 * hemis, rows_half, lon_dev)

    first_row, last_row, first_column, last_column = pl.pallas_call(
        edges_kernel,
        out_shape=[like((planes, lon_dev), F32)] * 2 + [like((rows_half, planes), F32)] * 2,
        in_specs=[VMEM],
        out_specs=[VMEM] * 4,
        compiler_params=grant(8),
        name="edges",
    )(fields)
    up = [(i, (i + 1) % lat_count) for i in range(lat_count)]
    east = [(i, (i + 1) % lon_count) for i in range(lon_count)]
    down = [(j, i) for i, j in up]
    west = [(j, i) for i, j in east]
    above = lax.ppermute(last_row, "lat", up)
    below = lax.ppermute(first_row, "lat", down)
    before = lax.ppermute(last_column, "lon", east)
    after = lax.ppermute(first_column, "lon", west)

    order = [
        lax.dynamic_slice_in_dim(wave_table, (lon_index ^ k) * slots_dev, slots_dev)
        for k in range(lon_count)
    ]
    my_waves = order[0]
    waves = jnp.concatenate(order)
    near_angle = angle_table(waves, jnp.arange(LANES, dtype=jnp.int32))
    near = jnp.concatenate([jnp.cos(near_angle), jnp.sin(near_angle)], axis=1)
    far_angle = angle_table(
        waves, lon_index * lon_dev + LANES * jnp.arange(lon_dev // LANES, dtype=jnp.int32)
    )
    far = jnp.concatenate([jnp.cos(far_angle), jnp.sin(far_angle)], axis=1) / math.sqrt(NLON)

    flags = jnp.stack([lat_index == 0, lat_index == lat_count - 1]).astype(jnp.int32)
    place = lat_index.astype(jnp.int32).reshape(1)
    weight_row = jnp.tile(quad_weight, sections)[None, :]

    def sums_shape(share):
        return [like((share, width), BF16 if k else F32) for k in range(lon_count)]

    def first_sums(flags_ref, fields_ref, winds_ref, step_ref, *refs):
        edges, near_ref, far_ref, stepped_ref = refs[:4], refs[4], refs[5], refs[6]
        advance(flags_ref, fields_ref, winds_ref, step_ref, *edges, stepped_ref)
        zonal_sums(lon_count, CUTS[0], 0, stepped_ref, near_ref, far_ref, refs[7:])

    stepped, *pieces = pl.pallas_call(
        first_sums,
        out_shape=[like((grid_count, lon_dev), F32)] + sums_shape(CUTS[0]),
        in_specs=[SMEM] + [VMEM] * 9,
        out_specs=[VMEM] * (1 + lon_count),
        compiler_params=grant(24),
        name="advance_and_sums",
    )(flags, fields, winds, zonal_step[:, None], above, below, before, after, near, far)

    def later_sums(share, first):
        def body(stepped_ref, near_ref, far_ref, *outs):
            zonal_sums(lon_count, share, first, stepped_ref, near_ref, far_ref, outs)

        return pl.pallas_call(
            body,
            out_shape=sums_shape(share),
            in_specs=[VMEM] * 3,
            out_specs=[VMEM] * lon_count,
            compiler_params=grant(24),
            name="sums",
        )(stepped, near, far)

    def swap_lon(parts):
        return [parts[0]] + [
            lax.ppermute(parts[k], "lon", pairs(lon_count, k)) for k in range(1, lon_count)
        ]

    swapped, first = [swap_lon(pieces)], CUTS[0]
    for share in CUTS[1:]:
        swapped.append(swap_lon(later_sums(share, first)))
        first += share

    def table_spec(first):
        return pl.BlockSpec(
            (GROUP, rows_half, columns), lambda g, *_: (first // GROUP + g, 0, 0)
        )

    def forward(first, share, parts, earlier, last):
        if last:
            shape = (lat_count // 2, degree_dev, half * slots_dev)
            shapes = [like(shape, F32)] * 2
        else:
            shapes = [like((columns, half * share), F32)]
        return pl.pallas_call(
            lambda *refs: forward_kernel(
                lon_count, sections, rows_half, degree_dev, last, *refs
            ),
            out_shape=shapes,
            grid_spec=pltpu.PrefetchScalarGridSpec(
                num_scalar_prefetch=2,
                grid=(share // GROUP,),
                in_specs=[whole_block((share, width))] * lon_count
                + [whole_block((1, width)), table_spec(first)]
                + [whole_block(other.shape) for other in earlier],
                out_specs=[whole_block(shape.shape) for shape in shapes],
                scratch_shapes=[
                    pltpu.VMEM((share, sections, LANES), F32),
                    pltpu.VMEM((columns // LANES, half * share, LANES), F32),
                    pltpu.VMEM((columns, half * share), F32),
                ],
            ),
            compiler_params=grant(50),
            name="forward",
        )(my_waves[first : first + share], place, *parts, weight_row, legendre, *earlier)

    earlier, first = [], 0
    for share, parts in zip(CUTS, swapped):
        last = first + share == slots_dev
        earlier = earlier + list(forward(first, share, parts, earlier if last else [], last))
        first += share
    own, other = earlier[-2:]

    other = lax.ppermute(other, "lat", pairs(lat_count, 1))
    sums = [own[j] + other[j] for j in range(lat_count // 2)]
    sums = [sums[0]] + [
        lax.ppermute(sums[j].astype(BF16), "lat", pairs(lat_count, 2 * j))
        for j in range(1, lat_count // 2)
    ]
    rounded, spectrum = pl.pallas_call(
        lambda *refs: correct_kernel(CUTS, levels, *refs),
        out_shape=[
            like((degree_dev, half * slots_dev), BF16),
            like((half, degree_dev, slots_dev), F32),
        ],
        in_specs=[SMEM] * 3 + [VMEM] * len(sums),
        out_specs=[VMEM] * 2,
        compiler_params=grant(8),
        name="correct",
    )(place, damping, vertical, *sums)
    joined = lax.all_gather(rounded, "lat", axis=0, tiled=True)

    def inverse(first, share):
        return pl.pallas_call(
            lambda *refs: inverse_kernel(sections, rows_half, first, *refs),
            out_shape=like((share, width), BF16),
            grid_spec=pltpu.PrefetchScalarGridSpec(
                num_scalar_prefetch=1,
                grid=(share // GROUP,),
                in_specs=[whole_block(joined.shape), table_spec(first)],
                out_specs=whole_block((share, width)),
                scratch_shapes=[
                    pltpu.VMEM((columns // LANES, half * share, LANES), F32),
                    pltpu.VMEM((share, sections, LANES), F32),
                ],
            ),
            compiler_params=grant(50),
            name="inverse",
        )(my_waves[first : first + share], joined, legendre)

    def values(first, share, parts, base):
        def body(near_ref, far_ref, *refs):
            start = refs[lon_count][...] if base else None
            refs[-1][...] = zonal_values(
                lon_count, share, first, near_ref, far_ref, refs[:lon_count], start
            )

        return pl.pallas_call(
            body,
            out_shape=like((grid_count, lon_dev), F32),
            in_specs=[VMEM] * (2 + lon_count + len(base)),
            out_specs=VMEM,
            compiler_params=grant(24),
            name="values",
        )(near, far, *parts, *base)

    base, first = [], 0
    for share in CUTS:
        coefs = inverse(first, share)
        base = [values(first, share, swap_lon([coefs] * lon_count), base)]
        first += share
    spectrum = spectrum.reshape(2, levels, degree_dev, slots_dev).transpose(2, 3, 0, 1)
    return (base[0].reshape(level_fields.shape), spectrum)


def solution(mesh):
    return jax.shard_map(
        shards,
        mesh=mesh,
        in_specs=(
            P(None, None, "lat", "lon"),
            P(None, None, "lat", "lon"),
            P("lat"),
            P("lat"),
            P("lon", "lat", None),
            P(),
            P(),
            P(),
        ),
        out_specs=(P(None, None, "lat", "lon"), P("lat", "lon", None, None)),
        check_vma=False,
    )
```

profile of v0, /device:TPU:0, one launch (start us, length us, event | category | flops | bytes accessed | tf_op | source)
XLA Modules:
  0.0 115.1 jit_solution(196800504186433307)
XLA Ops:
  0.6 1.1 copy-done
  2.5 2.9 %collective-permute-start.1 = (f32[4,640]{1,0:T(4,128)S(1)}, f32[4,640]{1,0:T(4,128)S(1)}, u32[]{:S(2)}, u32[]{:S(2)}) collective-permute-start(f32[4,640]{1,0:T(4,128)S(1)} %get-tuple-element.20), channel_id=1, source_target_pairs={{4,0},{8,4},{12,8},{16,12},{20,16},{24,20},{28,24},{0,28},{5,1},{9... | collective-permute-start | bytes 30728 | tf_op jit(solution)/shard_map/ppermute | solution.py:450
  5.4 2.3 %collective-permute-start.2 = (f32[80,4]{1,0:T(8,128)S(1)}, f32[80,4]{1,0:T(8,128)S(1)}, u32[]{:S(2)}, u32[]{:S(2)}) collective-permute-start(f32[80,4]{1,0:T(8,128)S(1)} %get-tuple-element.21), channel_id=1, source_target_pairs={{0,1},{1,2},{2,3},{3,0},{4,5},{5,6},{6,7},{7,4},{8,9},{9,10},{10,1... | collective-permute-start | bytes 3848 | tf_op jit(solution)/shard_map/ppermute | solution.py:451
  7.7 2.0 %collective-permute-start.3 = (f32[80,4]{1,0:T(8,128)S(1)}, f32[80,4]{1,0:T(8,128)S(1)}, u32[]{:S(2)}, u32[]{:S(2)}) collective-permute-start(f32[80,4]{1,0:T(8,128)S(1)} %get-tuple-element.22), channel_id=1, source_target_pairs={{1,0},{2,1},{3,2},{0,3},{5,4},{6,5},{7,6},{4,7},{9,8},{10,9},{11,1... | collective-permute-start | bytes 3848 | tf_op jit(solution)/shard_map/ppermute | solution.py:452
  10.7 1.4 %fusion.5 = (f32[640,128]{1,0:T(8,128)S(1)}, f32[640,128]{1,0:T(8,128)S(1)}) fusion(s32[640]{0:T(1024)S(1)} %pad_add_fusion), kind=kLoop, calls=%fused_computation.9 | loop fusion | flops 737280 | bytes 657920 | tf_op jit(solution)/shard_map/cos | solution.py:461
  13.4 1.1 copy-done.1
  14.6 1.1 copy-done.2
  15.7 3.2 %advance_and_sums.1 = (f32[320,640]{1,0:T(8,128)S(1)}, f32[64,640]{1,0:T(8,128)S(1)}, bf16[64,640]{1,0:T(8,128)(2,1)S(1)}, bf16[64,640]{1,0:T(8,128)(2,1)S(1)}, bf16[64,640]{1,0:T(8,128)(2,1)S(1)}) custom-call(s32[2]{0:T(128)S(1)} %add_convert_fusion.flags_ref, f32[4,80,640]{2,1,0:T(8,128)S(1)} %bitcast.20, f32[4,80,640]{2,1,0:T(8,128)S(1)} %bitcast.21, ...), custom_call_target="tpu_custom_call" | custom-call | tf_op jit(solution)/shard_map/advance_and_sums/pallas_call | solution.py:479
  19.0 2.6 %sums.1 = (f32[96,640]{1,0:T(8,128)S(1)}, bf16[96,640]{1,0:T(8,128)(2,1)S(1)}, bf16[96,640]{1,0:T(8,128)(2,1)S(1)}, bf16[96,640]{1,0:T(8,128)(2,1)S(1)}) custom-call(f32[320,640]{1,0:T(8,128)S(1)} %get-tuple-element.23.stepped_ref, f32[640,256]{1,0:T(8,128)S(1)} %pad_maximum_fusion.refs_4_.near_ref, f32[640,10]{1,0:T(8,128)S(1)} %broadcast_multiply_fusion.refs_5_.far_ref), custom_call_target="tpu_custom_call" | custom-call | tf_op jit(solution)/shard_map/sums/pallas_call | solution.py:492
  21.6 2.1 %collective-permute-start.4 = (bf16[96,640]{1,0:T(8,128)(2,1)S(1)}, bf16[96,640]{1,0:T(8,128)(2,1)S(1)}, u32[]{:S(2)}, u32[]{:S(2)}) collective-permute-start(bf16[96,640]{1,0:T(8,128)(2,1)S(1)} %get-tuple-element.25), channel_id=1, source_target_pairs={{0,1},{1,0},{2,3},{3,2},{4,5},{5,4},{6,7},{7,6},{8,9},{9,8},{10,11... | collective-permute-start | bytes 368648 | tf_op jit(solution)/shard_map/ppermute | solution.py:503
  23.7 1.0 collective-permute-start.5
  24.7 1.4 %collective-permute-start.6 = (bf16[96,640]{1,0:T(8,128)(2,1)S(1)}, bf16[96,640]{1,0:T(8,128)(2,1)S(1)}, u32[]{:S(2)}, u32[]{:S(2)}) collective-permute-start(bf16[96,640]{1,0:T(8,128)(2,1)S(1)} %get-tuple-element.27), channel_id=1, source_target_pairs={{0,3},{1,2},{2,1},{3,0},{4,7},{5,6},{6,5},{7,4},{8,11},{9,10},{10,... | collective-permute-start | bytes 368648 | tf_op jit(solution)/shard_map/ppermute | solution.py:503
  26.1 1.7 %collective-permute-start.8 = (bf16[64,640]{1,0:T(8,128)(2,1)S(1)}, bf16[64,640]{1,0:T(8,128)(2,1)S(1)}, u32[]{:S(2)}, u32[]{:S(2)}) collective-permute-start(bf16[64,640]{1,0:T(8,128)(2,1)S(1)} %get-tuple-element.30), channel_id=1, source_target_pairs={{0,2},{1,3},{2,0},{3,1},{4,6},{5,7},{6,4},{7,5},{8,10},{9,11},{10,... | collective-permute-start | bytes 245768 | tf_op jit(solution)/shard_map/ppermute | solution.py:503
  27.8 1.7 %collective-permute-start.9 = (bf16[64,640]{1,0:T(8,128)(2,1)S(1)}, bf16[64,640]{1,0:T(8,128)(2,1)S(1)}, u32[]{:S(2)}, u32[]{:S(2)}) collective-permute-start(bf16[64,640]{1,0:T(8,128)(2,1)S(1)} %get-tuple-element.31), channel_id=1, source_target_pairs={{0,3},{1,2},{2,1},{3,0},{4,7},{5,6},{6,5},{7,4},{8,11},{9,10},{10,... | collective-permute-start | bytes 245768 | tf_op jit(solution)/shard_map/ppermute | solution.py:503
  30.3 11.6 %collective-permute-done.8.refs_4_ = bf16[64,640]{1,0:T(8,128)(2,1)S(1)} collective-permute-done((bf16[64,640]{1,0:T(8,128)(2,1)S(1)}, bf16[64,640]{1,0:T(8,128)(2,1)S(1)}, u32[]{:S(2)}, u32[]{:S(2)}) %collective-permute-start.8) | collective-permute-done | bytes 81952 | tf_op jit(solution)/shard_map/ppermute | solution.py:503
  41.9 5.8 %forward.2.refs_8_ = f32[640,256]{1,0:T(8,128)S(1)} custom-call(s32[64]{0:T(128)S(1)} %slice.33.refs_0_, s32[1]{0:T(128)} %bitcast.refs_1_.refs_0_, f32[64,640]{1,0:T(8,128)S(1)} %get-tuple-element.28.refs_2_, bf16[64,640]{1,0:T(8,128)(2,1)S(1)} %collective-permute-done.7.refs_3_, bf16[64,640]{1,0:T(8,128)(2,1)S(1)} %collective-permute-done.8.refs_4_, ...), custom_call_target="tpu_custom_call" | custom-call | tf_op jit(solution)/shard_map/forward/pallas_call | solution.py:522
  47.8 8.3 %forward.3 = (f32[4,80,640]{2,1,0:T(8,128)S(1)}, f32[4,80,640]{2,1,0:T(8,128)S(1)}) custom-call(s32[96]{0:T(128)S(1)} %slice.32.refs_0_, s32[1]{0:T(128)} %bitcast.refs_1_.refs_0_, f32[96,640]{1,0:T(8,128)S(1)} %get-tuple-element.24.refs_2_, bf16[96,640]{1,0:T(8,128)(2,1)S(1)} %collective-permute-done.4.refs_3_, ...), custom_call_target="tpu_custom_call" | custom-call | tf_op jit(solution)/shard_map/forward/pallas_call | solution.py:522
  56.2 2.3 %collective-permute-done.10 = f32[4,80,640]{2,1,0:T(8,128)S(1)} collective-permute-done((f32[4,80,640]{2,1,0:T(8,128)S(1)}, f32[4,80,640]{2,1,0:T(8,128)S(1)}, u32[]{:S(2)}, u32[]{:S(2)}) %collective-permute-start.10) | collective-permute-done | bytes 819232 | tf_op jit(solution)/shard_map/ppermute | solution.py:551
  58.6 1.5 %collective-permute-start.13 = (bf16[80,640]{1,0:T(8,128)(2,1)S(1)}, bf16[80,640]{1,0:T(8,128)(2,1)S(1)}, u32[]{:S(2)}, u32[]{:S(2)}) collective-permute-start(bf16[80,640]{1,0:T(8,128)(2,1)S(1)} %get-tuple-element.36), channel_id=1, source_target_pairs={{0,24},{4,28},{8,16},{12,20},{16,8},{20,12},{24,0},{28,4},{1,25},{... | collective-permute-start | bytes 307208 | tf_op jit(solution)/shard_map/ppermute | solution.py:554
  60.1 1.5 %collective-permute-start.12 = (bf16[80,640]{1,0:T(8,128)(2,1)S(1)}, bf16[80,640]{1,0:T(8,128)(2,1)S(1)}, u32[]{:S(2)}, u32[]{:S(2)}) collective-permute-start(bf16[80,640]{1,0:T(8,128)(2,1)S(1)} %get-tuple-element.37), channel_id=1, source_target_pairs={{0,16},{4,20},{8,24},{12,28},{16,0},{20,4},{24,8},{28,12},{1,17},{... | collective-permute-start | bytes 307208 | tf_op jit(solution)/shard_map/ppermute | solution.py:554
  62.2 3.1 %collective-permute-done.13.refs_6_ = bf16[80,640]{1,0:T(8,128)(2,1)S(1)} collective-permute-done((bf16[80,640]{1,0:T(8,128)(2,1)S(1)}, bf16[80,640]{1,0:T(8,128)(2,1)S(1)}, u32[]{:S(2)}, u32[]{:S(2)}) %collective-permute-start.13) | collective-permute-done | bytes 102432 | tf_op jit(solution)/shard_map/ppermute | solution.py:554
  65.3 1.4 %collective-permute-done.12.refs_5_ = bf16[80,640]{1,0:T(8,128)(2,1)S(1)} collective-permute-done((bf16[80,640]{1,0:T(8,128)(2,1)S(1)}, bf16[80,640]{1,0:T(8,128)(2,1)S(1)}, u32[]{:S(2)}, u32[]{:S(2)}) %collective-permute-start.12) | collective-permute-done | bytes 102432 | tf_op jit(solution)/shard_map/ppermute | solution.py:554
  67.7 10.7 %all_gather.3.refs_1_ = bf16[640,640]{1,0:T(8,128)(2,1)S(1)} all-gather(bf16[80,640]{1,0:T(8,128)(2,1)S(1)} %get-tuple-element.34), channel_id=1, replica_groups=mesh['lat'=8,'lon'=4] {'lat'}, dimensions={0}, use_global_device_ids=true | all-gather | bytes 921600 | tf_op jit(solution)/shard_map/all_gather | solution.py:568
  78.3 5.9 %inverse.3.refs_0_ = bf16[64,640]{1,0:T(8,128)(2,1)S(1)} custom-call(s32[64]{0:T(128)S(1)} %slice.33.refs_0_, bf16[640,640]{1,0:T(8,128)(2,1)S(1)} %all_gather.3.refs_1_, bf16[160,80,640]{2,1,0:T(8,128)(2,1)} %refs_2_.5), custom_call_target="tpu_custom_call" | custom-call | tf_op jit(solution)/shard_map/inverse/pallas_call | solution.py:571
  84.2 1.8 %collective-permute-start.19 = (bf16[64,640]{1,0:T(8,128)(2,1)S(1)}, bf16[64,640]{1,0:T(8,128)(2,1)S(1)}, u32[]{:S(2)}, u32[]{:S(2)}) collective-permute-start(bf16[64,640]{1,0:T(8,128)(2,1)S(1)} %inverse.3.refs_0_), channel_id=1, source_target_pairs={{0,3},{1,2},{2,1},{3,0},{4,7},{5,6},{6,5},{7,4},{8,11},{9,10},{10,... | collective-permute-start | bytes 245768 | tf_op jit(solution)/shard_map/ppermute | solution.py:503
  86.0 8.2 %inverse.2.refs_0_ = bf16[96,640]{1,0:T(8,128)(2,1)S(1)} custom-call(s32[96]{0:T(128)S(1)} %slice.32.refs_0_, bf16[640,640]{1,0:T(8,128)(2,1)S(1)} %all_gather.3.refs_1_, bf16[160,80,640]{2,1,0:T(8,128)(2,1)} %refs_2_.5), custom_call_target="tpu_custom_call" | custom-call | tf_op jit(solution)/shard_map/inverse/pallas_call | solution.py:571
  94.3 2.1 %collective-permute-start.16 = (bf16[96,640]{1,0:T(8,128)(2,1)S(1)}, bf16[96,640]{1,0:T(8,128)(2,1)S(1)}, u32[]{:S(2)}, u32[]{:S(2)}) collective-permute-start(bf16[96,640]{1,0:T(8,128)(2,1)S(1)} %inverse.2.refs_0_), channel_id=1, source_target_pairs={{0,3},{1,2},{2,1},{3,0},{4,7},{5,6},{6,5},{7,4},{8,11},{9,10},{10,... | collective-permute-start | bytes 368648 | tf_op jit(solution)/shard_map/ppermute | solution.py:503
  96.4 2.3 %collective-permute-start.14 = (bf16[96,640]{1,0:T(8,128)(2,1)S(1)}, bf16[96,640]{1,0:T(8,128)(2,1)S(1)}, u32[]{:S(2)}, u32[]{:S(2)}) collective-permute-start(bf16[96,640]{1,0:T(8,128)(2,1)S(1)} %inverse.2.refs_0_), channel_id=1, source_target_pairs={{0,1},{1,0},{2,3},{3,2},{4,5},{5,4},{6,7},{7,6},{8,9},{9,8},{10,11... | collective-permute-start | bytes 368648 | tf_op jit(solution)/shard_map/ppermute | solution.py:503
  99.4 2.0 %collective-permute-start.17 = (bf16[64,640]{1,0:T(8,128)(2,1)S(1)}, bf16[64,640]{1,0:T(8,128)(2,1)S(1)}, u32[]{:S(2)}, u32[]{:S(2)}) collective-permute-start(bf16[64,640]{1,0:T(8,128)(2,1)S(1)} %inverse.3.refs_0_), channel_id=1, source_target_pairs={{0,1},{1,0},{2,3},{3,2},{4,5},{5,4},{6,7},{7,6},{8,9},{9,8},{10,11... | collective-permute-start | bytes 245768 | tf_op jit(solution)/shard_map/ppermute | solution.py:503
  102.4 8.7 %collective-permute-done.18.refs_2_ = bf16[64,640]{1,0:T(8,128)(2,1)S(1)} collective-permute-done((bf16[64,640]{1,0:T(8,128)(2,1)S(1)}, bf16[64,640]{1,0:T(8,128)(2,1)S(1)}, u32[]{:S(2)}, u32[]{:S(2)}) %collective-permute-start.18) | collective-permute-done | bytes 81952 | tf_op jit(solution)/shard_map/ppermute | solution.py:503
  111.1 1.2 %values.2.refs_4_ = f32[320,640]{1,0:T(8,128)S(1)} custom-call(f32[640,256]{1,0:T(8,128)S(1)} %pad_maximum_fusion.refs_4_.near_ref, f32[640,10]{1,0:T(8,128)S(1)} %broadcast_multiply_fusion.refs_5_.far_ref, bf16[64,640]{1,0:T(8,128)(2,1)S(1)} %inverse.3.refs_0_, bf16[64,640]{1,0:T(8,128)(2,1)S(1)} %collective-permute-done.17.refs_1_, ...), custom_call_target="tpu_custom_call" | custom-call | tf_op jit(solution)/shard_map/values/pallas_call | solution.py:595
  112.3 2.8 %values.3 = f32[320,640]{1,0:T(8,128)} custom-call(f32[640,256]{1,0:T(8,128)S(1)} %pad_maximum_fusion.refs_4_.near_ref, f32[640,10]{1,0:T(8,128)S(1)} %broadcast_multiply_fusion.refs_5_.far_ref, bf16[96,640]{1,0:T(8,128)(2,1)S(1)} %inverse.2.refs_0_, bf16[96,640]{1,0:T(8,128)(2,1)S(1)} %collective-permute-done.14.refs_1_, ...), custom_call_target="tpu_custom_call" | custom-call | tf_op jit(solution)/shard_map/values/pallas_call | solution.py:595
  (46 shorter events, 7.1 us)
Async XLA Ops:
  0.6 1.1 copy-start
  1.9 11.5 %collective-permute-start = (f32[4,640]{1,0:T(4,128)S(1)}, f32[4,640]{1,0:T(4,128)S(1)}, u32[]{:S(2)}, u32[]{:S(2)}) collective-permute-start(f32[4,640]{1,0:T(4,128)S(1)} %get-tuple-element.19), channel_id=1, source_target_pairs={{0,4},{4,8},{8,12},{12,16},{16,20},{20,24},{24,28},{28,0},{1,5},{5... | collective-permute-start | bytes 30728 | tf_op jit(solution)/shard_map/ppermute | solution.py:449
  2.5 10.9 %collective-permute-start.1 = (f32[4,640]{1,0:T(4,128)S(1)}, f32[4,640]{1,0:T(4,128)S(1)}, u32[]{:S(2)}, u32[]{:S(2)}) collective-permute-start(f32[4,640]{1,0:T(4,128)S(1)} %get-tuple-element.20), channel_id=1, source_target_pairs={{4,0},{8,4},{12,8},{16,12},{20,16},{24,20},{28,24},{0,28},{5,1},{9... | collective-permute-start | bytes 30728 | tf_op jit(solution)/shard_map/ppermute | solution.py:450
  5.4 8.0 %collective-permute-start.2 = (f32[80,4]{1,0:T(8,128)S(1)}, f32[80,4]{1,0:T(8,128)S(1)}, u32[]{:S(2)}, u32[]{:S(2)}) collective-permute-start(f32[80,4]{1,0:T(8,128)S(1)} %get-tuple-element.21), channel_id=1, source_target_pairs={{0,1},{1,2},{2,3},{3,0},{4,5},{5,6},{6,7},{7,4},{8,9},{9,10},{10,1... | collective-permute-start | bytes 3848 | tf_op jit(solution)/shard_map/ppermute | solution.py:451
  7.7 5.7 %collective-permute-start.3 = (f32[80,4]{1,0:T(8,128)S(1)}, f32[80,4]{1,0:T(8,128)S(1)}, u32[]{:S(2)}, u32[]{:S(2)}) collective-permute-start(f32[80,4]{1,0:T(8,128)S(1)} %get-tuple-element.22), channel_id=1, source_target_pairs={{1,0},{2,1},{3,2},{0,3},{5,4},{6,5},{7,6},{4,7},{9,8},{10,9},{11,1... | collective-permute-start | bytes 3848 | tf_op jit(solution)/shard_map/ppermute | solution.py:452
  13.4 1.1 copy-start.1
  14.6 1.1 copy-start.2
  18.9 8.9 %collective-permute-start.7 = (bf16[64,640]{1,0:T(8,128)(2,1)S(1)}, bf16[64,640]{1,0:T(8,128)(2,1)S(1)}, u32[]{:S(2)}, u32[]{:S(2)}) collective-permute-start(bf16[64,640]{1,0:T(8,128)(2,1)S(1)} %get-tuple-element.29), channel_id=1, source_target_pairs={{0,1},{1,0},{2,3},{3,2},{4,5},{5,4},{6,7},{7,6},{8,9},{9,8},{10,11... | collective-permute-start | bytes 245768 | tf_op jit(solution)/shard_map/ppermute | solution.py:503
  21.6 26.2 %collective-permute-start.4 = (bf16[96,640]{1,0:T(8,128)(2,1)S(1)}, bf16[96,640]{1,0:T(8,128)(2,1)S(1)}, u32[]{:S(2)}, u32[]{:S(2)}) collective-permute-start(bf16[96,640]{1,0:T(8,128)(2,1)S(1)} %get-tuple-element.25), channel_id=1, source_target_pairs={{0,1},{1,0},{2,3},{3,2},{4,5},{5,4},{6,7},{7,6},{8,9},{9,8},{10,11... | collective-permute-start | bytes 368648 | tf_op jit(solution)/shard_map/ppermute | solution.py:503
  23.7 24.1 %collective-permute-start.5 = (bf16[96,640]{1,0:T(8,128)(2,1)S(1)}, bf16[96,640]{1,0:T(8,128)(2,1)S(1)}, u32[]{:S(2)}, u32[]{:S(2)}) collective-permute-start(bf16[96,640]{1,0:T(8,128)(2,1)S(1)} %get-tuple-element.26), channel_id=1, source_target_pairs={{0,2},{1,3},{2,0},{3,1},{4,6},{5,7},{6,4},{7,5},{8,10},{9,11},{10,... | collective-permute-start | bytes 368648 | tf_op jit(solution)/shard_map/ppermute | solution.py:503
  24.7 23.1 %collective-permute-start.6 = (bf16[96,640]{1,0:T(8,128)(2,1)S(1)}, bf16[96,640]{1,0:T(8,128)(2,1)S(1)}, u32[]{:S(2)}, u32[]{:S(2)}) collective-permute-start(bf16[96,640]{1,0:T(8,128)(2,1)S(1)} %get-tuple-element.27), channel_id=1, source_target_pairs={{0,3},{1,2},{2,1},{3,0},{4,7},{5,6},{6,5},{7,4},{8,11},{9,10},{10,... | collective-permute-start | bytes 368648 | tf_op jit(solution)/shard_map/ppermute | solution.py:503
  26.1 15.8 %collective-permute-start.8 = (bf16[64,640]{1,0:T(8,128)(2,1)S(1)}, bf16[64,640]{1,0:T(8,128)(2,1)S(1)}, u32[]{:S(2)}, u32[]{:S(2)}) collective-permute-start(bf16[64,640]{1,0:T(8,128)(2,1)S(1)} %get-tuple-element.30), channel_id=1, source_target_pairs={{0,2},{1,3},{2,0},{3,1},{4,6},{5,7},{6,4},{7,5},{8,10},{9,11},{10,... | collective-permute-start | bytes 245768 | tf_op jit(solution)/shard_map/ppermute | solution.py:503
  27.8 14.2 %collective-permute-start.9 = (bf16[64,640]{1,0:T(8,128)(2,1)S(1)}, bf16[64,640]{1,0:T(8,128)(2,1)S(1)}, u32[]{:S(2)}, u32[]{:S(2)}) collective-permute-start(bf16[64,640]{1,0:T(8,128)(2,1)S(1)} %get-tuple-element.31), channel_id=1, source_target_pairs={{0,3},{1,2},{2,1},{3,0},{4,7},{5,6},{6,5},{7,4},{8,11},{9,10},{10,... | collective-permute-start | bytes 245768 | tf_op jit(solution)/shard_map/ppermute | solution.py:503
  41.9 24.8 %copy-start.3 = (f32[2,2]{1,0:T(2,128)S(1)}, f32[2,2]{1,0:T(2,128)}, u32[]{:S(2)}) copy-start(f32[2,2]{1,0:T(2,128)} %refs_2_.3) | copy-start | bytes 52
  41.9 24.8 %copy-start.4 = (f32[2]{0:T(128)S(1)}, f32[2]{0:T(128)}, u32[]{:S(2)}) copy-start(f32[2]{0:T(128)} %refs_1_.1) | copy-start | bytes 28
  56.1 2.4 %collective-permute-start.10 = (f32[4,80,640]{2,1,0:T(8,128)S(1)}, f32[4,80,640]{2,1,0:T(8,128)S(1)}, u32[]{:S(2)}, u32[]{:S(2)}) collective-permute-start(f32[4,80,640]{2,1,0:T(8,128)S(1)} %get-tuple-element.33), channel_id=1, source_target_pairs={{0,4},{4,0},{8,12},{12,8},{16,20},{20,16},{24,28},{28,24},{1,5},{5... | collective-permute-start | bytes 2457608 | tf_op jit(solution)/shard_map/ppermute | solution.py:551
  58.6 6.6 %collective-permute-start.13 = (bf16[80,640]{1,0:T(8,128)(2,1)S(1)}, bf16[80,640]{1,0:T(8,128)(2,1)S(1)}, u32[]{:S(2)}, u32[]{:S(2)}) collective-permute-start(bf16[80,640]{1,0:T(8,128)(2,1)S(1)} %get-tuple-element.36), channel_id=1, source_target_pairs={{0,24},{4,28},{8,16},{12,20},{16,8},{20,12},{24,0},{28,4},{1,25},{... | collective-permute-start | bytes 307208 | tf_op jit(solution)/shard_map/ppermute | solution.py:554
  60.1 6.6 %collective-permute-start.12 = (bf16[80,640]{1,0:T(8,128)(2,1)S(1)}, bf16[80,640]{1,0:T(8,128)(2,1)S(1)}, u32[]{:S(2)}, u32[]{:S(2)}) collective-permute-start(bf16[80,640]{1,0:T(8,128)(2,1)S(1)} %get-tuple-element.37), channel_id=1, source_target_pairs={{0,16},{4,20},{8,24},{12,28},{16,0},{20,4},{24,8},{28,12},{1,17},{... | collective-permute-start | bytes 307208 | tf_op jit(solution)/shard_map/ppermute | solution.py:554
  61.6 5.2 %collective-permute-start.11 = (bf16[80,640]{1,0:T(8,128)(2,1)S(1)}, bf16[80,640]{1,0:T(8,128)(2,1)S(1)}, u32[]{:S(2)}, u32[]{:S(2)}) collective-permute-start(bf16[80,640]{1,0:T(8,128)(2,1)S(1)} %get-tuple-element.38), channel_id=1, source_target_pairs={{0,8},{4,12},{8,0},{12,4},{16,24},{20,28},{24,16},{28,20},{1,9},{5... | collective-permute-start | bytes 307208 | tf_op jit(solution)/shard_map/ppermute | solution.py:554
  84.2 15.1 %collective-permute-start.19 = (bf16[64,640]{1,0:T(8,128)(2,1)S(1)}, bf16[64,640]{1,0:T(8,128)(2,1)S(1)}, u32[]{:S(2)}, u32[]{:S(2)}) collective-permute-start(bf16[64,640]{1,0:T(8,128)(2,1)S(1)} %inverse.3.refs_0_), channel_id=1, source_target_pairs={{0,3},{1,2},{2,1},{3,0},{4,7},{5,6},{6,5},{7,4},{8,11},{9,10},{10,... | collective-permute-start | bytes 245768 | tf_op jit(solution)/shard_map/ppermute | solution.py:503
  94.3 18.0 %collective-permute-start.16 = (bf16[96,640]{1,0:T(8,128)(2,1)S(1)}, bf16[96,640]{1,0:T(8,128)(2,1)S(1)}, u32[]{:S(2)}, u32[]{:S(2)}) collective-permute-start(bf16[96,640]{1,0:T(8,128)(2,1)S(1)} %inverse.2.refs_0_), channel_id=1, source_target_pairs={{0,3},{1,2},{2,1},{3,0},{4,7},{5,6},{6,5},{7,4},{8,11},{9,10},{10,... | collective-permute-start | bytes 368648 | tf_op jit(solution)/shard_map/ppermute | solution.py:503
  96.4 15.9 %collective-permute-start.15 = (bf16[96,640]{1,0:T(8,128)(2,1)S(1)}, bf16[96,640]{1,0:T(8,128)(2,1)S(1)}, u32[]{:S(2)}, u32[]{:S(2)}) collective-permute-start(bf16[96,640]{1,0:T(8,128)(2,1)S(1)} %inverse.2.refs_0_), channel_id=1, source_target_pairs={{0,2},{1,3},{2,0},{3,1},{4,6},{5,7},{6,4},{7,5},{8,10},{9,11},{10,... | collective-permute-start | bytes 368648 | tf_op jit(solution)/shard_map/ppermute | solution.py:503
  96.4 15.9 %collective-permute-start.14 = (bf16[96,640]{1,0:T(8,128)(2,1)S(1)}, bf16[96,640]{1,0:T(8,128)(2,1)S(1)}, u32[]{:S(2)}, u32[]{:S(2)}) collective-permute-start(bf16[96,640]{1,0:T(8,128)(2,1)S(1)} %inverse.2.refs_0_), channel_id=1, source_target_pairs={{0,1},{1,0},{2,3},{3,2},{4,5},{5,4},{6,7},{7,6},{8,9},{9,8},{10,11... | collective-permute-start | bytes 368648 | tf_op jit(solution)/shard_map/ppermute | solution.py:503
  98.7 12.3 %collective-permute-start.18 = (bf16[64,640]{1,0:T(8,128)(2,1)S(1)}, bf16[64,640]{1,0:T(8,128)(2,1)S(1)}, u32[]{:S(2)}, u32[]{:S(2)}) collective-permute-start(bf16[64,640]{1,0:T(8,128)(2,1)S(1)} %inverse.3.refs_0_), channel_id=1, source_target_pairs={{0,2},{1,3},{2,0},{3,1},{4,6},{5,7},{6,4},{7,5},{8,10},{9,11},{10,... | collective-permute-start | bytes 245768 | tf_op jit(solution)/shard_map/ppermute | solution.py:503
  99.4 11.7 %collective-permute-start.17 = (bf16[64,640]{1,0:T(8,128)(2,1)S(1)}, bf16[64,640]{1,0:T(8,128)(2,1)S(1)}, u32[]{:S(2)}, u32[]{:S(2)}) collective-permute-start(bf16[64,640]{1,0:T(8,128)(2,1)S(1)} %inverse.3.refs_0_), channel_id=1, source_target_pairs={{0,1},{1,0},{2,3},{3,2},{4,5},{5,4},{6,7},{7,6},{8,9},{9,8},{10,11... | collective-permute-start | bytes 245768 | tf_op jit(solution)/shard_map/ppermute | solution.py:503
where the time goes:
time: 116 us; the launch traced here: 115 us
  Pallas kernels  39.1 us (34%)
  starting transfers between devices  28.3 us (24%)
  waiting for transfers between devices  27.2 us (23%)
  blocking collectives  10.7 us (9%)
  local copies, waits for them, and re-layouts  7.05 us (6%)
  other arithmetic  1.91 us (2%)
    ppermute x12, waiting for transfers between devices, swap_lon(): lax.ppermute(parts[k], 'lon', pairs(lon_count, k))  20.3 us
    ppermute x12, starting transfers between devices, swap_lon(): lax.ppermute(parts[k], 'lon', pairs(lon_count, k))  16.9 us
    pallas_call x2, Pallas kernels, forward(): pl.pallas_call(lambda *refs: forward_kernel(lon_count, sections, rows_hal...  14.1 us
    pallas_call x2, Pallas kernels, inverse(): pl.pallas_call(lambda *refs: inverse_kernel(sections, rows_half, first, *...  14.1 us
    all_gather x1, blocking collectives, shards(): joined = lax.all_gather(rounded, 'lat', axis=0, tiled=True)  10.7 us
    ppermute x3, waiting for transfers between devices, shards(): lax.ppermute(sums[j].astype(BF16), 'lat', pairs(lat_count, 2 * j))  4.58 us
    pallas_call x2, Pallas kernels, values(): pl.pallas_call(body, out_shape=like((grid_count, lon_dev), F32), in_specs...  4.03 us
    ppermute x3, starting transfers between devices, shards(): lax.ppermute(sums[j].astype(BF16), 'lat', pairs(lat_count, 2 * j))  3.55 us
  transfers between devices with their start and end apart: 20, of which 6 were waited for; matrix products, arithmetic and copies ran while one was open for 5% of the time, Pallas kernels for 16%

commit v1 on v0

--- a/solution.py
+++ b/solution.py
@@ -136,8 +136,7 @@
     return (new_fields, spectrum)
 
 
-UNIT = 32
-CUTS = (64, 96)
+CUTS = (64, 64, 32)
 GROUP = 16
 LANES = 128
 F32 = jnp.float32
@@ -161,19 +160,48 @@
     return [(i, i ^ step) for i in range(count)]
 
 
-def edges_kernel(fields_ref, first_row, last_row, first_column, last_column):
+def load_kernel(fields_hbm, winds_hbm, fields_ref, winds_ref, *refs):
+    first_row, last_row, first_column, last_column, semaphores = refs
+    fields_copy = pltpu.make_async_copy(fields_hbm, fields_ref, semaphores.at[0])
+    winds_copy = pltpu.make_async_copy(winds_hbm, winds_ref, semaphores.at[1])
+    fields_copy.start()
+    winds_copy.start()
+    fields_copy.wait()
     count, rows, columns = fields_ref.shape
     for p in range(count):
         first_row[p : p + 1, :] = fields_ref[p, 0:1, :]
         last_row[p : p + 1, :] = fields_ref[p, rows - 1 : rows, :]
         first_column[:, p : p + 1] = fields_ref[p, :, 0:1]
         last_column[:, p : p + 1] = fields_ref[p, :, columns - 1 : columns]
+    winds_copy.wait()
+
+
+def load_table_kernel(after_ref, table_hbm, table_ref, semaphores):
+    parts = semaphores.shape[0]
+    share = table_ref.shape[0] // parts
+    copies = [
+        pltpu.make_async_copy(
+            table_hbm.at[pl.ds(i * share, share)],
+            table_ref.at[pl.ds(i * share, share)],
+            semaphores.at[i],
+        )
+        for i in range(parts)
+    ]
+    for copy in copies:
+        copy.start()
+    for copy in copies:
+        copy.wait()
 
 
 def advance(flags, fields_ref, wind_ref, step_ref, above, below, before, after, stepped_ref):
     count, rows, columns = fields_ref.shape
     lane = lax.broadcasted_iota(jnp.int32, (rows, columns), 1)
     row = lax.broadcasted_iota(jnp.int32, (rows, columns), 0)
+    square = (rows, rows)
+    diagonal = lax.broadcasted_iota(jnp.int32, square, 0) == lax.broadcasted_iota(
+        jnp.int32, square, 1
+    )
+    steps = jnp.sum(jnp.where(diagonal, step_ref[...], 0.0), axis=1, keepdims=True)
     for p in range(count):
         h = p % 2
         field = fields_ref[p]
@@ -186,7 +214,7 @@
         high_edge = jnp.where(flags[0] == 1, 0.0, above[p : p + 1, :])
         toward = jnp.where(row == rows - 1, low_edge, pltpu.roll(field, rows - 1, 0))
         poleward = jnp.where(row == 0, high_edge, pltpu.roll(field, 1, 0))
-        tendency = wind_ref[h] * step_ref[...] * (eastward - westward) + 0.25 * wind_ref[
+        tendency = wind_ref[h] * steps * (eastward - westward) + 0.25 * wind_ref[
             2 + h
         ] * (toward - poleward)
         stepped_ref[p * rows : (p + 1) * rows, :] = field - tendency
@@ -217,14 +245,15 @@
     for part in range(2):
         rows_high, rows_low = split_halves(table_rows(near, far, first, share, blocks, part))
         sums = dot_rows(rows_high, high) + (dot_rows(rows_high, low) + dot_rows(rows_low, high))
-        for k, out in enumerate(outs):
-            out[:, part * count : (part + 1) * count] = sums[
-                k * share : (k + 1) * share, :
-            ].astype(out.dtype)
+        lanes = slice(part * count, (part + 1) * count)
+        own, pair = outs
+        for k in range(0, blocks, 2):
+            own[k // 2, :, lanes] = sums[k * share : (k + 1) * share, :]
+            pair[k // 2, :, lanes] = sums[(k + 1) * share : (k + 2) * share, :].astype(BF16)
 
 
 def forward_kernel(
-    blocks, sections, rows, degree_dev, last, waves_ref, place_ref, *refs
+    blocks, sections, rows, degree_dev, first, last, waves_ref, place_ref, *refs
 ):
     received = refs[:blocks]
     weight_ref, table_ref = refs[blocks : blocks + 2]
@@ -233,7 +262,7 @@
     step = pl.program_id(0)
     half = sections // 2
     levels = half // 2
-    group = table_ref.shape[0]
+    group = GROUP
     columns = table_ref.shape[2]
     share = spread_ref.shape[0]
 
@@ -256,7 +285,7 @@
         for v in (u, u + 1):
             high, low = split_halves(spread_ref[step * group + v, :, 0:rows])
             both = jnp.concatenate([high.astype(F32), low.astype(F32)], axis=0).astype(BF16)
-            total = jnp.dot(both, table_ref[v], preferred_element_type=F32)
+            total = jnp.dot(both, table_ref[first + step * group + v], preferred_element_type=F32)
             sums.append(total[:sections] + total[sections:])
         north = jnp.concatenate([sums[0][:half], sums[1][:half]], axis=0)
         south = jnp.concatenate([sums[0][half:], sums[1][half:]], axis=0)
@@ -270,7 +299,7 @@
 
     @pl.when(step == pl.num_programs(0) - 1)
     def _():
-        target = turned_ref if last else rest[0]
+        target = turned_ref if last else rest[-4]
         for t in range(columns // LANES):
             tile = jnp.concatenate(
                 [kept_ref[t, pl.ds(j, share, stride=half), :] for j in range(half)], axis=0
@@ -322,7 +351,7 @@
     step = pl.program_id(0)
     half = sections // 2
     levels = half // 2
-    group = table_ref.shape[0]
+    group = GROUP
     columns = table_ref.shape[2]
     share = spread_ref.shape[0]
 
@@ -350,7 +379,7 @@
         odds = pltpu.roll(jnp.where(even, 0.0, values), half, 0)
         for v in range(2):
             both = jnp.where(upper, odds, evens) if v else jnp.where(upper, evens, odds)
-            sums = dot_rows(both.astype(BF16), table_ref[u + v])
+            sums = dot_rows(both.astype(BF16), table_ref[first + slot + v])
             factor = jnp.where(waves_ref[slot + v] == 0, 1.0, 2.0) / math.sqrt(M)
             sums = sums * factor
             swapped = pltpu.roll(sums, half, 0)
@@ -382,10 +411,15 @@
 
 VMEM = pl.BlockSpec(memory_space=pltpu.VMEM)
 SMEM = pl.BlockSpec(memory_space=pltpu.SMEM)
+HBM = pl.BlockSpec(memory_space=pltpu.HBM)
 
 
 def grant(size):
     return pltpu.CompilerParams(vmem_limit_bytes=size << 20)
+
+
+def cost(microseconds):
+    return pl.CostEstimate(flops=0, bytes_accessed=int(microseconds * 3.3e6), transcendentals=0)
 
 
 def like(shape, dtype):
@@ -413,6 +447,7 @@
         or lat_count & (lat_count - 1)
         or lat_count < 4
         or lon_count & (lon_count - 1)
+        or lon_count < 4
     ):
         return untiled(
             level_fields,
@@ -434,14 +469,18 @@
     fields = level_fields.reshape(planes, rows_half, lon_dev)
     winds = wind_field.reshape(2 * hemis, rows_half, lon_dev)
 
-    first_row, last_row, first_column, last_column = pl.pallas_call(
-        edges_kernel,
-        out_shape=[like((planes, lon_dev), F32)] * 2 + [like((rows_half, planes), F32)] * 2,
-        in_specs=[VMEM],
-        out_specs=[VMEM] * 4,
+    fields, winds, first_row, last_row, first_column, last_column = pl.pallas_call(
+        load_kernel,
+        out_shape=[pltpu.VMEM(fields.shape, F32), pltpu.VMEM(winds.shape, F32)]
+        + [like((planes, lon_dev), F32)] * 2
+        + [like((rows_half, planes), F32)] * 2,
+        in_specs=[HBM] * 2,
+        out_specs=[VMEM] * 6,
+        scratch_shapes=[pltpu.SemaphoreType.DMA((2,))],
         compiler_params=grant(8),
-        name="edges",
-    )(fields)
+        cost_estimate=cost(1.5),
+        name="load",
+    )(*[pltpu.with_memory_space_constraint(value, pltpu.HBM) for value in (fields, winds)])
     up = [(i, (i + 1) % lat_count) for i in range(lat_count)]
     east = [(i, (i + 1) % lon_count) for i in range(lon_count)]
     down = [(j, i) for i, j in up]
@@ -469,7 +508,7 @@
     weight_row = jnp.tile(quad_weight, sections)[None, :]
 
     def sums_shape(share):
-        return [like((share, width), BF16 if k else F32) for k in range(lon_count)]
+        return [like((lon_count // 2, share, width), dtype) for dtype in (F32, BF16)]
 
     def first_sums(flags_ref, fields_ref, winds_ref, step_ref, *refs):
         edges, near_ref, far_ref, stepped_ref = refs[:4], refs[4], refs[5], refs[6]
@@ -480,38 +519,57 @@
         first_sums,
         out_shape=[like((grid_count, lon_dev), F32)] + sums_shape(CUTS[0]),
         in_specs=[SMEM] + [VMEM] * 9,
-        out_specs=[VMEM] * (1 + lon_count),
+        out_specs=[VMEM] * 3,
         compiler_params=grant(24),
+        cost_estimate=cost(3.0),
         name="advance_and_sums",
-    )(flags, fields, winds, zonal_step[:, None], above, below, before, after, near, far)
-
-    def later_sums(share, first):
-        def body(stepped_ref, near_ref, far_ref, *outs):
+    )(flags, fields, winds, zonal_step[None, :], above, below, before, after, near, far)
+
+    def later_sums(share, first, after):
+        def body(stepped_ref, near_ref, far_ref, after_ref, *outs):
             zonal_sums(lon_count, share, first, stepped_ref, near_ref, far_ref, outs)
 
         return pl.pallas_call(
             body,
             out_shape=sums_shape(share),
-            in_specs=[VMEM] * 3,
-            out_specs=[VMEM] * lon_count,
+            in_specs=[VMEM] * 4,
+            out_specs=[VMEM] * 2,
             compiler_params=grant(24),
+            cost_estimate=cost(0.025 * share),
             name="sums",
-        )(stepped, near, far)
-
-    def swap_lon(parts):
-        return [parts[0]] + [
-            lax.ppermute(parts[k], "lon", pairs(lon_count, k)) for k in range(1, lon_count)
-        ]
-
-    swapped, first = [swap_lon(pieces)], CUTS[0]
+        )(stepped, near, far, after)
+
+    def to_owners(own, pair):
+        pair = lax.ppermute(pair, "lon", pairs(lon_count, 1))
+        parts = [own[0], pair[0]]
+        for k in range(1, lon_count // 2):
+            joint = (own[k] + pair[k].astype(F32)).astype(BF16)
+            parts.append(lax.ppermute(joint, "lon", pairs(lon_count, 2 * k)))
+        return parts
+
+    def from_owners(coefs):
+        near_by = lax.ppermute(coefs, "lon", pairs(lon_count, 1))
+        parts = [coefs, near_by]
+        for k in range(1, lon_count // 2):
+            distant = lax.ppermute(coefs, "lon", pairs(lon_count, 2 * k))
+            parts += [distant, lax.ppermute(distant, "lon", pairs(lon_count, 1))]
+        return parts
+
+    swapped, first = [to_owners(*pieces)], CUTS[0]
     for share in CUTS[1:]:
-        swapped.append(swap_lon(later_sums(share, first)))
+        pieces = later_sums(share, first, pieces[0])
+        swapped.append(to_owners(*pieces))
         first += share
-
-    def table_spec(first):
-        return pl.BlockSpec(
-            (GROUP, rows_half, columns), lambda g, *_: (first // GROUP + g, 0, 0)
-        )
+    table = pl.pallas_call(
+        load_table_kernel,
+        out_shape=pltpu.VMEM(legendre.shape, BF16),
+        in_specs=[VMEM, HBM],
+        out_specs=VMEM,
+        scratch_shapes=[pltpu.SemaphoreType.DMA((4,))],
+        compiler_params=grant(8),
+        cost_estimate=cost(5.7),
+        name="load_table",
+    )(pieces[0], pltpu.with_memory_space_constraint(legendre, pltpu.HBM))
 
     def forward(first, share, parts, earlier, last):
         if last:
@@ -521,14 +579,14 @@
             shapes = [like((columns, half * share), F32)]
         return pl.pallas_call(
             lambda *refs: forward_kernel(
-                lon_count, sections, rows_half, degree_dev, last, *refs
+                len(parts), sections, rows_half, degree_dev, first, last, *refs
             ),
             out_shape=shapes,
             grid_spec=pltpu.PrefetchScalarGridSpec(
                 num_scalar_prefetch=2,
                 grid=(share // GROUP,),
-                in_specs=[whole_block((share, width))] * lon_count
-                + [whole_block((1, width)), table_spec(first)]
+                in_specs=[whole_block((share, width))] * len(parts)
+                + [whole_block((1, width)), VMEM]
                 + [whole_block(other.shape) for other in earlier],
                 out_specs=[whole_block(shape.shape) for shape in shapes],
                 scratch_shapes=[
@@ -537,14 +595,15 @@
                     pltpu.VMEM((columns, half * share), F32),
                 ],
             ),
-            compiler_params=grant(50),
+            compiler_params=grant(20),
+            cost_estimate=cost(0.05 * share + 0.7),
             name="forward",
-        )(my_waves[first : first + share], place, *parts, weight_row, legendre, *earlier)
+        )(my_waves[first : first + share], place, *parts, weight_row, table, *earlier)
 
     earlier, first = [], 0
     for share, parts in zip(CUTS, swapped):
         last = first + share == slots_dev
-        earlier = earlier + list(forward(first, share, parts, earlier if last else [], last))
+        earlier = earlier + list(forward(first, share, parts, earlier, last))
         first += share
     own, other = earlier[-2:]
 
@@ -567,23 +626,25 @@
     )(place, damping, vertical, *sums)
     joined = lax.all_gather(rounded, "lat", axis=0, tiled=True)
 
-    def inverse(first, share):
+    def inverse(first, share, after):
+        count = 3 + len(after)
         return pl.pallas_call(
-            lambda *refs: inverse_kernel(sections, rows_half, first, *refs),
+            lambda *refs: inverse_kernel(sections, rows_half, first, *refs[:3], *refs[count:]),
             out_shape=like((share, width), BF16),
             grid_spec=pltpu.PrefetchScalarGridSpec(
                 num_scalar_prefetch=1,
                 grid=(share // GROUP,),
-                in_specs=[whole_block(joined.shape), table_spec(first)],
+                in_specs=[whole_block(joined.shape), VMEM] + [VMEM] * len(after),
                 out_specs=whole_block((share, width)),
                 scratch_shapes=[
                     pltpu.VMEM((columns // LANES, half * share, LANES), F32),
                     pltpu.VMEM((share, sections, LANES), F32),
                 ],
             ),
-            compiler_params=grant(50),
+            compiler_params=grant(20),
+            cost_estimate=cost(0.06 * share + 0.3),
             name="inverse",
-        )(my_waves[first : first + share], joined, legendre)
+        )(my_waves[first : first + share], joined, table, *after)
 
     def values(first, share, parts, base):
         def body(near_ref, far_ref, *refs):
@@ -598,14 +659,15 @@
             in_specs=[VMEM] * (2 + lon_count + len(base)),
             out_specs=VMEM,
             compiler_params=grant(24),
+            cost_estimate=cost(0.025 * share),
             name="values",
         )(near, far, *parts, *base)
 
-    base, first = [], 0
-    for share in CUTS:
-        coefs = inverse(first, share)
-        base = [values(first, share, swap_lon([coefs] * lon_count), base)]
-        first += share
+    base, first, coefs = [], slots_dev, []
+    for share in reversed(CUTS):
+        first -= share
+        coefs = [inverse(first, share, coefs)]
+        base = [values(first, share, from_owners(coefs[0]), base)]
     spectrum = spectrum.reshape(2, levels, degree_dev, slots_dev).transpose(2, 3, 0, 1)
     return (base[0].reshape(level_fields.shape), spectrum)
 

time: 116 us -> 99.6 us (0.86)
  waiting for transfers between devices: 27.2 us -> 17.5 us
  local copies, waits for them, and re-layouts: 7.05 us -> 3.55 us
  Pallas kernels: 39.1 us -> 35.8 us
    ppermute x12 -> x15, waiting for transfers between devices: 20.3 us -> 10.5 us  [the longest x3 4.48 us: to_owners(): parts.append(lax.ppermute(joint, 'lon', pairs(lon_count, 2 * k)))]
    pallas_call x2 -> x3, Pallas kernels: 14.1 us -> 9.22 us  [inverse(): pl.pallas_call(lambda *refs: inverse_kernel(sections, rows_half, first, *...]
    unnamed x10 -> x6, local copies, waits for them, and re-layouts: 3.43 us -> 0.66 us
    pallas_call x4 -> x7, Pallas kernels: 16.8 us -> 18.6 us  [the longest x3 8.3 us: forward(): pl.pallas_call(lambda *refs: forward_kernel(len(parts), sections, rows_ha...]
    ppermute x12 -> x15, starting transfers between devices: 16.9 us -> 18 us  [the longest x3 5.93 us: to_owners(): parts.append(lax.ppermute(joint, 'lon', pairs(lon_count, 2 * k)))]
    pallas_call x2 -> x3, Pallas kernels: 4.03 us -> 4.15 us  [values(): pl.pallas_call(body, out_shape=like((grid_count, lon_dev), F32), in_specs...]
  transfers between devices with their start and end apart: 20 -> 23, of which waited for: 6 -> 7; matrix products, arithmetic and copies ran while one was open for 5% -> 5% of each run, Pallas kernels for 16% -> 18%
where the time goes in v1:
time: 99.6 us; the launch traced here: 99.3 us
  Pallas kernels  35.8 us (36%)
  starting transfers between devices  29.4 us (30%)
  waiting for transfers between devices  17.5 us (18%)
  blocking collectives  10.2 us (10%)
  local copies, waits for them, and re-layouts  3.55 us (4%)
  other arithmetic  1.99 us (2%)
    all_gather x1, blocking collectives, shards(): joined = lax.all_gather(rounded, 'lat', axis=0, tiled=True)  10.2 us
    pallas_call x3, Pallas kernels, inverse(): pl.pallas_call(lambda *refs: inverse_kernel(sections, rows_half, first, *...  9.22 us
    pallas_call x3, Pallas kernels, forward(): pl.pallas_call(lambda *refs: forward_kernel(len(parts), sections, rows_ha...  8.3 us
    ppermute x3, starting transfers between devices, to_owners(): parts.append(lax.ppermute(joint, 'lon', pairs(lon_count, 2 * k)))  5.93 us
    pallas_call x1, Pallas kernels, shards(): pl.pallas_call(load_table_kernel, out_shape=pltpu.VMEM(legendre.shape, BF...  5.77 us
    ppermute x3, waiting for transfers between devices, shards(): lax.ppermute(sums[j].astype(BF16), 'lat', pairs(lat_count, 2 * j))  4.63 us
    ppermute x3, waiting for transfers between devices, to_owners(): parts.append(lax.ppermute(joint, 'lon', pairs(lon_count, 2 * k)))  4.48 us
    pallas_call x3, Pallas kernels, values(): pl.pallas_call(body, out_shape=like((grid_count, lon_dev), F32), in_specs...  4.15 us
  transfers between devices with their start and end apart: 23, of which 7 were waited for; matrix products, arithmetic and copies ran while one was open for 5% of the time, Pallas kernels for 18%

profile of v1, /device:TPU:0, one launch (start us, length us, event | category | flops | bytes accessed | tf_op | source)
XLA Modules:
  0.0 99.3 jit_solution(3344159401822599418)
XLA Ops:
  0.6 1.4 %load.1 = (f32[4,80,640]{2,1,0:T(8,128)S(1)}, f32[4,80,640]{2,1,0:T(8,128)S(1)}, f32[4,640]{1,0:T(4,128)S(1)}, f32[4,640]{1,0:T(4,128)S(1)}, f32[80,4]{1,0:T(8,128)S(1)}, /*index=5*/f32[80,4]{1,0:T(8,128)S(1)}) custom-call(f32[4,80,640]{2,1,0:T(8,128)} %bitcast.39, f32[4,80,640]{2,1,0:T(8,128)} %bitcast.40), custom_call_target="tpu_custom_call" | custom-call | bytes 4950000 | tf_op jit(solution)/shard_map/load/pallas_call | solution.py:472
  2.6 2.9 %collective-permute-start.1 = (f32[4,640]{1,0:T(4,128)S(1)}, f32[4,640]{1,0:T(4,128)S(1)}, u32[]{:S(2)}, u32[]{:S(2)}) collective-permute-start(f32[4,640]{1,0:T(4,128)S(1)} %get-tuple-element.22), channel_id=1, source_target_pairs={{4,0},{8,4},{12,8},{16,12},{20,16},{24,20},{28,24},{0,28},{5,1},{9... | collective-permute-start | bytes 30728 | tf_op jit(solution)/shard_map/ppermute | solution.py:489
  5.5 2.3 %collective-permute-start.2 = (f32[80,4]{1,0:T(8,128)S(1)}, f32[80,4]{1,0:T(8,128)S(1)}, u32[]{:S(2)}, u32[]{:S(2)}) collective-permute-start(f32[80,4]{1,0:T(8,128)S(1)} %get-tuple-element.23), channel_id=1, source_target_pairs={{0,1},{1,2},{2,3},{3,0},{4,5},{5,6},{6,7},{7,4},{8,9},{9,10},{10,1... | collective-permute-start | bytes 3848 | tf_op jit(solution)/shard_map/ppermute | solution.py:490
  7.8 2.0 %collective-permute-start.3 = (f32[80,4]{1,0:T(8,128)S(1)}, f32[80,4]{1,0:T(8,128)S(1)}, u32[]{:S(2)}, u32[]{:S(2)}) collective-permute-start(f32[80,4]{1,0:T(8,128)S(1)} %get-tuple-element.24), channel_id=1, source_target_pairs={{1,0},{2,1},{3,2},{0,3},{5,4},{6,5},{7,6},{4,7},{9,8},{10,9},{11,1... | collective-permute-start | bytes 3848 | tf_op jit(solution)/shard_map/ppermute | solution.py:491
  10.8 1.4 %fusion.5 = (f32[640,128]{1,0:T(8,128)S(1)}, f32[640,128]{1,0:T(8,128)S(1)}) fusion(s32[640]{0:T(1024)S(1)} %pad_add_fusion), kind=kLoop, calls=%fused_computation.9 | loop fusion | flops 737280 | bytes 657920 | tf_op jit(solution)/shard_map/cos | solution.py:500
  13.4 3.1 %advance_and_sums.1 = (f32[320,640]{1,0:T(8,128)S(1)}, f32[2,64,640]{2,1,0:T(8,128)S(1)}, bf16[2,64,640]{2,1,0:T(8,128)(2,1)S(1)}) custom-call(s32[2]{0:T(128)S(1)} %add_convert_fusion.3.flags_ref, f32[4,80,640]{2,1,0:T(8,128)S(1)} %get-tuple-element.19.fields_ref, f32[4,80,640]{2,1,0:T(8,128)S(1)} %get-tuple-element.20.winds_ref, f32[1,80]{1,0:T(1,128)S(1)} %bitcast.38, ...), custom_call_target="tpu_custom_call" | custom-call | bytes 9900000 | tf_op jit(solution)/shard_map/advance_and_sums/pallas_call | solution.py:518
  16.5 1.8 %sums.2 = (f32[2,64,640]{2,1,0:T(8,128)S(1)}, bf16[2,64,640]{2,1,0:T(8,128)(2,1)S(1)}) custom-call(f32[320,640]{1,0:T(8,128)S(1)} %get-tuple-element.25.stepped_ref, f32[640,256]{1,0:T(8,128)S(1)} %pad_maximum_fusion.refs_4_.near_ref, f32[640,10]{1,0:T(8,128)S(1)} %broadcast_multiply_fusion.refs_5_.far_ref, f32[2,64,640]{2,1,0:T(8,128)S(1)} %get-tuple-element.26.after_ref), custom_call_target="tpu_custom_call" | custom-call | bytes 5280000 | tf_op jit(solution)/shard_map/sums/pallas_call | solution.py:532
  18.4 1.3 %sums.3 = (f32[2,32,640]{2,1,0:T(8,128)S(1)}, bf16[2,32,640]{2,1,0:T(8,128)(2,1)S(1)}) custom-call(f32[320,640]{1,0:T(8,128)S(1)} %get-tuple-element.25.stepped_ref, f32[640,256]{1,0:T(8,128)S(1)} %pad_maximum_fusion.refs_4_.near_ref, f32[640,10]{1,0:T(8,128)S(1)} %broadcast_multiply_fusion.refs_5_.far_ref, f32[2,64,640]{2,1,0:T(8,128)S(1)} %get-tuple-element.27.after_ref), custom_call_target="tpu_custom_call" | custom-call | bytes 2640000 | tf_op jit(solution)/shard_map/sums/pallas_call | solution.py:532
  21.1 1.5 %collective-permute-start.6 = (bf16[2,64,640]{2,1,0:T(8,128)(2,1)S(1)}, bf16[2,64,640]{2,1,0:T(8,128)(2,1)S(1)}, u32[]{:S(2)}, u32[]{:S(2)}) collective-permute-start(bf16[2,64,640]{2,1,0:T(8,128)(2,1)S(1)} %get-tuple-element.30), channel_id=1, source_target_pairs={{0,1},{1,0},{2,3},{3,2},{4,5},{5,4},{6,7},{7,6},{8,9},{9,8},{10,11... | collective-permute-start | bytes 491528 | tf_op jit(solution)/shard_map/ppermute | solution.py:543
  23.2 5.8 %load_table.1.refs_6_.refs_2_ = bf16[160,80,640]{2,1,0:T(8,128)(2,1)S(1)} custom-call(f32[2,32,640]{2,1,0:T(8,128)S(1)} %get-tuple-element.28.after_ref, bf16[160,80,640]{2,1,0:T(8,128)(2,1)} %table_hbm.1), custom_call_target="tpu_custom_call" | custom-call | bytes 18810000 | tf_op jit(solution)/shard_map/load_table/pallas_call | solution.py:563
  29.0 2.9 %collective-permute-start.5 = (bf16[32,640]{1,0:T(8,128)(2,1)S(1)}, bf16[32,640]{1,0:T(8,128)(2,1)S(1)}, u32[]{:S(2)}, u32[]{:S(2)}) collective-permute-start(bf16[32,640]{1,0:T(8,128)(2,1)S(1)} %get-tuple-element.44), channel_id=1, source_target_pairs={{0,2},{1,3},{2,0},{3,1},{4,6},{5,7},{6,4},{7,5},{8,10},{9,11},{10,... | collective-permute-start | bytes 122888 | tf_op jit(solution)/shard_map/ppermute | solution.py:547
  32.1 2.9 %collective-permute-start.9 = (bf16[64,640]{1,0:T(8,128)(2,1)S(1)}, bf16[64,640]{1,0:T(8,128)(2,1)S(1)}, u32[]{:S(2)}, u32[]{:S(2)}) collective-permute-start(bf16[64,640]{1,0:T(8,128)(2,1)S(1)} %get-tuple-element.40), channel_id=1, source_target_pairs={{0,2},{1,3},{2,0},{3,1},{4,6},{5,7},{6,4},{7,5},{8,10},{9,11},{10,... | collective-permute-start | bytes 245768 | tf_op jit(solution)/shard_map/ppermute | solution.py:547
  35.1 4.5 %collective-permute-done.7.refs_4_ = bf16[64,640]{1,0:T(8,128)(2,1)S(1)} collective-permute-done((bf16[64,640]{1,0:T(8,128)(2,1)S(1)}, bf16[64,640]{1,0:T(8,128)(2,1)S(1)}, u32[]{:S(2)}, u32[]{:S(2)}) %collective-permute-start.7) | collective-permute-done | bytes 81952 | tf_op jit(solution)/shard_map/ppermute | solution.py:547
  39.5 3.2 %forward.3.refs_7_ = f32[640,256]{1,0:T(8,128)S(1)} custom-call(s32[64]{0:T(128)S(1)} %get-tuple-element.55.refs_0_, s32[1]{0:T(128)} %bitcast.refs_1_.refs_0_, f32[64,640]{1,0:T(8,128)S(1)} %get-tuple-element.43.refs_2_, bf16[64,640]{1,0:T(8,128)(2,1)S(1)} %slice_bitcast_fusion.3.refs_3_, bf16[64,640]{1,0:T(8,128)(2,1)S(1)} %collective-permute-done.7.refs_4_, ...), custom_call_target="tpu_custom_call" | custom-call | bytes 12870000 | tf_op jit(solution)/shard_map/forward/pallas_call | solution.py:580
  42.7 3.2 %forward.4.refs_8_ = f32[640,256]{1,0:T(8,128)S(1)} custom-call(s32[64]{0:T(128)S(1)} %get-tuple-element.54.refs_0_, s32[1]{0:T(128)} %bitcast.refs_1_.refs_0_, f32[64,640]{1,0:T(8,128)S(1)} %get-tuple-element.41.refs_2_, bf16[64,640]{1,0:T(8,128)(2,1)S(1)} %slice_bitcast_fusion.2.refs_3_, bf16[64,640]{1,0:T(8,128)(2,1)S(1)} %collective-permute-done.9.refs_4_, ...), custom_call_target="tpu_custom_call" | custom-call | bytes 12870000 | tf_op jit(solution)/shard_map/forward/pallas_call | solution.py:580
  45.9 2.0 %forward.5 = (f32[4,80,640]{2,1,0:T(8,128)S(1)}, f32[4,80,640]{2,1,0:T(8,128)S(1)}) custom-call(s32[32]{0:T(128)S(1)} %slice.73.refs_0_, s32[1]{0:T(128)} %bitcast.refs_1_.refs_0_, f32[32,640]{1,0:T(8,128)S(1)} %get-tuple-element.45.refs_2_, bf16[32,640]{1,0:T(8,128)(2,1)S(1)} %slice_bitcast_fusion.5.refs_3_, ...), custom_call_target="tpu_custom_call" | custom-call | bytes 7589999 | tf_op jit(solution)/shard_map/forward/pallas_call | solution.py:580
  48.0 2.3 %collective-permute-done.10 = f32[4,80,640]{2,1,0:T(8,128)S(1)} collective-permute-done((f32[4,80,640]{2,1,0:T(8,128)S(1)}, f32[4,80,640]{2,1,0:T(8,128)S(1)}, u32[]{:S(2)}, u32[]{:S(2)}) %collective-permute-start.10) | collective-permute-done | bytes 819232 | tf_op jit(solution)/shard_map/ppermute | solution.py:610
  50.4 1.3 %collective-permute-start.13 = (bf16[80,640]{1,0:T(8,128)(2,1)S(1)}, bf16[80,640]{1,0:T(8,128)(2,1)S(1)}, u32[]{:S(2)}, u32[]{:S(2)}) collective-permute-start(bf16[80,640]{1,0:T(8,128)(2,1)S(1)} %get-tuple-element.36), channel_id=1, source_target_pairs={{0,24},{4,28},{8,16},{12,20},{16,8},{20,12},{24,0},{28,4},{1,25},{... | collective-permute-start | bytes 307208 | tf_op jit(solution)/shard_map/ppermute | solution.py:613
  52.7 1.3 %collective-permute-start.11 = (bf16[80,640]{1,0:T(8,128)(2,1)S(1)}, bf16[80,640]{1,0:T(8,128)(2,1)S(1)}, u32[]{:S(2)}, u32[]{:S(2)}) collective-permute-start(bf16[80,640]{1,0:T(8,128)(2,1)S(1)} %get-tuple-element.38), channel_id=1, source_target_pairs={{0,8},{4,12},{8,0},{12,4},{16,24},{20,28},{24,16},{28,20},{1,9},{5... | collective-permute-start | bytes 307208 | tf_op jit(solution)/shard_map/ppermute | solution.py:613
  54.0 3.2 %collective-permute-done.13.refs_6_ = bf16[80,640]{1,0:T(8,128)(2,1)S(1)} collective-permute-done((bf16[80,640]{1,0:T(8,128)(2,1)S(1)}, bf16[80,640]{1,0:T(8,128)(2,1)S(1)}, u32[]{:S(2)}, u32[]{:S(2)}) %collective-permute-start.13) | collective-permute-done | bytes 102432 | tf_op jit(solution)/shard_map/ppermute | solution.py:613
  57.1 1.4 %collective-permute-done.12.refs_5_ = bf16[80,640]{1,0:T(8,128)(2,1)S(1)} collective-permute-done((bf16[80,640]{1,0:T(8,128)(2,1)S(1)}, bf16[80,640]{1,0:T(8,128)(2,1)S(1)}, u32[]{:S(2)}, u32[]{:S(2)}) %collective-permute-start.12) | collective-permute-done | bytes 102432 | tf_op jit(solution)/shard_map/ppermute | solution.py:613
  59.4 10.2 %all_gather.3.refs_1_ = bf16[640,640]{1,0:T(8,128)(2,1)S(1)} all-gather(bf16[80,640]{1,0:T(8,128)(2,1)S(1)} %get-tuple-element.34), channel_id=1, replica_groups=mesh['lat'=8,'lon'=4] {'lat'}, dimensions={0}, use_global_device_ids=true | all-gather | bytes 921600 | tf_op jit(solution)/shard_map/all_gather | solution.py:627
  69.6 2.1 %inverse.3.refs_3_.refs_0_ = bf16[32,640]{1,0:T(8,128)(2,1)S(1)} custom-call(s32[32]{0:T(128)S(1)} %slice.73.refs_0_, bf16[640,640]{1,0:T(8,128)(2,1)S(1)} %all_gather.3.refs_1_, bf16[160,80,640]{2,1,0:T(8,128)(2,1)S(1)} %load_table.1.refs_6_.refs_2_), custom_call_target="tpu_custom_call" | custom-call | bytes 7325999 | tf_op jit(solution)/shard_map/inverse/pallas_call | solution.py:631
  71.7 3.5 %inverse.4.refs_3_.refs_0_ = bf16[64,640]{1,0:T(8,128)(2,1)S(1)} custom-call(s32[64]{0:T(128)S(1)} %get-tuple-element.54.refs_0_, bf16[640,640]{1,0:T(8,128)(2,1)S(1)} %all_gather.3.refs_1_, bf16[160,80,640]{2,1,0:T(8,128)(2,1)S(1)} %load_table.1.refs_6_.refs_2_, bf16[32,640]{1,0:T(8,128)(2,1)S(1)} %inverse.3.refs_3_.refs_0_), custom_call_target="tpu_custom_call" | custom-call | bytes 13661999 | tf_op jit(solution)/shard_map/inverse/pallas_call | solution.py:631
  75.3 3.5 %inverse.5.refs_0_ = bf16[64,640]{1,0:T(8,128)(2,1)S(1)} custom-call(s32[64]{0:T(128)S(1)} %get-tuple-element.55.refs_0_, bf16[640,640]{1,0:T(8,128)(2,1)S(1)} %all_gather.3.refs_1_, bf16[160,80,640]{2,1,0:T(8,128)(2,1)S(1)} %load_table.1.refs_6_.refs_2_, bf16[64,640]{1,0:T(8,128)(2,1)S(1)} %inverse.4.refs_3_.refs_0_), custom_call_target="tpu_custom_call" | custom-call | bytes 13661999 | tf_op jit(solution)/shard_map/inverse/pallas_call | solution.py:631
  78.9 3.0 %collective-permute-start.15 = (bf16[64,640]{1,0:T(8,128)(2,1)S(1)}, bf16[64,640]{1,0:T(8,128)(2,1)S(1)}, u32[]{:S(2)}, u32[]{:S(2)}) collective-permute-start(bf16[64,640]{1,0:T(8,128)(2,1)S(1)} %inverse.5.refs_0_), channel_id=1, source_target_pairs={{0,2},{1,3},{2,0},{3,1},{4,6},{5,7},{6,4},{7,5},{8,10},{9,11},{10,... | collective-permute-start | bytes 245768 | tf_op jit(solution)/shard_map/ppermute | solution.py:554
  81.9 2.1 %collective-permute-start.20 = (bf16[32,640]{1,0:T(8,128)(2,1)S(1)}, bf16[32,640]{1,0:T(8,128)(2,1)S(1)}, u32[]{:S(2)}, u32[]{:S(2)}) collective-permute-start(bf16[32,640]{1,0:T(8,128)(2,1)S(1)} %inverse.3.refs_3_.refs_0_), channel_id=1, source_target_pairs={{0,1},{1,0},{2,3},{3,2},{4,5},{5,4},{6,7},{7,6},{8,9},{9,8},{10,11... | collective-permute-start | bytes 122888 | tf_op jit(solution)/shard_map/ppermute | solution.py:551
  84.0 2.0 %collective-permute-start.19 = (bf16[64,640]{1,0:T(8,128)(2,1)S(1)}, bf16[64,640]{1,0:T(8,128)(2,1)S(1)}, u32[]{:S(2)}, u32[]{:S(2)}) collective-permute-start(bf16[64,640]{1,0:T(8,128)(2,1)S(1)} %collective-permute-done.18.refs_2_), channel_id=1, source_target_pairs={{0,1},{1,0},{2,3},{3,2},{4,5},{5,4},{6,7},{7,6},{8,9},{9,8},{10,11... | collective-permute-start | bytes 245768 | tf_op jit(solution)/shard_map/ppermute | solution.py:555
  86.0 2.1 %collective-permute-done.21.refs_2_ = bf16[32,640]{1,0:T(8,128)(2,1)S(1)} collective-permute-done((bf16[32,640]{1,0:T(8,128)(2,1)S(1)}, bf16[32,640]{1,0:T(8,128)(2,1)S(1)}, u32[]{:S(2)}, u32[]{:S(2)}) %collective-permute-start.21) | collective-permute-done | bytes 40992 | tf_op jit(solution)/shard_map/ppermute | solution.py:554
  88.2 2.0 %collective-permute-start.16 = (bf16[64,640]{1,0:T(8,128)(2,1)S(1)}, bf16[64,640]{1,0:T(8,128)(2,1)S(1)}, u32[]{:S(2)}, u32[]{:S(2)}) collective-permute-start(bf16[64,640]{1,0:T(8,128)(2,1)S(1)} %collective-permute-done.15.refs_2_), channel_id=1, source_target_pairs={{0,1},{1,0},{2,3},{3,2},{4,5},{5,4},{6,7},{7,6},{8,9},{9,8},{10,11... | collective-permute-start | bytes 245768 | tf_op jit(solution)/shard_map/ppermute | solution.py:555
  91.3 3.9 %collective-permute-done.22.refs_3_ = bf16[32,640]{1,0:T(8,128)(2,1)S(1)} collective-permute-done((bf16[32,640]{1,0:T(8,128)(2,1)S(1)}, bf16[32,640]{1,0:T(8,128)(2,1)S(1)}, u32[]{:S(2)}, u32[]{:S(2)}) %collective-permute-start.22) | collective-permute-done | bytes 40992 | tf_op jit(solution)/shard_map/ppermute | solution.py:555
  97.2 2.1 %values.5 = f32[320,640]{1,0:T(8,128)} custom-call(f32[640,256]{1,0:T(8,128)S(1)} %pad_maximum_fusion.refs_4_.near_ref, f32[640,10]{1,0:T(8,128)S(1)} %broadcast_multiply_fusion.refs_5_.far_ref, bf16[64,640]{1,0:T(8,128)(2,1)S(1)} %inverse.5.refs_0_, bf16[64,640]{1,0:T(8,128)(2,1)S(1)} %collective-permute-done.14.refs_1_, ...), custom_call_target="tpu_custom_call" | custom-call | bytes 5280000 | tf_op jit(solution)/shard_map/values/pallas_call | solution.py:656
  (58 shorter events, 10.4 us)
Async XLA Ops:
  2.0 10.7 %collective-permute-start = (f32[4,640]{1,0:T(4,128)S(1)}, f32[4,640]{1,0:T(4,128)S(1)}, u32[]{:S(2)}, u32[]{:S(2)}) collective-permute-start(f32[4,640]{1,0:T(4,128)S(1)} %get-tuple-element.21), channel_id=1, source_target_pairs={{0,4},{4,8},{8,12},{12,16},{16,20},{20,24},{24,28},{28,0},{1,5},{5... | collective-permute-start | bytes 30728 | tf_op jit(solution)/shard_map/ppermute | solution.py:488
  2.6 10.2 %collective-permute-start.1 = (f32[4,640]{1,0:T(4,128)S(1)}, f32[4,640]{1,0:T(4,128)S(1)}, u32[]{:S(2)}, u32[]{:S(2)}) collective-permute-start(f32[4,640]{1,0:T(4,128)S(1)} %get-tuple-element.22), channel_id=1, source_target_pairs={{4,0},{8,4},{12,8},{16,12},{20,16},{24,20},{28,24},{0,28},{5,1},{9... | collective-permute-start | bytes 30728 | tf_op jit(solution)/shard_map/ppermute | solution.py:489
  5.5 7.2 %collective-permute-start.2 = (f32[80,4]{1,0:T(8,128)S(1)}, f32[80,4]{1,0:T(8,128)S(1)}, u32[]{:S(2)}, u32[]{:S(2)}) collective-permute-start(f32[80,4]{1,0:T(8,128)S(1)} %get-tuple-element.23), channel_id=1, source_target_pairs={{0,1},{1,2},{2,3},{3,0},{4,5},{5,6},{6,7},{7,4},{8,9},{9,10},{10,1... | collective-permute-start | bytes 3848 | tf_op jit(solution)/shard_map/ppermute | solution.py:490
  7.8 5.0 %collective-permute-start.3 = (f32[80,4]{1,0:T(8,128)S(1)}, f32[80,4]{1,0:T(8,128)S(1)}, u32[]{:S(2)}, u32[]{:S(2)}) collective-permute-start(f32[80,4]{1,0:T(8,128)S(1)} %get-tuple-element.24), channel_id=1, source_target_pairs={{1,0},{2,1},{3,2},{0,3},{5,4},{6,5},{7,6},{4,7},{9,8},{10,9},{11,1... | collective-permute-start | bytes 3848 | tf_op jit(solution)/shard_map/ppermute | solution.py:491
  12.8 0.7 copy-start.1
  19.6 9.4 %collective-permute-start.4 = (bf16[2,32,640]{2,1,0:T(8,128)(2,1)S(1)}, bf16[2,32,640]{2,1,0:T(8,128)(2,1)S(1)}, u32[]{:S(2)}, u32[]{:S(2)}) collective-permute-start(bf16[2,32,640]{2,1,0:T(8,128)(2,1)S(1)} %get-tuple-element.29), channel_id=1, source_target_pairs={{0,1},{1,0},{2,3},{3,2},{4,5},{5,4},{6,7},{7,6},{8,9},{9,8},{10,11... | collective-permute-start | bytes 245768 | tf_op jit(solution)/shard_map/ppermute | solution.py:543
  21.1 10.8 %collective-permute-start.6 = (bf16[2,64,640]{2,1,0:T(8,128)(2,1)S(1)}, bf16[2,64,640]{2,1,0:T(8,128)(2,1)S(1)}, u32[]{:S(2)}, u32[]{:S(2)}) collective-permute-start(bf16[2,64,640]{2,1,0:T(8,128)(2,1)S(1)} %get-tuple-element.30), channel_id=1, source_target_pairs={{0,1},{1,0},{2,3},{3,2},{4,5},{5,4},{6,7},{7,6},{8,9},{9,8},{10,11... | collective-permute-start | bytes 491528 | tf_op jit(solution)/shard_map/ppermute | solution.py:543
  22.6 9.5 %collective-permute-start.8 = (bf16[2,64,640]{2,1,0:T(8,128)(2,1)S(1)}, bf16[2,64,640]{2,1,0:T(8,128)(2,1)S(1)}, u32[]{:S(2)}, u32[]{:S(2)}) collective-permute-start(bf16[2,64,640]{2,1,0:T(8,128)(2,1)S(1)} %get-tuple-element.31), channel_id=1, source_target_pairs={{0,1},{1,0},{2,3},{3,2},{4,5},{5,4},{6,7},{7,6},{8,9},{9,8},{10,11... | collective-permute-start | bytes 491528 | tf_op jit(solution)/shard_map/ppermute | solution.py:543
  29.0 16.9 %collective-permute-start.5 = (bf16[32,640]{1,0:T(8,128)(2,1)S(1)}, bf16[32,640]{1,0:T(8,128)(2,1)S(1)}, u32[]{:S(2)}, u32[]{:S(2)}) collective-permute-start(bf16[32,640]{1,0:T(8,128)(2,1)S(1)} %get-tuple-element.44), channel_id=1, source_target_pairs={{0,2},{1,3},{2,0},{3,1},{4,6},{5,7},{6,4},{7,5},{8,10},{9,11},{10,... | collective-permute-start | bytes 122888 | tf_op jit(solution)/shard_map/ppermute | solution.py:547
  31.9 7.6 %collective-permute-start.7 = (bf16[64,640]{1,0:T(8,128)(2,1)S(1)}, bf16[64,640]{1,0:T(8,128)(2,1)S(1)}, u32[]{:S(2)}, u32[]{:S(2)}) collective-permute-start(bf16[64,640]{1,0:T(8,128)(2,1)S(1)} %get-tuple-element.42), channel_id=1, source_target_pairs={{0,2},{1,3},{2,0},{3,1},{4,6},{5,7},{6,4},{7,5},{8,10},{9,11},{10,... | collective-permute-start | bytes 245768 | tf_op jit(solution)/shard_map/ppermute | solution.py:547
  32.1 10.5 %collective-permute-start.9 = (bf16[64,640]{1,0:T(8,128)(2,1)S(1)}, bf16[64,640]{1,0:T(8,128)(2,1)S(1)}, u32[]{:S(2)}, u32[]{:S(2)}) collective-permute-start(bf16[64,640]{1,0:T(8,128)(2,1)S(1)} %get-tuple-element.40), channel_id=1, source_target_pairs={{0,2},{1,3},{2,0},{3,1},{4,6},{5,7},{6,4},{7,5},{8,10},{9,11},{10,... | collective-permute-start | bytes 245768 | tf_op jit(solution)/shard_map/ppermute | solution.py:547
  42.7 15.9 %copy-start = (f32[2,2]{1,0:T(2,128)S(1)}, f32[2,2]{1,0:T(2,128)}, u32[]{:S(2)}) copy-start(f32[2,2]{1,0:T(2,128)} %refs_2_.1) | copy-start | bytes 52
  42.7 15.9 %copy-start.2 = (f32[2]{0:T(128)S(1)}, f32[2]{0:T(128)}, u32[]{:S(2)}) copy-start(f32[2]{0:T(128)} %refs_1_.1) | copy-start | bytes 28
  47.9 2.4 %collective-permute-start.10 = (f32[4,80,640]{2,1,0:T(8,128)S(1)}, f32[4,80,640]{2,1,0:T(8,128)S(1)}, u32[]{:S(2)}, u32[]{:S(2)}) collective-permute-start(f32[4,80,640]{2,1,0:T(8,128)S(1)} %get-tuple-element.33), channel_id=1, source_target_pairs={{0,4},{4,0},{8,12},{12,8},{16,20},{20,16},{24,28},{28,24},{1,5},{5... | collective-permute-start | bytes 2457608 | tf_op jit(solution)/shard_map/ppermute | solution.py:610
  50.4 6.7 %collective-permute-start.13 = (bf16[80,640]{1,0:T(8,128)(2,1)S(1)}, bf16[80,640]{1,0:T(8,128)(2,1)S(1)}, u32[]{:S(2)}, u32[]{:S(2)}) collective-permute-start(bf16[80,640]{1,0:T(8,128)(2,1)S(1)} %get-tuple-element.36), channel_id=1, source_target_pairs={{0,24},{4,28},{8,16},{12,20},{16,8},{20,12},{24,0},{28,4},{1,25},{... | collective-permute-start | bytes 307208 | tf_op jit(solution)/shard_map/ppermute | solution.py:613
  51.7 6.8 %collective-permute-start.12 = (bf16[80,640]{1,0:T(8,128)(2,1)S(1)}, bf16[80,640]{1,0:T(8,128)(2,1)S(1)}, u32[]{:S(2)}, u32[]{:S(2)}) collective-permute-start(bf16[80,640]{1,0:T(8,128)(2,1)S(1)} %get-tuple-element.37), channel_id=1, source_target_pairs={{0,16},{4,20},{8,24},{12,28},{16,0},{20,4},{24,8},{28,12},{1,17},{... | collective-permute-start | bytes 307208 | tf_op jit(solution)/shard_map/ppermute | solution.py:613
  52.7 5.9 %collective-permute-start.11 = (bf16[80,640]{1,0:T(8,128)(2,1)S(1)}, bf16[80,640]{1,0:T(8,128)(2,1)S(1)}, u32[]{:S(2)}, u32[]{:S(2)}) collective-permute-start(bf16[80,640]{1,0:T(8,128)(2,1)S(1)} %get-tuple-element.38), channel_id=1, source_target_pairs={{0,8},{4,12},{8,0},{12,4},{16,24},{20,28},{24,16},{28,20},{1,9},{5... | collective-permute-start | bytes 307208 | tf_op jit(solution)/shard_map/ppermute | solution.py:613
  75.3 8.8 %collective-permute-start.18 = (bf16[64,640]{1,0:T(8,128)(2,1)S(1)}, bf16[64,640]{1,0:T(8,128)(2,1)S(1)}, u32[]{:S(2)}, u32[]{:S(2)}) collective-permute-start(bf16[64,640]{1,0:T(8,128)(2,1)S(1)} %inverse.4.refs_3_.refs_0_), channel_id=1, source_target_pairs={{0,2},{1,3},{2,0},{3,1},{4,6},{5,7},{6,4},{7,5},{8,10},{9,11},{10,... | collective-permute-start | bytes 245768 | tf_op jit(solution)/shard_map/ppermute | solution.py:554
  78.9 9.3 %collective-permute-start.15 = (bf16[64,640]{1,0:T(8,128)(2,1)S(1)}, bf16[64,640]{1,0:T(8,128)(2,1)S(1)}, u32[]{:S(2)}, u32[]{:S(2)}) collective-permute-start(bf16[64,640]{1,0:T(8,128)(2,1)S(1)} %inverse.5.refs_0_), channel_id=1, source_target_pairs={{0,2},{1,3},{2,0},{3,1},{4,6},{5,7},{6,4},{7,5},{8,10},{9,11},{10,... | collective-permute-start | bytes 245768 | tf_op jit(solution)/shard_map/ppermute | solution.py:554
  81.9 6.3 %collective-permute-start.21 = (bf16[32,640]{1,0:T(8,128)(2,1)S(1)}, bf16[32,640]{1,0:T(8,128)(2,1)S(1)}, u32[]{:S(2)}, u32[]{:S(2)}) collective-permute-start(bf16[32,640]{1,0:T(8,128)(2,1)S(1)} %inverse.3.refs_3_.refs_0_), channel_id=1, source_target_pairs={{0,2},{1,3},{2,0},{3,1},{4,6},{5,7},{6,4},{7,5},{8,10},{9,11},{10,... | collective-permute-start | bytes 122888 | tf_op jit(solution)/shard_map/ppermute | solution.py:554
  81.9 8.3 %collective-permute-start.20 = (bf16[32,640]{1,0:T(8,128)(2,1)S(1)}, bf16[32,640]{1,0:T(8,128)(2,1)S(1)}, u32[]{:S(2)}, u32[]{:S(2)}) collective-permute-start(bf16[32,640]{1,0:T(8,128)(2,1)S(1)} %inverse.3.refs_3_.refs_0_), channel_id=1, source_target_pairs={{0,1},{1,0},{2,3},{3,2},{4,5},{5,4},{6,7},{7,6},{8,9},{9,8},{10,11... | collective-permute-start | bytes 122888 | tf_op jit(solution)/shard_map/ppermute | solution.py:551
  84.0 12.0 %collective-permute-start.17 = (bf16[64,640]{1,0:T(8,128)(2,1)S(1)}, bf16[64,640]{1,0:T(8,128)(2,1)S(1)}, u32[]{:S(2)}, u32[]{:S(2)}) collective-permute-start(bf16[64,640]{1,0:T(8,128)(2,1)S(1)} %inverse.4.refs_3_.refs_0_), channel_id=1, source_target_pairs={{0,1},{1,0},{2,3},{3,2},{4,5},{5,4},{6,7},{7,6},{8,9},{9,8},{10,11... | collective-permute-start | bytes 245768 | tf_op jit(solution)/shard_map/ppermute | solution.py:551
  84.0 11.9 %collective-permute-start.19 = (bf16[64,640]{1,0:T(8,128)(2,1)S(1)}, bf16[64,640]{1,0:T(8,128)(2,1)S(1)}, u32[]{:S(2)}, u32[]{:S(2)}) collective-permute-start(bf16[64,640]{1,0:T(8,128)(2,1)S(1)} %collective-permute-done.18.refs_2_), channel_id=1, source_target_pairs={{0,1},{1,0},{2,3},{3,2},{4,5},{5,4},{6,7},{7,6},{8,9},{9,8},{10,11... | collective-permute-start | bytes 245768 | tf_op jit(solution)/shard_map/ppermute | solution.py:555
  88.2 9.0 %collective-permute-start.14 = (bf16[64,640]{1,0:T(8,128)(2,1)S(1)}, bf16[64,640]{1,0:T(8,128)(2,1)S(1)}, u32[]{:S(2)}, u32[]{:S(2)}) collective-permute-start(bf16[64,640]{1,0:T(8,128)(2,1)S(1)} %inverse.5.refs_0_), channel_id=1, source_target_pairs={{0,1},{1,0},{2,3},{3,2},{4,5},{5,4},{6,7},{7,6},{8,9},{9,8},{10,11... | collective-permute-start | bytes 245768 | tf_op jit(solution)/shard_map/ppermute | solution.py:551
  88.2 9.0 %collective-permute-start.16 = (bf16[64,640]{1,0:T(8,128)(2,1)S(1)}, bf16[64,640]{1,0:T(8,128)(2,1)S(1)}, u32[]{:S(2)}, u32[]{:S(2)}) collective-permute-start(bf16[64,640]{1,0:T(8,128)(2,1)S(1)} %collective-permute-done.15.refs_2_), channel_id=1, source_target_pairs={{0,1},{1,0},{2,3},{3,2},{4,5},{5,4},{6,7},{7,6},{8,9},{9,8},{10,11... | collective-permute-start | bytes 245768 | tf_op jit(solution)/shard_map/ppermute | solution.py:555
  90.2 4.9 %collective-permute-start.22 = (bf16[32,640]{1,0:T(8,128)(2,1)S(1)}, bf16[32,640]{1,0:T(8,128)(2,1)S(1)}, u32[]{:S(2)}, u32[]{:S(2)}) collective-permute-start(bf16[32,640]{1,0:T(8,128)(2,1)S(1)} %collective-permute-done.21.refs_2_), channel_id=1, source_target_pairs={{0,1},{1,0},{2,3},{3,2},{4,5},{5,4},{6,7},{7,6},{8,9},{9,8},{10,11... | collective-permute-start | bytes 122888 | tf_op jit(solution)/shard_map/ppermute | solution.py:555

commit v2 on v1

--- a/solution.py
+++ b/solution.py
@@ -6,6 +6,7 @@
 from jax.experimental import pallas as pl
 from jax.experimental.pallas import tpu as pltpu
 from jax.sharding import PartitionSpec as P
+
 
 NLON = 2560
 M = 640
@@ -176,21 +177,13 @@
     winds_copy.wait()
 
 
-def load_table_kernel(after_ref, table_hbm, table_ref, semaphores):
-    parts = semaphores.shape[0]
-    share = table_ref.shape[0] // parts
-    copies = [
-        pltpu.make_async_copy(
-            table_hbm.at[pl.ds(i * share, share)],
-            table_ref.at[pl.ds(i * share, share)],
-            semaphores.at[i],
-        )
-        for i in range(parts)
-    ]
-    for copy in copies:
-        copy.start()
-    for copy in copies:
-        copy.wait()
+def table_copy(table_hbm, table_ref, first, step, semaphores):
+    at = pl.multiple_of(step * GROUP, GROUP)
+    return pltpu.make_async_copy(
+        table_hbm.at[pl.ds(first + at, GROUP)],
+        table_ref.at[pl.ds(at, GROUP)],
+        semaphores.at[step],
+    )
 
 
 def advance(flags, fields_ref, wind_ref, step_ref, above, below, before, after, stepped_ref):
@@ -256,8 +249,8 @@
     blocks, sections, rows, degree_dev, first, last, waves_ref, place_ref, *refs
 ):
     received = refs[:blocks]
-    weight_ref, table_ref = refs[blocks : blocks + 2]
-    rest = refs[blocks + 2 :]
+    weight_ref, table_hbm = refs[blocks : blocks + 2]
+    *rest, table_ref, semaphores = refs[blocks + 2 :]
     spread_ref, kept_ref, turned_ref = rest[-3:]
     step = pl.program_id(0)
     half = sections // 2
@@ -268,6 +261,8 @@
 
     @pl.when(step == 0)
     def _():
+        for i in range(share // group):
+            table_copy(table_hbm, table_ref, first, i, semaphores).start()
         total = received[0][...].astype(F32)
         for other in received[1:]:
             total = total + other[...].astype(F32)
@@ -278,6 +273,7 @@
                     at = ((c * levels + level) * 2 + h) * rows
                     spread_ref[:, h * half + level * 2 + c, 0:rows] = total[:, at : at + rows]
 
+    table_copy(table_hbm, table_ref, first, step, semaphores).wait()
     degree = lax.broadcasted_iota(jnp.int32, (2 * half, columns), 1)
     row = lax.broadcasted_iota(jnp.int32, (2 * half, 1), 0)
     for u in range(0, group, 2):
@@ -285,7 +281,7 @@
         for v in (u, u + 1):
             high, low = split_halves(spread_ref[step * group + v, :, 0:rows])
             both = jnp.concatenate([high.astype(F32), low.astype(F32)], axis=0).astype(BF16)
-            total = jnp.dot(both, table_ref[first + step * group + v], preferred_element_type=F32)
+            total = jnp.dot(both, table_ref[step * group + v], preferred_element_type=F32)
             sums.append(total[:sections] + total[sections:])
         north = jnp.concatenate([sums[0][:half], sums[1][:half]], axis=0)
         south = jnp.concatenate([sums[0][half:], sums[1][half:]], axis=0)
@@ -347,7 +343,8 @@
         at, slot = at + levels * wide, slot + share
 
 
-def inverse_kernel(sections, rows, first, waves_ref, joined_ref, table_ref, out_ref, kept_ref, spread_ref):
+def inverse_kernel(sections, rows, first, waves_ref, joined_ref, table_hbm, *refs):
+    own_ref, out_ref, kept_ref, spread_ref, table_ref, semaphores = refs
     step = pl.program_id(0)
     half = sections // 2
     levels = half // 2
@@ -357,6 +354,8 @@
 
     @pl.when(step == 0)
     def _():
+        for i in range(share // group):
+            table_copy(table_hbm, table_ref, first, i, semaphores).start()
         for t in range(columns // LANES):
             tile = joined_ref[t * LANES : (t + 1) * LANES, half * first : half * (first + share)]
             turned = tile.astype(F32).T
@@ -368,6 +367,7 @@
     degree = lax.broadcasted_iota(jnp.int32, (2 * half, columns), 1)
     row = lax.broadcasted_iota(jnp.int32, (2 * half, 1), 0)
     upper = row < half
+    table_copy(table_hbm, table_ref, first, step, semaphores).wait()
     for u in range(0, group, 2):
         slot = step * group + u
         at = pl.ds(pl.multiple_of(slot * half, 2 * half), 2 * half)
@@ -379,7 +379,7 @@
         odds = pltpu.roll(jnp.where(even, 0.0, values), half, 0)
         for v in range(2):
             both = jnp.where(upper, odds, evens) if v else jnp.where(upper, evens, odds)
-            sums = dot_rows(both.astype(BF16), table_ref[first + slot + v])
+            sums = dot_rows(both.astype(BF16), table_ref[slot + v])
             factor = jnp.where(waves_ref[slot + v] == 0, 1.0, 2.0) / math.sqrt(M)
             sums = sums * factor
             swapped = pltpu.roll(sums, half, 0)
@@ -392,19 +392,20 @@
             for level in range(levels):
                 for h in range(2):
                     at = ((c * levels + level) * 2 + h) * rows
-                    out_ref[:, at : at + rows] = spread_ref[
-                        :, h * half + level * 2 + c, 0:rows
-                    ].astype(out_ref.dtype)
+                    value = spread_ref[:, h * half + level * 2 + c, 0:rows]
+                    own_ref[:, at : at + rows] = value
+                    out_ref[:, at : at + rows] = value.astype(out_ref.dtype)
 
 
 def zonal_values(blocks, share, first, near, far, received, total):
     for part in range(2):
         count = received[0].shape[1] // 2
         rows_high, rows_low = split_halves(table_rows(near, far, first, share, blocks, part))
-        coefs = jnp.concatenate(
-            [other[:, part * count : (part + 1) * count] for other in received], axis=0
-        )
+        lanes = slice(part * count, (part + 1) * count)
+        own_high, own_low = split_halves(received[0][:, lanes])
+        coefs = jnp.concatenate([own_high] + [other[:, lanes] for other in received[1:]], axis=0)
         term = dot_columns(coefs, rows_high) + dot_columns(coefs, rows_low)
+        term = term + dot_columns(own_low, rows_high[:share])
         total = term if total is None else total + term
     return total
 
@@ -430,7 +431,7 @@
     return pl.BlockSpec(shape, lambda *_: (0,) * len(shape))
 
 
-def shards(
+def tiled(
     level_fields, wind_field, zonal_step, quad_weight, legendre, wave_table, damping, vertical
 ):
     levels, hemis, rows_half, lon_dev = level_fields.shape
@@ -438,27 +439,6 @@
     lat_count = lax.axis_size("lat")
     lon_count = lax.axis_size("lon")
     degree_dev = columns // lat_count
-    if (
-        rows_half % 16
-        or degree_dev % 16
-        or lon_dev % LANES
-        or slots_dev != sum(CUTS)
-        or levels != 2
-        or lat_count & (lat_count - 1)
-        or lat_count < 4
-        or lon_count & (lon_count - 1)
-        or lon_count < 4
-    ):
-        return untiled(
-            level_fields,
-            wind_field,
-            zonal_step,
-            quad_weight,
-            legendre,
-            wave_table,
-            damping,
-            vertical,
-        )
     lat_index = lax.axis_index("lat")
     lon_index = lax.axis_index("lon")
     planes = levels * hemis
@@ -510,8 +490,10 @@
     def sums_shape(share):
         return [like((lon_count // 2, share, width), dtype) for dtype in (F32, BF16)]
 
+    table = pltpu.with_memory_space_constraint(legendre, pltpu.HBM)
+
     def first_sums(flags_ref, fields_ref, winds_ref, step_ref, *refs):
-        edges, near_ref, far_ref, stepped_ref = refs[:4], refs[4], refs[5], refs[6]
+        edges, near_ref, far_ref, stepped_ref = refs[:4], *refs[4:7]
         advance(flags_ref, fields_ref, winds_ref, step_ref, *edges, stepped_ref)
         zonal_sums(lon_count, CUTS[0], 0, stepped_ref, near_ref, far_ref, refs[7:])
 
@@ -520,12 +502,16 @@
         out_shape=[like((grid_count, lon_dev), F32)] + sums_shape(CUTS[0]),
         in_specs=[SMEM] + [VMEM] * 9,
         out_specs=[VMEM] * 3,
-        compiler_params=grant(24),
+        compiler_params=grant(20),
         cost_estimate=cost(3.0),
         name="advance_and_sums",
-    )(flags, fields, winds, zonal_step[None, :], above, below, before, after, near, far)
-
-    def later_sums(share, first, after):
+    )(
+        flags, fields, winds, zonal_step[None, :], above, below, before, after, near, far
+    )
+
+    def later_sums(chunk, first, after):
+        share = CUTS[chunk]
+
         def body(stepped_ref, near_ref, far_ref, after_ref, *outs):
             zonal_sums(lon_count, share, first, stepped_ref, near_ref, far_ref, outs)
 
@@ -534,42 +520,35 @@
             out_shape=sums_shape(share),
             in_specs=[VMEM] * 4,
             out_specs=[VMEM] * 2,
-            compiler_params=grant(24),
-            cost_estimate=cost(0.025 * share),
+            compiler_params=grant(20),
+            cost_estimate=cost(0.035 * share),
             name="sums",
         )(stepped, near, far, after)
 
+    def swap(value, axis, step):
+        return lax.ppermute(value, axis, pairs(lax.axis_size(axis), step))
+
     def to_owners(own, pair):
-        pair = lax.ppermute(pair, "lon", pairs(lon_count, 1))
+        pair = swap(pair, "lon", 1)
         parts = [own[0], pair[0]]
         for k in range(1, lon_count // 2):
             joint = (own[k] + pair[k].astype(F32)).astype(BF16)
-            parts.append(lax.ppermute(joint, "lon", pairs(lon_count, 2 * k)))
+            parts.append(swap(joint, "lon", 2 * k))
         return parts
 
-    def from_owners(coefs):
-        near_by = lax.ppermute(coefs, "lon", pairs(lon_count, 1))
-        parts = [coefs, near_by]
+    def from_owners(own, coefs):
+        parts = [own, swap(coefs, "lon", 1)]
         for k in range(1, lon_count // 2):
-            distant = lax.ppermute(coefs, "lon", pairs(lon_count, 2 * k))
-            parts += [distant, lax.ppermute(distant, "lon", pairs(lon_count, 1))]
+            distant = swap(coefs, "lon", 2 * k)
+            parts += [distant, swap(distant, "lon", 1)]
         return parts
 
     swapped, first = [to_owners(*pieces)], CUTS[0]
-    for share in CUTS[1:]:
-        pieces = later_sums(share, first, pieces[0])
+    for chunk in range(1, len(CUTS)):
+        pieces = later_sums(chunk, first, pieces[0])
         swapped.append(to_owners(*pieces))
-        first += share
-    table = pl.pallas_call(
-        load_table_kernel,
-        out_shape=pltpu.VMEM(legendre.shape, BF16),
-        in_specs=[VMEM, HBM],
-        out_specs=VMEM,
-        scratch_shapes=[pltpu.SemaphoreType.DMA((4,))],
-        compiler_params=grant(8),
-        cost_estimate=cost(5.7),
-        name="load_table",
-    )(pieces[0], pltpu.with_memory_space_constraint(legendre, pltpu.HBM))
+        first += CUTS[chunk]
+
 
     def forward(first, share, parts, earlier, last):
         if last:
@@ -586,13 +565,15 @@
                 num_scalar_prefetch=2,
                 grid=(share // GROUP,),
                 in_specs=[whole_block((share, width))] * len(parts)
-                + [whole_block((1, width)), VMEM]
+                + [whole_block((1, width)), HBM]
                 + [whole_block(other.shape) for other in earlier],
                 out_specs=[whole_block(shape.shape) for shape in shapes],
                 scratch_shapes=[
                     pltpu.VMEM((share, sections, LANES), F32),
                     pltpu.VMEM((columns // LANES, half * share, LANES), F32),
                     pltpu.VMEM((columns, half * share), F32),
+                    pltpu.VMEM((share, rows_half, columns), BF16),
+                    pltpu.SemaphoreType.DMA((share // GROUP,)),
                 ],
             ),
             compiler_params=grant(20),
@@ -601,18 +582,15 @@
         )(my_waves[first : first + share], place, *parts, weight_row, table, *earlier)
 
     earlier, first = [], 0
-    for share, parts in zip(CUTS, swapped):
-        last = first + share == slots_dev
-        earlier = earlier + list(forward(first, share, parts, earlier, last))
+    for chunk, share in enumerate(CUTS):
+        last = chunk == len(CUTS) - 1
+        earlier += forward(first, share, swapped[chunk], earlier, last)
         first += share
     own, other = earlier[-2:]
 
-    other = lax.ppermute(other, "lat", pairs(lat_count, 1))
+    other = swap(other, "lat", 1)
     sums = [own[j] + other[j] for j in range(lat_count // 2)]
-    sums = [sums[0]] + [
-        lax.ppermute(sums[j].astype(BF16), "lat", pairs(lat_count, 2 * j))
-        for j in range(1, lat_count // 2)
-    ]
+    sums = [sums[0]] + [swap(sums[j], "lat", 2 * j) for j in range(1, lat_count // 2)]
     rounded, spectrum = pl.pallas_call(
         lambda *refs: correct_kernel(CUTS, levels, *refs),
         out_shape=[
@@ -630,15 +608,17 @@
         count = 3 + len(after)
         return pl.pallas_call(
             lambda *refs: inverse_kernel(sections, rows_half, first, *refs[:3], *refs[count:]),
-            out_shape=like((share, width), BF16),
+            out_shape=[like((share, width), F32), like((share, width), BF16)],
             grid_spec=pltpu.PrefetchScalarGridSpec(
                 num_scalar_prefetch=1,
                 grid=(share // GROUP,),
-                in_specs=[whole_block(joined.shape), VMEM] + [VMEM] * len(after),
-                out_specs=whole_block((share, width)),
+                in_specs=[whole_block(joined.shape), HBM] + [VMEM] * len(after),
+                out_specs=[whole_block((share, width))] * 2,
                 scratch_shapes=[
                     pltpu.VMEM((columns // LANES, half * share, LANES), F32),
                     pltpu.VMEM((share, sections, LANES), F32),
+                    pltpu.VMEM((share, rows_half, columns), BF16),
+                    pltpu.SemaphoreType.DMA((share // GROUP,)),
                 ],
             ),
             compiler_params=grant(20),
@@ -664,12 +644,48 @@
         )(near, far, *parts, *base)
 
     base, first, coefs = [], slots_dev, []
-    for share in reversed(CUTS):
+    for chunk in reversed(range(len(CUTS))):
+        share = CUTS[chunk]
         first -= share
-        coefs = [inverse(first, share, coefs)]
-        base = [values(first, share, from_owners(coefs[0]), base)]
+        own, sent = inverse(first, share, coefs)
+        coefs = [sent]
+        parts = from_owners(own, sent)
+        base = [values(first, share, parts, base)]
     spectrum = spectrum.reshape(2, levels, degree_dev, slots_dev).transpose(2, 3, 0, 1)
     return (base[0].reshape(level_fields.shape), spectrum)
+
+
+def shards(
+    level_fields, wind_field, zonal_step, quad_weight, legendre, wave_table, damping, vertical
+):
+    levels, _, rows_half, lon_dev = level_fields.shape
+    slots_dev, _, columns = legendre.shape
+    lat_count = lax.axis_size("lat")
+    lon_count = lax.axis_size("lon")
+    degree_dev = columns // lat_count
+    body = tiled
+    if (
+        rows_half % 16
+        or degree_dev % 16
+        or lon_dev % LANES
+        or slots_dev != sum(CUTS)
+        or levels != 2
+        or lat_count & (lat_count - 1)
+        or lat_count < 4
+        or lon_count & (lon_count - 1)
+        or lon_count != 4
+    ):
+        body = untiled
+    return body(
+        level_fields,
+        wind_field,
+        zonal_step,
+        quad_weight,
+        legendre,
+        wave_table,
+        damping,
+        vertical,
+    )
 
 
 def solution(mesh):

time: 99.6 us -> 111 us (1.11)
  waiting for transfers between devices: 17.5 us -> 23.9 us
  Pallas kernels: 35.8 us -> 39.6 us
    ppermute x23, waiting for transfers between devices: 17.5 us -> 23.9 us  [the longest x19 23.9 us: swap(): return lax.ppermute(value, axis, pairs(lax.axis_size(axis), step))]
    pallas_call x4 -> x3, Pallas kernels: 11 us -> 5.26 us  [the longest x1 3.05 us: tiled(): pl.pallas_call(first_sums, out_shape=[like((grid_count, lon_dev), F32)] +...]
    pallas_call x3, Pallas kernels: 8.3 us -> 12.8 us  [forward(): pl.pallas_call(lambda *refs: forward_kernel(len(parts), sections, rows_ha...]
    pallas_call x3, Pallas kernels: 9.22 us -> 13.5 us  [inverse(): pl.pallas_call(lambda *refs: inverse_kernel(sections, rows_half, first, *...]
  transfers between devices with their start and end apart: 23 -> 23, of which waited for: 7 -> 10; matrix products, arithmetic and copies ran while one was open for 5% -> 4% of each run, Pallas kernels for 18% -> 15%
where the time goes in v2:
time: 111 us
  Pallas kernels  39.6 us (36%)
  starting transfers between devices  30 us (27%)
  waiting for transfers between devices  23.9 us (22%)
  blocking collectives  10.9 us (10%)
  local copies, waits for them, and re-layouts  3.55 us (3%)
  other arithmetic  2.02 us (2%)
    ppermute x19, waiting for transfers between devices, swap(): return lax.ppermute(value, axis, pairs(lax.axis_size(axis), step))  23.9 us
    ppermute x19, starting transfers between devices, swap(): return lax.ppermute(value, axis, pairs(lax.axis_size(axis), step))  22.2 us
    pallas_call x3, Pallas kernels, inverse(): pl.pallas_call(lambda *refs: inverse_kernel(sections, rows_half, first, *...  13.5 us
    pallas_call x3, Pallas kernels, forward(): pl.pallas_call(lambda *refs: forward_kernel(len(parts), sections, rows_ha...  12.8 us
    all_gather x1, blocking collectives, tiled(): joined = lax.all_gather(rounded, 'lat', axis=0, tiled=True)  10.9 us
    pallas_call x3, Pallas kernels, values(): pl.pallas_call(body, out_shape=like((grid_count, lon_dev), F32), in_specs...  4.89 us
    pallas_call x2, Pallas kernels, later_sums(): pl.pallas_call(body, out_shape=sums_shape(share), in_specs=[VMEM] * 4, ou...  3.11 us
    pallas_call x1, Pallas kernels, tiled(): pl.pallas_call(first_sums, out_shape=[like((grid_count, lon_dev), F32)] +...  3.05 us
  transfers between devices with their start and end apart: 23, of which 10 were waited for; matrix products, arithmetic and copies ran while one was open for 4% of the time, Pallas kernels for 15%

profile of v2, /device:TPU:0, one launch (start us, length us, event | category | flops | bytes accessed | tf_op | source)
XLA Modules:
  0.0 110.9 jit_solution(15036224484765496150)
XLA Ops:
  0.6 1.4 %load.1 = (f32[4,80,640]{2,1,0:T(8,128)S(1)}, f32[4,80,640]{2,1,0:T(8,128)S(1)}, f32[4,640]{1,0:T(4,128)S(1)}, f32[4,640]{1,0:T(4,128)S(1)}, f32[80,4]{1,0:T(8,128)S(1)}, /*index=5*/f32[80,4]{1,0:T(8,128)S(1)}) custom-call(f32[4,80,640]{2,1,0:T(8,128)} %bitcast.39, f32[4,80,640]{2,1,0:T(8,128)} %bitcast.40), custom_call_target="tpu_custom_call" | custom-call | bytes 4950000 | tf_op jit(solution)/shard_map/load/pallas_call | solution.py:452
  2.6 2.9 %collective-permute-start.1 = (f32[4,640]{1,0:T(4,128)S(1)}, f32[4,640]{1,0:T(4,128)S(1)}, u32[]{:S(2)}, u32[]{:S(2)}) collective-permute-start(f32[4,640]{1,0:T(4,128)S(1)} %get-tuple-element.28), channel_id=1, source_target_pairs={{4,0},{8,4},{12,8},{16,12},{20,16},{24,20},{28,24},{0,28},{5,1},{9... | collective-permute-start | bytes 30728 | tf_op jit(solution)/shard_map/ppermute | solution.py:469
  5.5 2.3 %collective-permute-start.2 = (f32[80,4]{1,0:T(8,128)S(1)}, f32[80,4]{1,0:T(8,128)S(1)}, u32[]{:S(2)}, u32[]{:S(2)}) collective-permute-start(f32[80,4]{1,0:T(8,128)S(1)} %get-tuple-element.29), channel_id=1, source_target_pairs={{0,1},{1,2},{2,3},{3,0},{4,5},{5,6},{6,7},{7,4},{8,9},{9,10},{10,1... | collective-permute-start | bytes 3848 | tf_op jit(solution)/shard_map/ppermute | solution.py:470
  7.8 2.0 %collective-permute-start.3 = (f32[80,4]{1,0:T(8,128)S(1)}, f32[80,4]{1,0:T(8,128)S(1)}, u32[]{:S(2)}, u32[]{:S(2)}) collective-permute-start(f32[80,4]{1,0:T(8,128)S(1)} %get-tuple-element.30), channel_id=1, source_target_pairs={{1,0},{2,1},{3,2},{0,3},{5,4},{6,5},{7,6},{4,7},{9,8},{10,9},{11,1... | collective-permute-start | bytes 3848 | tf_op jit(solution)/shard_map/ppermute | solution.py:471
  13.4 3.1 %advance_and_sums.1 = (f32[320,640]{1,0:T(8,128)S(1)}, f32[2,64,640]{2,1,0:T(8,128)S(1)}, bf16[2,64,640]{2,1,0:T(8,128)(2,1)S(1)}) custom-call(s32[2]{0:T(128)S(1)} %add_convert_fusion.3.flags_ref, f32[4,80,640]{2,1,0:T(8,128)S(1)} %get-tuple-element.25.fields_ref, f32[4,80,640]{2,1,0:T(8,128)S(1)} %get-tuple-element.26.winds_ref, f32[1,80]{1,0:T(1,128)S(1)} %bitcast.38, ...), custom_call_target="tpu_custom_call" | custom-call | bytes 9900000 | tf_op jit(solution)/shard_map/advance_and_sums/pallas_call | solution.py:500
  16.5 1.8 %sums.2 = (f32[2,64,640]{2,1,0:T(8,128)S(1)}, bf16[2,64,640]{2,1,0:T(8,128)(2,1)S(1)}) custom-call(f32[320,640]{1,0:T(8,128)S(1)} %get-tuple-element.31.stepped_ref, f32[640,256]{1,0:T(8,128)S(1)} %pad_maximum_fusion.refs_4_.near_ref, f32[640,10]{1,0:T(8,128)S(1)} %broadcast_multiply_fusion.refs_5_.far_ref, f32[2,64,640]{2,1,0:T(8,128)S(1)} %get-tuple-element.32.after_ref), custom_call_target="tpu_custom_call" | custom-call | bytes 7392000 | tf_op jit(solution)/shard_map/sums/pallas_call | solution.py:518
  21.1 1.5 %collective-permute-start.6 = (bf16[2,64,640]{2,1,0:T(8,128)(2,1)S(1)}, bf16[2,64,640]{2,1,0:T(8,128)(2,1)S(1)}, u32[]{:S(2)}, u32[]{:S(2)}) collective-permute-start(bf16[2,64,640]{2,1,0:T(8,128)(2,1)S(1)} %get-tuple-element.36), channel_id=1, source_target_pairs={{0,1},{1,0},{2,3},{3,2},{4,5},{5,4},{6,7},{7,6},{8,9},{9,8},{10,11... | collective-permute-start | bytes 491528 | tf_op jit(solution)/shard_map/ppermute | solution.py:529
  23.2 1.8 %collective-permute-done.4 = bf16[2,32,640]{2,1,0:T(8,128)(2,1)S(1)} collective-permute-done((bf16[2,32,640]{2,1,0:T(8,128)(2,1)S(1)}, bf16[2,32,640]{2,1,0:T(8,128)(2,1)S(1)}, u32[]{:S(2)}, u32[]{:S(2)}) %collective-permute-start.4) | collective-permute-done | bytes 81952 | tf_op jit(solution)/shard_map/ppermute | solution.py:529
  25.0 1.7 %collective-permute-start.5 = (bf16[32,640]{1,0:T(8,128)(2,1)S(1)}, bf16[32,640]{1,0:T(8,128)(2,1)S(1)}, u32[]{:S(2)}, u32[]{:S(2)}) collective-permute-start(bf16[32,640]{1,0:T(8,128)(2,1)S(1)} %get-tuple-element.56), channel_id=1, source_target_pairs={{0,2},{1,3},{2,0},{3,1},{4,6},{5,7},{6,4},{7,5},{8,10},{9,11},{10,... | collective-permute-start | bytes 122888 | tf_op jit(solution)/shard_map/ppermute | solution.py:529
  26.7 2.6 %collective-permute-done.6 = bf16[2,64,640]{2,1,0:T(8,128)(2,1)S(1)} collective-permute-done((bf16[2,64,640]{2,1,0:T(8,128)(2,1)S(1)}, bf16[2,64,640]{2,1,0:T(8,128)(2,1)S(1)}, u32[]{:S(2)}, u32[]{:S(2)}) %collective-permute-start.6) | collective-permute-done | bytes 163872 | tf_op jit(solution)/shard_map/ppermute | solution.py:529
  29.4 1.8 %collective-permute-start.7 = (bf16[64,640]{1,0:T(8,128)(2,1)S(1)}, bf16[64,640]{1,0:T(8,128)(2,1)S(1)}, u32[]{:S(2)}, u32[]{:S(2)}) collective-permute-start(bf16[64,640]{1,0:T(8,128)(2,1)S(1)} %get-tuple-element.54), channel_id=1, source_target_pairs={{0,2},{1,3},{2,0},{3,1},{4,6},{5,7},{6,4},{7,5},{8,10},{9,11},{10,... | collective-permute-start | bytes 245768 | tf_op jit(solution)/shard_map/ppermute | solution.py:529
  31.6 2.7 %collective-permute-start.9 = (bf16[64,640]{1,0:T(8,128)(2,1)S(1)}, bf16[64,640]{1,0:T(8,128)(2,1)S(1)}, u32[]{:S(2)}, u32[]{:S(2)}) collective-permute-start(bf16[64,640]{1,0:T(8,128)(2,1)S(1)} %get-tuple-element.52), channel_id=1, source_target_pairs={{0,2},{1,3},{2,0},{3,1},{4,6},{5,7},{6,4},{7,5},{8,10},{9,11},{10,... | collective-permute-start | bytes 245768 | tf_op jit(solution)/shard_map/ppermute | solution.py:529
  34.3 2.0 %collective-permute-done.7.refs_4_ = bf16[64,640]{1,0:T(8,128)(2,1)S(1)} collective-permute-done((bf16[64,640]{1,0:T(8,128)(2,1)S(1)}, bf16[64,640]{1,0:T(8,128)(2,1)S(1)}, u32[]{:S(2)}, u32[]{:S(2)}) %collective-permute-start.7) | collective-permute-done | bytes 81952 | tf_op jit(solution)/shard_map/ppermute | solution.py:529
  36.4 4.8 %forward.3.refs_7_ = f32[640,256]{1,0:T(8,128)S(1)} custom-call(s32[64]{0:T(128)S(1)} %get-tuple-element.67.refs_0_, s32[1]{0:T(128)} %bitcast.refs_1_.refs_0_, f32[64,640]{1,0:T(8,128)S(1)} %get-tuple-element.55.refs_2_, bf16[64,640]{1,0:T(8,128)(2,1)S(1)} %slice_bitcast_fusion.3.refs_3_, bf16[64,640]{1,0:T(8,128)(2,1)S(1)} %collective-permute-done.7.refs_4_, ...), custom_call_target="tpu_custom_call" | custom-call | bytes 12870000 | tf_op jit(solution)/shard_map/forward/pallas_call | solution.py:559
  41.2 4.8 %forward.4.refs_8_ = f32[640,256]{1,0:T(8,128)S(1)} custom-call(s32[64]{0:T(128)S(1)} %get-tuple-element.66.refs_0_, s32[1]{0:T(128)} %bitcast.refs_1_.refs_0_, f32[64,640]{1,0:T(8,128)S(1)} %get-tuple-element.53.refs_2_, bf16[64,640]{1,0:T(8,128)(2,1)S(1)} %slice_bitcast_fusion.2.refs_3_, bf16[64,640]{1,0:T(8,128)(2,1)S(1)} %collective-permute-done.9.refs_4_, ...), custom_call_target="tpu_custom_call" | custom-call | bytes 12870000 | tf_op jit(solution)/shard_map/forward/pallas_call | solution.py:559
  46.0 3.2 %forward.5 = (f32[4,80,640]{2,1,0:T(8,128)S(1)}, f32[4,80,640]{2,1,0:T(8,128)S(1)}) custom-call(s32[32]{0:T(128)S(1)} %slice.73.refs_0_, s32[1]{0:T(128)} %bitcast.refs_1_.refs_0_, f32[32,640]{1,0:T(8,128)S(1)} %get-tuple-element.57.refs_2_, bf16[32,640]{1,0:T(8,128)(2,1)S(1)} %slice_bitcast_fusion.5.refs_3_, ...), custom_call_target="tpu_custom_call" | custom-call | bytes 7589999 | tf_op jit(solution)/shard_map/forward/pallas_call | solution.py:559
  49.3 2.3 %collective-permute-done.10 = f32[4,80,640]{2,1,0:T(8,128)S(1)} collective-permute-done((f32[4,80,640]{2,1,0:T(8,128)S(1)}, f32[4,80,640]{2,1,0:T(8,128)S(1)}, u32[]{:S(2)}, u32[]{:S(2)}) %collective-permute-start.10) | collective-permute-done | bytes 819232 | tf_op jit(solution)/shard_map/ppermute | solution.py:529
  53.1 2.6 %collective-permute-start.12 = (f32[80,640]{1,0:T(8,128)S(1)}, f32[80,640]{1,0:T(8,128)S(1)}, u32[]{:S(2)}, u32[]{:S(2)}) collective-permute-start(f32[80,640]{1,0:T(8,128)S(1)} %get-tuple-element.49), channel_id=1, source_target_pairs={{0,16},{4,20},{8,24},{12,28},{16,0},{20,4},{24,8},{28,12},{1,17},{... | collective-permute-start | bytes 614408 | tf_op jit(solution)/shard_map/ppermute | solution.py:529
  55.7 5.0 %collective-permute-done.13.refs_6_ = f32[80,640]{1,0:T(8,128)S(1)} collective-permute-done((f32[80,640]{1,0:T(8,128)S(1)}, f32[80,640]{1,0:T(8,128)S(1)}, u32[]{:S(2)}, u32[]{:S(2)}) %collective-permute-start.13) | collective-permute-done | bytes 204832 | tf_op jit(solution)/shard_map/ppermute | solution.py:529
  60.7 3.5 %collective-permute-done.12.refs_5_ = f32[80,640]{1,0:T(8,128)S(1)} collective-permute-done((f32[80,640]{1,0:T(8,128)S(1)}, f32[80,640]{1,0:T(8,128)S(1)}, u32[]{:S(2)}, u32[]{:S(2)}) %collective-permute-start.12) | collective-permute-done | bytes 204832 | tf_op jit(solution)/shard_map/ppermute | solution.py:529
  65.1 10.9 %all_gather.3.refs_1_ = bf16[640,640]{1,0:T(8,128)(2,1)S(1)} all-gather(bf16[80,640]{1,0:T(8,128)(2,1)S(1)} %get-tuple-element.40), channel_id=1, replica_groups=mesh['lat'=8,'lon'=4] {'lat'}, dimensions={0}, use_global_device_ids=true | all-gather | bytes 921600 | tf_op jit(solution)/shard_map/all_gather | solution.py:605
  76.1 3.5 %inverse.3 = (f32[32,640]{1,0:T(8,128)S(1)}, bf16[32,640]{1,0:T(8,128)(2,1)S(1)}) custom-call(s32[32]{0:T(128)S(1)} %slice.73.refs_0_, bf16[640,640]{1,0:T(8,128)(2,1)S(1)} %all_gather.3.refs_1_, bf16[160,80,640]{2,1,0:T(8,128)(2,1)} %refs_2_.7), custom_call_target="tpu_custom_call" | custom-call | bytes 7325999 | tf_op jit(solution)/shard_map/inverse/pallas_call | solution.py:609
  79.6 5.0 %inverse.4 = (f32[64,640]{1,0:T(8,128)S(1)}, bf16[64,640]{1,0:T(8,128)(2,1)S(1)}) custom-call(s32[64]{0:T(128)S(1)} %get-tuple-element.66.refs_0_, bf16[640,640]{1,0:T(8,128)(2,1)S(1)} %all_gather.3.refs_1_, bf16[160,80,640]{2,1,0:T(8,128)(2,1)} %refs_2_.7, bf16[32,640]{1,0:T(8,128)(2,1)S(1)} %get-tuple-element.41.refs_3_), custom_call_target="tpu_custom_call" | custom-call | bytes 13661999 | tf_op jit(solution)/shard_map/inverse/pallas_call | solution.py:609
  84.7 5.0 %inverse.5 = (f32[64,640]{1,0:T(8,128)S(1)}, bf16[64,640]{1,0:T(8,128)(2,1)S(1)}) custom-call(s32[64]{0:T(128)S(1)} %get-tuple-element.67.refs_0_, bf16[640,640]{1,0:T(8,128)(2,1)S(1)} %all_gather.3.refs_1_, bf16[160,80,640]{2,1,0:T(8,128)(2,1)} %refs_2_.7, bf16[64,640]{1,0:T(8,128)(2,1)S(1)} %get-tuple-element.42.refs_3_), custom_call_target="tpu_custom_call" | custom-call | bytes 13661999 | tf_op jit(solution)/shard_map/inverse/pallas_call | solution.py:609
  89.7 3.0 %collective-permute-start.15 = (bf16[64,640]{1,0:T(8,128)(2,1)S(1)}, bf16[64,640]{1,0:T(8,128)(2,1)S(1)}, u32[]{:S(2)}, u32[]{:S(2)}) collective-permute-start(bf16[64,640]{1,0:T(8,128)(2,1)S(1)} %get-tuple-element.44), channel_id=1, source_target_pairs={{0,2},{1,3},{2,0},{3,1},{4,6},{5,7},{6,4},{7,5},{8,10},{9,11},{10,... | collective-permute-start | bytes 245768 | tf_op jit(solution)/shard_map/ppermute | solution.py:529
  92.7 2.0 %collective-permute-start.20 = (bf16[32,640]{1,0:T(8,128)(2,1)S(1)}, bf16[32,640]{1,0:T(8,128)(2,1)S(1)}, u32[]{:S(2)}, u32[]{:S(2)}) collective-permute-start(bf16[32,640]{1,0:T(8,128)(2,1)S(1)} %get-tuple-element.41.refs_3_), channel_id=1, source_target_pairs={{0,1},{1,0},{2,3},{3,2},{4,5},{5,4},{6,7},{7,6},{8,9},{9,8},{10,11... | collective-permute-start | bytes 122888 | tf_op jit(solution)/shard_map/ppermute | solution.py:529
  94.8 2.0 %collective-permute-start.19 = (bf16[64,640]{1,0:T(8,128)(2,1)S(1)}, bf16[64,640]{1,0:T(8,128)(2,1)S(1)}, u32[]{:S(2)}, u32[]{:S(2)}) collective-permute-start(bf16[64,640]{1,0:T(8,128)(2,1)S(1)} %collective-permute-done.18.refs_2_), channel_id=1, source_target_pairs={{0,1},{1,0},{2,3},{3,2},{4,5},{5,4},{6,7},{7,6},{8,9},{9,8},{10,11... | collective-permute-start | bytes 245768 | tf_op jit(solution)/shard_map/ppermute | solution.py:529
  96.8 2.2 %collective-permute-done.21.refs_2_ = bf16[32,640]{1,0:T(8,128)(2,1)S(1)} collective-permute-done((bf16[32,640]{1,0:T(8,128)(2,1)S(1)}, bf16[32,640]{1,0:T(8,128)(2,1)S(1)}, u32[]{:S(2)}, u32[]{:S(2)}) %collective-permute-start.21) | collective-permute-done | bytes 40992 | tf_op jit(solution)/shard_map/ppermute | solution.py:529
  99.0 2.0 %collective-permute-start.16 = (bf16[64,640]{1,0:T(8,128)(2,1)S(1)}, bf16[64,640]{1,0:T(8,128)(2,1)S(1)}, u32[]{:S(2)}, u32[]{:S(2)}) collective-permute-start(bf16[64,640]{1,0:T(8,128)(2,1)S(1)} %collective-permute-done.15.refs_2_), channel_id=1, source_target_pairs={{0,1},{1,0},{2,3},{3,2},{4,5},{5,4},{6,7},{7,6},{8,9},{9,8},{10,11... | collective-permute-start | bytes 245768 | tf_op jit(solution)/shard_map/ppermute | solution.py:529
  102.0 3.9 %collective-permute-done.22.refs_3_ = bf16[32,640]{1,0:T(8,128)(2,1)S(1)} collective-permute-done((bf16[32,640]{1,0:T(8,128)(2,1)S(1)}, bf16[32,640]{1,0:T(8,128)(2,1)S(1)}, u32[]{:S(2)}, u32[]{:S(2)}) %collective-permute-start.22) | collective-permute-done | bytes 40992 | tf_op jit(solution)/shard_map/ppermute | solution.py:529
  107.1 1.5 %values.4.refs_4_ = f32[320,640]{1,0:T(8,128)S(1)} custom-call(f32[640,256]{1,0:T(8,128)S(1)} %pad_maximum_fusion.refs_4_.near_ref, f32[640,10]{1,0:T(8,128)S(1)} %broadcast_multiply_fusion.refs_5_.far_ref, f32[64,640]{1,0:T(8,128)S(1)} %get-tuple-element.45.refs_0_, bf16[64,640]{1,0:T(8,128)(2,1)S(1)} %collective-permute-done.17.refs_1_, ...), custom_call_target="tpu_custom_call" | custom-call | bytes 5280000 | tf_op jit(solution)/shard_map/values/pallas_call | solution.py:636
  108.6 2.4 %values.5 = f32[320,640]{1,0:T(8,128)} custom-call(f32[640,256]{1,0:T(8,128)S(1)} %pad_maximum_fusion.refs_4_.near_ref, f32[640,10]{1,0:T(8,128)S(1)} %broadcast_multiply_fusion.refs_5_.far_ref, f32[64,640]{1,0:T(8,128)S(1)} %get-tuple-element.43.refs_0_, bf16[64,640]{1,0:T(8,128)(2,1)S(1)} %collective-permute-done.14.refs_1_, ...), custom_call_target="tpu_custom_call" | custom-call | bytes 5280000 | tf_op jit(solution)/shard_map/values/pallas_call | solution.py:636
  (57 shorter events, 12.7 us)
Async XLA Ops:
  2.0 10.7 %collective-permute-start = (f32[4,640]{1,0:T(4,128)S(1)}, f32[4,640]{1,0:T(4,128)S(1)}, u32[]{:S(2)}, u32[]{:S(2)}) collective-permute-start(f32[4,640]{1,0:T(4,128)S(1)} %get-tuple-element.27), channel_id=1, source_target_pairs={{0,4},{4,8},{8,12},{12,16},{16,20},{20,24},{24,28},{28,0},{1,5},{5... | collective-permute-start | bytes 30728 | tf_op jit(solution)/shard_map/ppermute | solution.py:468
  2.6 10.2 %collective-permute-start.1 = (f32[4,640]{1,0:T(4,128)S(1)}, f32[4,640]{1,0:T(4,128)S(1)}, u32[]{:S(2)}, u32[]{:S(2)}) collective-permute-start(f32[4,640]{1,0:T(4,128)S(1)} %get-tuple-element.28), channel_id=1, source_target_pairs={{4,0},{8,4},{12,8},{16,12},{20,16},{24,20},{28,24},{0,28},{5,1},{9... | collective-permute-start | bytes 30728 | tf_op jit(solution)/shard_map/ppermute | solution.py:469
  5.5 7.2 %collective-permute-start.2 = (f32[80,4]{1,0:T(8,128)S(1)}, f32[80,4]{1,0:T(8,128)S(1)}, u32[]{:S(2)}, u32[]{:S(2)}) collective-permute-start(f32[80,4]{1,0:T(8,128)S(1)} %get-tuple-element.29), channel_id=1, source_target_pairs={{0,1},{1,2},{2,3},{3,0},{4,5},{5,6},{6,7},{7,4},{8,9},{9,10},{10,1... | collective-permute-start | bytes 3848 | tf_op jit(solution)/shard_map/ppermute | solution.py:470
  7.8 5.0 %collective-permute-start.3 = (f32[80,4]{1,0:T(8,128)S(1)}, f32[80,4]{1,0:T(8,128)S(1)}, u32[]{:S(2)}, u32[]{:S(2)}) collective-permute-start(f32[80,4]{1,0:T(8,128)S(1)} %get-tuple-element.30), channel_id=1, source_target_pairs={{1,0},{2,1},{3,2},{0,3},{5,4},{6,5},{7,6},{4,7},{9,8},{10,9},{11,1... | collective-permute-start | bytes 3848 | tf_op jit(solution)/shard_map/ppermute | solution.py:471
  12.8 0.7 copy-start.1
  19.6 5.4 %collective-permute-start.4 = (bf16[2,32,640]{2,1,0:T(8,128)(2,1)S(1)}, bf16[2,32,640]{2,1,0:T(8,128)(2,1)S(1)}, u32[]{:S(2)}, u32[]{:S(2)}) collective-permute-start(bf16[2,32,640]{2,1,0:T(8,128)(2,1)S(1)} %get-tuple-element.35), channel_id=1, source_target_pairs={{0,1},{1,0},{2,3},{3,2},{4,5},{5,4},{6,7},{7,6},{8,9},{9,8},{10,11... | collective-permute-start | bytes 245768 | tf_op jit(solution)/shard_map/ppermute | solution.py:529
  21.1 8.2 %collective-permute-start.6 = (bf16[2,64,640]{2,1,0:T(8,128)(2,1)S(1)}, bf16[2,64,640]{2,1,0:T(8,128)(2,1)S(1)}, u32[]{:S(2)}, u32[]{:S(2)}) collective-permute-start(bf16[2,64,640]{2,1,0:T(8,128)(2,1)S(1)} %get-tuple-element.36), channel_id=1, source_target_pairs={{0,1},{1,0},{2,3},{3,2},{4,5},{5,4},{6,7},{7,6},{8,9},{9,8},{10,11... | collective-permute-start | bytes 491528 | tf_op jit(solution)/shard_map/ppermute | solution.py:529
  22.6 8.9 %collective-permute-start.8 = (bf16[2,64,640]{2,1,0:T(8,128)(2,1)S(1)}, bf16[2,64,640]{2,1,0:T(8,128)(2,1)S(1)}, u32[]{:S(2)}, u32[]{:S(2)}) collective-permute-start(bf16[2,64,640]{2,1,0:T(8,128)(2,1)S(1)} %get-tuple-element.37), channel_id=1, source_target_pairs={{0,1},{1,0},{2,3},{3,2},{4,5},{5,4},{6,7},{7,6},{8,9},{9,8},{10,11... | collective-permute-start | bytes 491528 | tf_op jit(solution)/shard_map/ppermute | solution.py:529
  25.0 21.0 %collective-permute-start.5 = (bf16[32,640]{1,0:T(8,128)(2,1)S(1)}, bf16[32,640]{1,0:T(8,128)(2,1)S(1)}, u32[]{:S(2)}, u32[]{:S(2)}) collective-permute-start(bf16[32,640]{1,0:T(8,128)(2,1)S(1)} %get-tuple-element.56), channel_id=1, source_target_pairs={{0,2},{1,3},{2,0},{3,1},{4,6},{5,7},{6,4},{7,5},{8,10},{9,11},{10,... | collective-permute-start | bytes 122888 | tf_op jit(solution)/shard_map/ppermute | solution.py:529
  29.4 7.0 %collective-permute-start.7 = (bf16[64,640]{1,0:T(8,128)(2,1)S(1)}, bf16[64,640]{1,0:T(8,128)(2,1)S(1)}, u32[]{:S(2)}, u32[]{:S(2)}) collective-permute-start(bf16[64,640]{1,0:T(8,128)(2,1)S(1)} %get-tuple-element.54), channel_id=1, source_target_pairs={{0,2},{1,3},{2,0},{3,1},{4,6},{5,7},{6,4},{7,5},{8,10},{9,11},{10,... | collective-permute-start | bytes 245768 | tf_op jit(solution)/shard_map/ppermute | solution.py:529
  31.6 9.6 %collective-permute-start.9 = (bf16[64,640]{1,0:T(8,128)(2,1)S(1)}, bf16[64,640]{1,0:T(8,128)(2,1)S(1)}, u32[]{:S(2)}, u32[]{:S(2)}) collective-permute-start(bf16[64,640]{1,0:T(8,128)(2,1)S(1)} %get-tuple-element.52), channel_id=1, source_target_pairs={{0,2},{1,3},{2,0},{3,1},{4,6},{5,7},{6,4},{7,5},{8,10},{9,11},{10,... | collective-permute-start | bytes 245768 | tf_op jit(solution)/shard_map/ppermute | solution.py:529
  41.2 23.2 %copy-start = (f32[2,2]{1,0:T(2,128)S(1)}, f32[2,2]{1,0:T(2,128)}, u32[]{:S(2)}) copy-start(f32[2,2]{1,0:T(2,128)} %refs_2_.4) | copy-start | bytes 52
  41.2 23.1 %copy-start.2 = (f32[2]{0:T(128)S(1)}, f32[2]{0:T(128)}, u32[]{:S(2)}) copy-start(f32[2]{0:T(128)} %refs_1_.1) | copy-start | bytes 28
  49.2 2.4 %collective-permute-start.10 = (f32[4,80,640]{2,1,0:T(8,128)S(1)}, f32[4,80,640]{2,1,0:T(8,128)S(1)}, u32[]{:S(2)}, u32[]{:S(2)}) collective-permute-start(f32[4,80,640]{2,1,0:T(8,128)S(1)} %get-tuple-element.39), channel_id=1, source_target_pairs={{0,4},{4,0},{8,12},{12,8},{16,20},{20,16},{24,28},{28,24},{1,5},{5... | collective-permute-start | bytes 2457608 | tf_op jit(solution)/shard_map/ppermute | solution.py:529
  51.8 9.0 %collective-permute-start.13 = (f32[80,640]{1,0:T(8,128)S(1)}, f32[80,640]{1,0:T(8,128)S(1)}, u32[]{:S(2)}, u32[]{:S(2)}) collective-permute-start(f32[80,640]{1,0:T(8,128)S(1)} %get-tuple-element.48), channel_id=1, source_target_pairs={{0,24},{4,28},{8,16},{12,20},{16,8},{20,12},{24,0},{28,4},{1,25},{... | collective-permute-start | bytes 614408 | tf_op jit(solution)/shard_map/ppermute | solution.py:529
  53.1 11.1 %collective-permute-start.12 = (f32[80,640]{1,0:T(8,128)S(1)}, f32[80,640]{1,0:T(8,128)S(1)}, u32[]{:S(2)}, u32[]{:S(2)}) collective-permute-start(f32[80,640]{1,0:T(8,128)S(1)} %get-tuple-element.49), channel_id=1, source_target_pairs={{0,16},{4,20},{8,24},{12,28},{16,0},{20,4},{24,8},{28,12},{1,17},{... | collective-permute-start | bytes 614408 | tf_op jit(solution)/shard_map/ppermute | solution.py:529
  55.7 8.6 %collective-permute-start.11 = (f32[80,640]{1,0:T(8,128)S(1)}, f32[80,640]{1,0:T(8,128)S(1)}, u32[]{:S(2)}, u32[]{:S(2)}) collective-permute-start(f32[80,640]{1,0:T(8,128)S(1)} %get-tuple-element.50), channel_id=1, source_target_pairs={{0,8},{4,12},{8,0},{12,4},{16,24},{20,28},{24,16},{28,20},{1,9},{5... | collective-permute-start | bytes 614408 | tf_op jit(solution)/shard_map/ppermute | solution.py:529
  84.6 10.2 %collective-permute-start.18 = (bf16[64,640]{1,0:T(8,128)(2,1)S(1)}, bf16[64,640]{1,0:T(8,128)(2,1)S(1)}, u32[]{:S(2)}, u32[]{:S(2)}) collective-permute-start(bf16[64,640]{1,0:T(8,128)(2,1)S(1)} %get-tuple-element.42.refs_3_), channel_id=1, source_target_pairs={{0,2},{1,3},{2,0},{3,1},{4,6},{5,7},{6,4},{7,5},{8,10},{9,11},{10,... | collective-permute-start | bytes 245768 | tf_op jit(solution)/shard_map/ppermute | solution.py:529
  89.7 9.3 %collective-permute-start.15 = (bf16[64,640]{1,0:T(8,128)(2,1)S(1)}, bf16[64,640]{1,0:T(8,128)(2,1)S(1)}, u32[]{:S(2)}, u32[]{:S(2)}) collective-permute-start(bf16[64,640]{1,0:T(8,128)(2,1)S(1)} %get-tuple-element.44), channel_id=1, source_target_pairs={{0,2},{1,3},{2,0},{3,1},{4,6},{5,7},{6,4},{7,5},{8,10},{9,11},{10,... | collective-permute-start | bytes 245768 | tf_op jit(solution)/shard_map/ppermute | solution.py:529
  92.7 6.3 %collective-permute-start.21 = (bf16[32,640]{1,0:T(8,128)(2,1)S(1)}, bf16[32,640]{1,0:T(8,128)(2,1)S(1)}, u32[]{:S(2)}, u32[]{:S(2)}) collective-permute-start(bf16[32,640]{1,0:T(8,128)(2,1)S(1)} %get-tuple-element.41.refs_3_), channel_id=1, source_target_pairs={{0,2},{1,3},{2,0},{3,1},{4,6},{5,7},{6,4},{7,5},{8,10},{9,11},{10,... | collective-permute-start | bytes 122888 | tf_op jit(solution)/shard_map/ppermute | solution.py:529
  92.7 8.3 %collective-permute-start.20 = (bf16[32,640]{1,0:T(8,128)(2,1)S(1)}, bf16[32,640]{1,0:T(8,128)(2,1)S(1)}, u32[]{:S(2)}, u32[]{:S(2)}) collective-permute-start(bf16[32,640]{1,0:T(8,128)(2,1)S(1)} %get-tuple-element.41.refs_3_), channel_id=1, source_target_pairs={{0,1},{1,0},{2,3},{3,2},{4,5},{5,4},{6,7},{7,6},{8,9},{9,8},{10,11... | collective-permute-start | bytes 122888 | tf_op jit(solution)/shard_map/ppermute | solution.py:529
  94.7 12.3 %collective-permute-start.17 = (bf16[64,640]{1,0:T(8,128)(2,1)S(1)}, bf16[64,640]{1,0:T(8,128)(2,1)S(1)}, u32[]{:S(2)}, u32[]{:S(2)}) collective-permute-start(bf16[64,640]{1,0:T(8,128)(2,1)S(1)} %get-tuple-element.42.refs_3_), channel_id=1, source_target_pairs={{0,1},{1,0},{2,3},{3,2},{4,5},{5,4},{6,7},{7,6},{8,9},{9,8},{10,11... | collective-permute-start | bytes 245768 | tf_op jit(solution)/shard_map/ppermute | solution.py:529
  94.8 12.3 %collective-permute-start.19 = (bf16[64,640]{1,0:T(8,128)(2,1)S(1)}, bf16[64,640]{1,0:T(8,128)(2,1)S(1)}, u32[]{:S(2)}, u32[]{:S(2)}) collective-permute-start(bf16[64,640]{1,0:T(8,128)(2,1)S(1)} %collective-permute-done.18.refs_2_), channel_id=1, source_target_pairs={{0,1},{1,0},{2,3},{3,2},{4,5},{5,4},{6,7},{7,6},{8,9},{9,8},{10,11... | collective-permute-start | bytes 245768 | tf_op jit(solution)/shard_map/ppermute | solution.py:529
  99.0 9.6 %collective-permute-start.14 = (bf16[64,640]{1,0:T(8,128)(2,1)S(1)}, bf16[64,640]{1,0:T(8,128)(2,1)S(1)}, u32[]{:S(2)}, u32[]{:S(2)}) collective-permute-start(bf16[64,640]{1,0:T(8,128)(2,1)S(1)} %get-tuple-element.44), channel_id=1, source_target_pairs={{0,1},{1,0},{2,3},{3,2},{4,5},{5,4},{6,7},{7,6},{8,9},{9,8},{10,11... | collective-permute-start | bytes 245768 | tf_op jit(solution)/shard_map/ppermute | solution.py:529
  99.0 9.6 %collective-permute-start.16 = (bf16[64,640]{1,0:T(8,128)(2,1)S(1)}, bf16[64,640]{1,0:T(8,128)(2,1)S(1)}, u32[]{:S(2)}, u32[]{:S(2)}) collective-permute-start(bf16[64,640]{1,0:T(8,128)(2,1)S(1)} %collective-permute-done.15.refs_2_), channel_id=1, source_target_pairs={{0,1},{1,0},{2,3},{3,2},{4,5},{5,4},{6,7},{7,6},{8,9},{9,8},{10,11... | collective-permute-start | bytes 245768 | tf_op jit(solution)/shard_map/ppermute | solution.py:529
  101.0 5.0 %collective-permute-start.22 = (bf16[32,640]{1,0:T(8,128)(2,1)S(1)}, bf16[32,640]{1,0:T(8,128)(2,1)S(1)}, u32[]{:S(2)}, u32[]{:S(2)}) collective-permute-start(bf16[32,640]{1,0:T(8,128)(2,1)S(1)} %collective-permute-done.21.refs_2_), channel_id=1, source_target_pairs={{0,1},{1,0},{2,3},{3,2},{4,5},{5,4},{6,7},{7,6},{8,9},{9,8},{10,11... | collective-permute-start | bytes 122888 | tf_op jit(solution)/shard_map/ppermute | solution.py:529

commit v3 on v2

--- a/solution.py
+++ b/solution.py
@@ -177,13 +177,21 @@
     winds_copy.wait()
 
 
-def table_copy(table_hbm, table_ref, first, step, semaphores):
-    at = pl.multiple_of(step * GROUP, GROUP)
-    return pltpu.make_async_copy(
-        table_hbm.at[pl.ds(first + at, GROUP)],
-        table_ref.at[pl.ds(at, GROUP)],
-        semaphores.at[step],
-    )
+def load_table_kernel(after_ref, table_hbm, table_ref, semaphores):
+    parts = semaphores.shape[0]
+    share = table_ref.shape[0] // parts
+    copies = [
+        pltpu.make_async_copy(
+            table_hbm.at[pl.ds(i * share, share)],
+            table_ref.at[pl.ds(i * share, share)],
+            semaphores.at[i],
+        )
+        for i in range(parts)
+    ]
+    for copy in copies:
+        copy.start()
+    for copy in copies:
+        copy.wait()
 
 
 def advance(flags, fields_ref, wind_ref, step_ref, above, below, before, after, stepped_ref):
@@ -249,8 +257,8 @@
     blocks, sections, rows, degree_dev, first, last, waves_ref, place_ref, *refs
 ):
     received = refs[:blocks]
-    weight_ref, table_hbm = refs[blocks : blocks + 2]
-    *rest, table_ref, semaphores = refs[blocks + 2 :]
+    weight_ref, table_ref = refs[blocks : blocks + 2]
+    rest = refs[blocks + 2 :]
     spread_ref, kept_ref, turned_ref = rest[-3:]
     step = pl.program_id(0)
     half = sections // 2
@@ -261,8 +269,6 @@
 
     @pl.when(step == 0)
     def _():
-        for i in range(share // group):
-            table_copy(table_hbm, table_ref, first, i, semaphores).start()
         total = received[0][...].astype(F32)
         for other in received[1:]:
             total = total + other[...].astype(F32)
@@ -273,7 +279,6 @@
                     at = ((c * levels + level) * 2 + h) * rows
                     spread_ref[:, h * half + level * 2 + c, 0:rows] = total[:, at : at + rows]
 
-    table_copy(table_hbm, table_ref, first, step, semaphores).wait()
     degree = lax.broadcasted_iota(jnp.int32, (2 * half, columns), 1)
     row = lax.broadcasted_iota(jnp.int32, (2 * half, 1), 0)
     for u in range(0, group, 2):
@@ -281,7 +286,7 @@
         for v in (u, u + 1):
             high, low = split_halves(spread_ref[step * group + v, :, 0:rows])
             both = jnp.concatenate([high.astype(F32), low.astype(F32)], axis=0).astype(BF16)
-            total = jnp.dot(both, table_ref[step * group + v], preferred_element_type=F32)
+            total = jnp.dot(both, table_ref[first + step * group + v], preferred_element_type=F32)
             sums.append(total[:sections] + total[sections:])
         north = jnp.concatenate([sums[0][:half], sums[1][:half]], axis=0)
         south = jnp.concatenate([sums[0][half:], sums[1][half:]], axis=0)
@@ -343,8 +348,8 @@
         at, slot = at + levels * wide, slot + share
 
 
-def inverse_kernel(sections, rows, first, waves_ref, joined_ref, table_hbm, *refs):
-    own_ref, out_ref, kept_ref, spread_ref, table_ref, semaphores = refs
+def inverse_kernel(sections, rows, first, waves_ref, joined_ref, table_ref, *refs):
+    own_ref, out_ref, kept_ref, spread_ref = refs
     step = pl.program_id(0)
     half = sections // 2
     levels = half // 2
@@ -354,8 +359,6 @@
 
     @pl.when(step == 0)
     def _():
-        for i in range(share // group):
-            table_copy(table_hbm, table_ref, first, i, semaphores).start()
         for t in range(columns // LANES):
             tile = joined_ref[t * LANES : (t + 1) * LANES, half * first : half * (first + share)]
             turned = tile.astype(F32).T
@@ -367,7 +370,6 @@
     degree = lax.broadcasted_iota(jnp.int32, (2 * half, columns), 1)
     row = lax.broadcasted_iota(jnp.int32, (2 * half, 1), 0)
     upper = row < half
-    table_copy(table_hbm, table_ref, first, step, semaphores).wait()
     for u in range(0, group, 2):
         slot = step * group + u
         at = pl.ds(pl.multiple_of(slot * half, 2 * half), 2 * half)
@@ -379,7 +381,7 @@
         odds = pltpu.roll(jnp.where(even, 0.0, values), half, 0)
         for v in range(2):
             both = jnp.where(upper, odds, evens) if v else jnp.where(upper, evens, odds)
-            sums = dot_rows(both.astype(BF16), table_ref[slot + v])
+            sums = dot_rows(both.astype(BF16), table_ref[first + slot + v])
             factor = jnp.where(waves_ref[slot + v] == 0, 1.0, 2.0) / math.sqrt(M)
             sums = sums * factor
             swapped = pltpu.roll(sums, half, 0)
@@ -490,8 +492,6 @@
     def sums_shape(share):
         return [like((lon_count // 2, share, width), dtype) for dtype in (F32, BF16)]
 
-    table = pltpu.with_memory_space_constraint(legendre, pltpu.HBM)
-
     def first_sums(flags_ref, fields_ref, winds_ref, step_ref, *refs):
         edges, near_ref, far_ref, stepped_ref = refs[:4], *refs[4:7]
         advance(flags_ref, fields_ref, winds_ref, step_ref, *edges, stepped_ref)
@@ -548,6 +548,16 @@
         pieces = later_sums(chunk, first, pieces[0])
         swapped.append(to_owners(*pieces))
         first += CUTS[chunk]
+    table = pl.pallas_call(
+        load_table_kernel,
+        out_shape=pltpu.VMEM(legendre.shape, BF16),
+        in_specs=[VMEM, HBM],
+        out_specs=VMEM,
+        scratch_shapes=[pltpu.SemaphoreType.DMA((4,))],
+        compiler_params=grant(8),
+        cost_estimate=cost(5.7),
+        name="load_table",
+    )(pieces[0], pltpu.with_memory_space_constraint(legendre, pltpu.HBM))
 
 
     def forward(first, share, parts, earlier, last):
@@ -565,15 +575,13 @@
                 num_scalar_prefetch=2,
                 grid=(share // GROUP,),
                 in_specs=[whole_block((share, width))] * len(parts)
-                + [whole_block((1, width)), HBM]
+                + [whole_block((1, width)), VMEM]
                 + [whole_block(other.shape) for other in earlier],
                 out_specs=[whole_block(shape.shape) for shape in shapes],
                 scratch_shapes=[
                     pltpu.VMEM((share, sections, LANES), F32),
                     pltpu.VMEM((columns // LANES, half * share, LANES), F32),
                     pltpu.VMEM((columns, half * share), F32),
-                    pltpu.VMEM((share, rows_half, columns), BF16),
-                    pltpu.SemaphoreType.DMA((share // GROUP,)),
                 ],
             ),
             compiler_params=grant(20),
@@ -590,7 +598,7 @@
 
     other = swap(other, "lat", 1)
     sums = [own[j] + other[j] for j in range(lat_count // 2)]
-    sums = [sums[0]] + [swap(sums[j], "lat", 2 * j) for j in range(1, lat_count // 2)]
+    sums = [sums[0]] + [swap(sums[j].astype(BF16), "lat", 2 * j) for j in range(1, lat_count // 2)]
     rounded, spectrum = pl.pallas_call(
         lambda *refs: correct_kernel(CUTS, levels, *refs),
         out_shape=[
@@ -612,13 +620,11 @@
             grid_spec=pltpu.PrefetchScalarGridSpec(
                 num_scalar_prefetch=1,
                 grid=(share // GROUP,),
-                in_specs=[whole_block(joined.shape), HBM] + [VMEM] * len(after),
+                in_specs=[whole_block(joined.shape), VMEM] + [VMEM] * len(after),
                 out_specs=[whole_block((share, width))] * 2,
                 scratch_shapes=[
                     pltpu.VMEM((columns // LANES, half * share, LANES), F32),
                     pltpu.VMEM((share, sections, LANES), F32),
-                    pltpu.VMEM((share, rows_half, columns), BF16),
-                    pltpu.SemaphoreType.DMA((share // GROUP,)),
                 ],
             ),
             compiler_params=grant(20),

time: 111 us -> 101 us (0.910)
  waiting for transfers between devices: 23.9 us -> 17.5 us
  Pallas kernels: 39.6 us -> 36.9 us
    ppermute x19, waiting for transfers between devices: 23.9 us -> 17.5 us  [swap(): return lax.ppermute(value, axis, pairs(lax.axis_size(axis), step))]
    pallas_call x0 -> x1, Pallas kernels: none -> 5.77 us  [tiled(): pl.pallas_call(load_table_kernel, out_shape=pltpu.VMEM(legendre.shape, BF...]
    pallas_call x3, Pallas kernels: 12.8 us -> 8.3 us  [forward(): pl.pallas_call(lambda *refs: forward_kernel(len(parts), sections, rows_ha...]
    pallas_call x3, Pallas kernels: 13.5 us -> 9.59 us  [inverse(): pl.pallas_call(lambda *refs: inverse_kernel(sections, rows_half, first, *...]
  transfers between devices with their start and end apart: 23 -> 23, of which waited for: 10 -> 7; matrix products, arithmetic and copies ran while one was open for 4% -> 5% of each run, Pallas kernels for 15% -> 18%
where the time goes in v3:
time: 101 us; the launch traced here: 100 us
  Pallas kernels  36.9 us (37%)
  starting transfers between devices  29.4 us (29%)
  waiting for transfers between devices  17.5 us (17%)
  blocking collectives  10.2 us (10%)
  local copies, waits for them, and re-layouts  3.55 us (4%)
  other arithmetic  1.96 us (2%)
    ppermute x19, starting transfers between devices, swap(): return lax.ppermute(value, axis, pairs(lax.axis_size(axis), step))  21.6 us
    ppermute x19, waiting for transfers between devices, swap(): return lax.ppermute(value, axis, pairs(lax.axis_size(axis), step))  17.5 us
    all_gather x1, blocking collectives, tiled(): joined = lax.all_gather(rounded, 'lat', axis=0, tiled=True)  10.2 us
    pallas_call x3, Pallas kernels, inverse(): pl.pallas_call(lambda *refs: inverse_kernel(sections, rows_half, first, *...  9.59 us
    pallas_call x3, Pallas kernels, forward(): pl.pallas_call(lambda *refs: forward_kernel(len(parts), sections, rows_ha...  8.3 us
    pallas_call x1, Pallas kernels, tiled(): pl.pallas_call(load_table_kernel, out_shape=pltpu.VMEM(legendre.shape, BF...  5.77 us
    pallas_call x3, Pallas kernels, values(): pl.pallas_call(body, out_shape=like((grid_count, lon_dev), F32), in_specs...  4.9 us
    pallas_call x2, Pallas kernels, later_sums(): pl.pallas_call(body, out_shape=sums_shape(share), in_specs=[VMEM] * 4, ou...  3.11 us
  transfers between devices with their start and end apart: 23, of which 7 were waited for; matrix products, arithmetic and copies ran while one was open for 5% of the time, Pallas kernels for 18%

profile of v3, /device:TPU:0, one launch (start us, length us, event | category | flops | bytes accessed | tf_op | source)
XLA Modules:
  0.0 100.4 jit_solution(5281186464843842651)
XLA Ops:
  0.6 1.4 %load.1 = (f32[4,80,640]{2,1,0:T(8,128)S(1)}, f32[4,80,640]{2,1,0:T(8,128)S(1)}, f32[4,640]{1,0:T(4,128)S(1)}, f32[4,640]{1,0:T(4,128)S(1)}, f32[80,4]{1,0:T(8,128)S(1)}, /*index=5*/f32[80,4]{1,0:T(8,128)S(1)}) custom-call(f32[4,80,640]{2,1,0:T(8,128)} %bitcast.39, f32[4,80,640]{2,1,0:T(8,128)} %bitcast.40), custom_call_target="tpu_custom_call" | custom-call | bytes 4950000 | tf_op jit(solution)/shard_map/load/pallas_call | solution.py:454
  2.6 2.9 %collective-permute-start.1 = (f32[4,640]{1,0:T(4,128)S(1)}, f32[4,640]{1,0:T(4,128)S(1)}, u32[]{:S(2)}, u32[]{:S(2)}) collective-permute-start(f32[4,640]{1,0:T(4,128)S(1)} %get-tuple-element.28), channel_id=1, source_target_pairs={{4,0},{8,4},{12,8},{16,12},{20,16},{24,20},{28,24},{0,28},{5,1},{9... | collective-permute-start | bytes 30728 | tf_op jit(solution)/shard_map/ppermute | solution.py:471
  5.5 2.3 %collective-permute-start.2 = (f32[80,4]{1,0:T(8,128)S(1)}, f32[80,4]{1,0:T(8,128)S(1)}, u32[]{:S(2)}, u32[]{:S(2)}) collective-permute-start(f32[80,4]{1,0:T(8,128)S(1)} %get-tuple-element.29), channel_id=1, source_target_pairs={{0,1},{1,2},{2,3},{3,0},{4,5},{5,6},{6,7},{7,4},{8,9},{9,10},{10,1... | collective-permute-start | bytes 3848 | tf_op jit(solution)/shard_map/ppermute | solution.py:472
  7.8 2.0 %collective-permute-start.3 = (f32[80,4]{1,0:T(8,128)S(1)}, f32[80,4]{1,0:T(8,128)S(1)}, u32[]{:S(2)}, u32[]{:S(2)}) collective-permute-start(f32[80,4]{1,0:T(8,128)S(1)} %get-tuple-element.30), channel_id=1, source_target_pairs={{1,0},{2,1},{3,2},{0,3},{5,4},{6,5},{7,6},{4,7},{9,8},{10,9},{11,1... | collective-permute-start | bytes 3848 | tf_op jit(solution)/shard_map/ppermute | solution.py:473
  10.8 1.4 %fusion.5 = (f32[640,128]{1,0:T(8,128)S(1)}, f32[640,128]{1,0:T(8,128)S(1)}) fusion(s32[640]{0:T(1024)S(1)} %pad_add_fusion), kind=kLoop, calls=%fused_computation.9 | loop fusion | flops 737280 | bytes 657920 | tf_op jit(solution)/shard_map/cos | solution.py:482
  13.4 3.1 %advance_and_sums.1 = (f32[320,640]{1,0:T(8,128)S(1)}, f32[2,64,640]{2,1,0:T(8,128)S(1)}, bf16[2,64,640]{2,1,0:T(8,128)(2,1)S(1)}) custom-call(s32[2]{0:T(128)S(1)} %add_convert_fusion.3.flags_ref, f32[4,80,640]{2,1,0:T(8,128)S(1)} %get-tuple-element.25.fields_ref, f32[4,80,640]{2,1,0:T(8,128)S(1)} %get-tuple-element.26.winds_ref, f32[1,80]{1,0:T(1,128)S(1)} %bitcast.38, ...), custom_call_target="tpu_custom_call" | custom-call | bytes 9900000 | tf_op jit(solution)/shard_map/advance_and_sums/pallas_call | solution.py:500
  16.5 1.8 %sums.2 = (f32[2,64,640]{2,1,0:T(8,128)S(1)}, bf16[2,64,640]{2,1,0:T(8,128)(2,1)S(1)}) custom-call(f32[320,640]{1,0:T(8,128)S(1)} %get-tuple-element.31.stepped_ref, f32[640,256]{1,0:T(8,128)S(1)} %pad_maximum_fusion.refs_4_.near_ref, f32[640,10]{1,0:T(8,128)S(1)} %broadcast_multiply_fusion.refs_5_.far_ref, f32[2,64,640]{2,1,0:T(8,128)S(1)} %get-tuple-element.32.after_ref), custom_call_target="tpu_custom_call" | custom-call | bytes 7392000 | tf_op jit(solution)/shard_map/sums/pallas_call | solution.py:518
  18.4 1.3 %sums.3 = (f32[2,32,640]{2,1,0:T(8,128)S(1)}, bf16[2,32,640]{2,1,0:T(8,128)(2,1)S(1)}) custom-call(f32[320,640]{1,0:T(8,128)S(1)} %get-tuple-element.31.stepped_ref, f32[640,256]{1,0:T(8,128)S(1)} %pad_maximum_fusion.refs_4_.near_ref, f32[640,10]{1,0:T(8,128)S(1)} %broadcast_multiply_fusion.refs_5_.far_ref, f32[2,64,640]{2,1,0:T(8,128)S(1)} %get-tuple-element.33.after_ref), custom_call_target="tpu_custom_call" | custom-call | bytes 3696000 | tf_op jit(solution)/shard_map/sums/pallas_call | solution.py:518
  21.1 1.5 %collective-permute-start.6 = (bf16[2,64,640]{2,1,0:T(8,128)(2,1)S(1)}, bf16[2,64,640]{2,1,0:T(8,128)(2,1)S(1)}, u32[]{:S(2)}, u32[]{:S(2)}) collective-permute-start(bf16[2,64,640]{2,1,0:T(8,128)(2,1)S(1)} %get-tuple-element.36), channel_id=1, source_target_pairs={{0,1},{1,0},{2,3},{3,2},{4,5},{5,4},{6,7},{7,6},{8,9},{9,8},{10,11... | collective-permute-start | bytes 491528 | tf_op jit(solution)/shard_map/ppermute | solution.py:529
  23.2 5.8 %load_table.1.refs_6_.refs_2_ = bf16[160,80,640]{2,1,0:T(8,128)(2,1)S(1)} custom-call(f32[2,32,640]{2,1,0:T(8,128)S(1)} %get-tuple-element.34.after_ref, bf16[160,80,640]{2,1,0:T(8,128)(2,1)} %table_hbm.1), custom_call_target="tpu_custom_call" | custom-call | bytes 18810000 | tf_op jit(solution)/shard_map/load_table/pallas_call | solution.py:551
  29.0 2.9 %collective-permute-start.5 = (bf16[32,640]{1,0:T(8,128)(2,1)S(1)}, bf16[32,640]{1,0:T(8,128)(2,1)S(1)}, u32[]{:S(2)}, u32[]{:S(2)}) collective-permute-start(bf16[32,640]{1,0:T(8,128)(2,1)S(1)} %get-tuple-element.56), channel_id=1, source_target_pairs={{0,2},{1,3},{2,0},{3,1},{4,6},{5,7},{6,4},{7,5},{8,10},{9,11},{10,... | collective-permute-start | bytes 122888 | tf_op jit(solution)/shard_map/ppermute | solution.py:529
  32.1 2.9 %collective-permute-start.9 = (bf16[64,640]{1,0:T(8,128)(2,1)S(1)}, bf16[64,640]{1,0:T(8,128)(2,1)S(1)}, u32[]{:S(2)}, u32[]{:S(2)}) collective-permute-start(bf16[64,640]{1,0:T(8,128)(2,1)S(1)} %get-tuple-element.52), channel_id=1, source_target_pairs={{0,2},{1,3},{2,0},{3,1},{4,6},{5,7},{6,4},{7,5},{8,10},{9,11},{10,... | collective-permute-start | bytes 245768 | tf_op jit(solution)/shard_map/ppermute | solution.py:529
  35.1 4.5 %collective-permute-done.7.refs_4_ = bf16[64,640]{1,0:T(8,128)(2,1)S(1)} collective-permute-done((bf16[64,640]{1,0:T(8,128)(2,1)S(1)}, bf16[64,640]{1,0:T(8,128)(2,1)S(1)}, u32[]{:S(2)}, u32[]{:S(2)}) %collective-permute-start.7) | collective-permute-done | bytes 81952 | tf_op jit(solution)/shard_map/ppermute | solution.py:529
  39.5 3.2 %forward.3.refs_7_ = f32[640,256]{1,0:T(8,128)S(1)} custom-call(s32[64]{0:T(128)S(1)} %get-tuple-element.67.refs_0_, s32[1]{0:T(128)} %bitcast.refs_1_.refs_0_, f32[64,640]{1,0:T(8,128)S(1)} %get-tuple-element.55.refs_2_, bf16[64,640]{1,0:T(8,128)(2,1)S(1)} %slice_bitcast_fusion.3.refs_3_, bf16[64,640]{1,0:T(8,128)(2,1)S(1)} %collective-permute-done.7.refs_4_, ...), custom_call_target="tpu_custom_call" | custom-call | bytes 12870000 | tf_op jit(solution)/shard_map/forward/pallas_call | solution.py:569
  42.7 3.2 %forward.4.refs_8_ = f32[640,256]{1,0:T(8,128)S(1)} custom-call(s32[64]{0:T(128)S(1)} %get-tuple-element.66.refs_0_, s32[1]{0:T(128)} %bitcast.refs_1_.refs_0_, f32[64,640]{1,0:T(8,128)S(1)} %get-tuple-element.53.refs_2_, bf16[64,640]{1,0:T(8,128)(2,1)S(1)} %slice_bitcast_fusion.2.refs_3_, bf16[64,640]{1,0:T(8,128)(2,1)S(1)} %collective-permute-done.9.refs_4_, ...), custom_call_target="tpu_custom_call" | custom-call | bytes 12870000 | tf_op jit(solution)/shard_map/forward/pallas_call | solution.py:569
  45.9 2.0 %forward.5 = (f32[4,80,640]{2,1,0:T(8,128)S(1)}, f32[4,80,640]{2,1,0:T(8,128)S(1)}) custom-call(s32[32]{0:T(128)S(1)} %slice.73.refs_0_, s32[1]{0:T(128)} %bitcast.refs_1_.refs_0_, f32[32,640]{1,0:T(8,128)S(1)} %get-tuple-element.57.refs_2_, bf16[32,640]{1,0:T(8,128)(2,1)S(1)} %slice_bitcast_fusion.5.refs_3_, ...), custom_call_target="tpu_custom_call" | custom-call | bytes 7589999 | tf_op jit(solution)/shard_map/forward/pallas_call | solution.py:569
  48.0 2.3 %collective-permute-done.10 = f32[4,80,640]{2,1,0:T(8,128)S(1)} collective-permute-done((f32[4,80,640]{2,1,0:T(8,128)S(1)}, f32[4,80,640]{2,1,0:T(8,128)S(1)}, u32[]{:S(2)}, u32[]{:S(2)}) %collective-permute-start.10) | collective-permute-done | bytes 819232 | tf_op jit(solution)/shard_map/ppermute | solution.py:529
  50.4 1.3 %collective-permute-start.13 = (bf16[80,640]{1,0:T(8,128)(2,1)S(1)}, bf16[80,640]{1,0:T(8,128)(2,1)S(1)}, u32[]{:S(2)}, u32[]{:S(2)}) collective-permute-start(bf16[80,640]{1,0:T(8,128)(2,1)S(1)} %get-tuple-element.48), channel_id=1, source_target_pairs={{0,24},{4,28},{8,16},{12,20},{16,8},{20,12},{24,0},{28,4},{1,25},{... | collective-permute-start | bytes 307208 | tf_op jit(solution)/shard_map/ppermute | solution.py:529
  53.9 3.2 %collective-permute-done.13.refs_6_ = bf16[80,640]{1,0:T(8,128)(2,1)S(1)} collective-permute-done((bf16[80,640]{1,0:T(8,128)(2,1)S(1)}, bf16[80,640]{1,0:T(8,128)(2,1)S(1)}, u32[]{:S(2)}, u32[]{:S(2)}) %collective-permute-start.13) | collective-permute-done | bytes 102432 | tf_op jit(solution)/shard_map/ppermute | solution.py:529
  57.1 1.4 %collective-permute-done.12.refs_5_ = bf16[80,640]{1,0:T(8,128)(2,1)S(1)} collective-permute-done((bf16[80,640]{1,0:T(8,128)(2,1)S(1)}, bf16[80,640]{1,0:T(8,128)(2,1)S(1)}, u32[]{:S(2)}, u32[]{:S(2)}) %collective-permute-start.12) | collective-permute-done | bytes 102432 | tf_op jit(solution)/shard_map/ppermute | solution.py:529
  59.4 10.2 %all_gather.3.refs_1_ = bf16[640,640]{1,0:T(8,128)(2,1)S(1)} all-gather(bf16[80,640]{1,0:T(8,128)(2,1)S(1)} %get-tuple-element.40), channel_id=1, replica_groups=mesh['lat'=8,'lon'=4] {'lat'}, dimensions={0}, use_global_device_ids=true | all-gather | bytes 921600 | tf_op jit(solution)/shard_map/all_gather | solution.py:613
  69.5 2.2 %inverse.3 = (f32[32,640]{1,0:T(8,128)S(1)}, bf16[32,640]{1,0:T(8,128)(2,1)S(1)}) custom-call(s32[32]{0:T(128)S(1)} %slice.73.refs_0_, bf16[640,640]{1,0:T(8,128)(2,1)S(1)} %all_gather.3.refs_1_, bf16[160,80,640]{2,1,0:T(8,128)(2,1)S(1)} %load_table.1.refs_6_.refs_2_), custom_call_target="tpu_custom_call" | custom-call | bytes 7325999 | tf_op jit(solution)/shard_map/inverse/pallas_call | solution.py:617
  71.7 3.7 %inverse.4 = (f32[64,640]{1,0:T(8,128)S(1)}, bf16[64,640]{1,0:T(8,128)(2,1)S(1)}) custom-call(s32[64]{0:T(128)S(1)} %get-tuple-element.66.refs_0_, bf16[640,640]{1,0:T(8,128)(2,1)S(1)} %all_gather.3.refs_1_, bf16[160,80,640]{2,1,0:T(8,128)(2,1)S(1)} %load_table.1.refs_6_.refs_2_, bf16[32,640]{1,0:T(8,128)(2,1)S(1)} %get-tuple-element.41.refs_3_), custom_call_target="tpu_custom_call" | custom-call | bytes 13661999 | tf_op jit(solution)/shard_map/inverse/pallas_call | solution.py:617
  75.5 3.7 %inverse.5 = (f32[64,640]{1,0:T(8,128)S(1)}, bf16[64,640]{1,0:T(8,128)(2,1)S(1)}) custom-call(s32[64]{0:T(128)S(1)} %get-tuple-element.67.refs_0_, bf16[640,640]{1,0:T(8,128)(2,1)S(1)} %all_gather.3.refs_1_, bf16[160,80,640]{2,1,0:T(8,128)(2,1)S(1)} %load_table.1.refs_6_.refs_2_, bf16[64,640]{1,0:T(8,128)(2,1)S(1)} %get-tuple-element.42.refs_3_), custom_call_target="tpu_custom_call" | custom-call | bytes 13661999 | tf_op jit(solution)/shard_map/inverse/pallas_call | solution.py:617
  79.2 3.0 %collective-permute-start.15 = (bf16[64,640]{1,0:T(8,128)(2,1)S(1)}, bf16[64,640]{1,0:T(8,128)(2,1)S(1)}, u32[]{:S(2)}, u32[]{:S(2)}) collective-permute-start(bf16[64,640]{1,0:T(8,128)(2,1)S(1)} %get-tuple-element.44), channel_id=1, source_target_pairs={{0,2},{1,3},{2,0},{3,1},{4,6},{5,7},{6,4},{7,5},{8,10},{9,11},{10,... | collective-permute-start | bytes 245768 | tf_op jit(solution)/shard_map/ppermute | solution.py:529
  82.3 2.1 %collective-permute-start.20 = (bf16[32,640]{1,0:T(8,128)(2,1)S(1)}, bf16[32,640]{1,0:T(8,128)(2,1)S(1)}, u32[]{:S(2)}, u32[]{:S(2)}) collective-permute-start(bf16[32,640]{1,0:T(8,128)(2,1)S(1)} %get-tuple-element.41.refs_3_), channel_id=1, source_target_pairs={{0,1},{1,0},{2,3},{3,2},{4,5},{5,4},{6,7},{7,6},{8,9},{9,8},{10,11... | collective-permute-start | bytes 122888 | tf_op jit(solution)/shard_map/ppermute | solution.py:529
  84.4 2.0 %collective-permute-start.19 = (bf16[64,640]{1,0:T(8,128)(2,1)S(1)}, bf16[64,640]{1,0:T(8,128)(2,1)S(1)}, u32[]{:S(2)}, u32[]{:S(2)}) collective-permute-start(bf16[64,640]{1,0:T(8,128)(2,1)S(1)} %collective-permute-done.18.refs_2_), channel_id=1, source_target_pairs={{0,1},{1,0},{2,3},{3,2},{4,5},{5,4},{6,7},{7,6},{8,9},{9,8},{10,11... | collective-permute-start | bytes 245768 | tf_op jit(solution)/shard_map/ppermute | solution.py:529
  86.4 2.1 %collective-permute-done.21.refs_2_ = bf16[32,640]{1,0:T(8,128)(2,1)S(1)} collective-permute-done((bf16[32,640]{1,0:T(8,128)(2,1)S(1)}, bf16[32,640]{1,0:T(8,128)(2,1)S(1)}, u32[]{:S(2)}, u32[]{:S(2)}) %collective-permute-start.21) | collective-permute-done | bytes 40992 | tf_op jit(solution)/shard_map/ppermute | solution.py:529
  88.5 2.0 %collective-permute-start.16 = (bf16[64,640]{1,0:T(8,128)(2,1)S(1)}, bf16[64,640]{1,0:T(8,128)(2,1)S(1)}, u32[]{:S(2)}, u32[]{:S(2)}) collective-permute-start(bf16[64,640]{1,0:T(8,128)(2,1)S(1)} %collective-permute-done.15.refs_2_), channel_id=1, source_target_pairs={{0,1},{1,0},{2,3},{3,2},{4,5},{5,4},{6,7},{7,6},{8,9},{9,8},{10,11... | collective-permute-start | bytes 245768 | tf_op jit(solution)/shard_map/ppermute | solution.py:529
  91.6 3.9 %collective-permute-done.22.refs_3_ = bf16[32,640]{1,0:T(8,128)(2,1)S(1)} collective-permute-done((bf16[32,640]{1,0:T(8,128)(2,1)S(1)}, bf16[32,640]{1,0:T(8,128)(2,1)S(1)}, u32[]{:S(2)}, u32[]{:S(2)}) %collective-permute-start.22) | collective-permute-done | bytes 40992 | tf_op jit(solution)/shard_map/ppermute | solution.py:529
  96.6 1.5 %values.4.refs_4_ = f32[320,640]{1,0:T(8,128)S(1)} custom-call(f32[640,256]{1,0:T(8,128)S(1)} %pad_maximum_fusion.refs_4_.near_ref, f32[640,10]{1,0:T(8,128)S(1)} %broadcast_multiply_fusion.refs_5_.far_ref, f32[64,640]{1,0:T(8,128)S(1)} %get-tuple-element.45.refs_0_, bf16[64,640]{1,0:T(8,128)(2,1)S(1)} %collective-permute-done.17.refs_1_, ...), custom_call_target="tpu_custom_call" | custom-call | bytes 5280000 | tf_op jit(solution)/shard_map/values/pallas_call | solution.py:642
  98.1 2.3 %values.5 = f32[320,640]{1,0:T(8,128)} custom-call(f32[640,256]{1,0:T(8,128)S(1)} %pad_maximum_fusion.refs_4_.near_ref, f32[640,10]{1,0:T(8,128)S(1)} %broadcast_multiply_fusion.refs_5_.far_ref, f32[64,640]{1,0:T(8,128)S(1)} %get-tuple-element.43.refs_0_, bf16[64,640]{1,0:T(8,128)(2,1)S(1)} %collective-permute-done.14.refs_1_, ...), custom_call_target="tpu_custom_call" | custom-call | bytes 5280000 | tf_op jit(solution)/shard_map/values/pallas_call | solution.py:642
  (58 shorter events, 10.7 us)
Async XLA Ops:
  2.0 10.7 %collective-permute-start = (f32[4,640]{1,0:T(4,128)S(1)}, f32[4,640]{1,0:T(4,128)S(1)}, u32[]{:S(2)}, u32[]{:S(2)}) collective-permute-start(f32[4,640]{1,0:T(4,128)S(1)} %get-tuple-element.27), channel_id=1, source_target_pairs={{0,4},{4,8},{8,12},{12,16},{16,20},{20,24},{24,28},{28,0},{1,5},{5... | collective-permute-start | bytes 30728 | tf_op jit(solution)/shard_map/ppermute | solution.py:470
  2.6 10.2 %collective-permute-start.1 = (f32[4,640]{1,0:T(4,128)S(1)}, f32[4,640]{1,0:T(4,128)S(1)}, u32[]{:S(2)}, u32[]{:S(2)}) collective-permute-start(f32[4,640]{1,0:T(4,128)S(1)} %get-tuple-element.28), channel_id=1, source_target_pairs={{4,0},{8,4},{12,8},{16,12},{20,16},{24,20},{28,24},{0,28},{5,1},{9... | collective-permute-start | bytes 30728 | tf_op jit(solution)/shard_map/ppermute | solution.py:471
  5.5 7.2 %collective-permute-start.2 = (f32[80,4]{1,0:T(8,128)S(1)}, f32[80,4]{1,0:T(8,128)S(1)}, u32[]{:S(2)}, u32[]{:S(2)}) collective-permute-start(f32[80,4]{1,0:T(8,128)S(1)} %get-tuple-element.29), channel_id=1, source_target_pairs={{0,1},{1,2},{2,3},{3,0},{4,5},{5,6},{6,7},{7,4},{8,9},{9,10},{10,1... | collective-permute-start | bytes 3848 | tf_op jit(solution)/shard_map/ppermute | solution.py:472
  7.8 5.0 %collective-permute-start.3 = (f32[80,4]{1,0:T(8,128)S(1)}, f32[80,4]{1,0:T(8,128)S(1)}, u32[]{:S(2)}, u32[]{:S(2)}) collective-permute-start(f32[80,4]{1,0:T(8,128)S(1)} %get-tuple-element.30), channel_id=1, source_target_pairs={{1,0},{2,1},{3,2},{0,3},{5,4},{6,5},{7,6},{4,7},{9,8},{10,9},{11,1... | collective-permute-start | bytes 3848 | tf_op jit(solution)/shard_map/ppermute | solution.py:473
  12.8 0.7 copy-start.1
  19.6 9.4 %collective-permute-start.4 = (bf16[2,32,640]{2,1,0:T(8,128)(2,1)S(1)}, bf16[2,32,640]{2,1,0:T(8,128)(2,1)S(1)}, u32[]{:S(2)}, u32[]{:S(2)}) collective-permute-start(bf16[2,32,640]{2,1,0:T(8,128)(2,1)S(1)} %get-tuple-element.35), channel_id=1, source_target_pairs={{0,1},{1,0},{2,3},{3,2},{4,5},{5,4},{6,7},{7,6},{8,9},{9,8},{10,11... | collective-permute-start | bytes 245768 | tf_op jit(solution)/shard_map/ppermute | solution.py:529
  21.1 10.8 %collective-permute-start.6 = (bf16[2,64,640]{2,1,0:T(8,128)(2,1)S(1)}, bf16[2,64,640]{2,1,0:T(8,128)(2,1)S(1)}, u32[]{:S(2)}, u32[]{:S(2)}) collective-permute-start(bf16[2,64,640]{2,1,0:T(8,128)(2,1)S(1)} %get-tuple-element.36), channel_id=1, source_target_pairs={{0,1},{1,0},{2,3},{3,2},{4,5},{5,4},{6,7},{7,6},{8,9},{9,8},{10,11... | collective-permute-start | bytes 491528 | tf_op jit(solution)/shard_map/ppermute | solution.py:529
  22.6 9.5 %collective-permute-start.8 = (bf16[2,64,640]{2,1,0:T(8,128)(2,1)S(1)}, bf16[2,64,640]{2,1,0:T(8,128)(2,1)S(1)}, u32[]{:S(2)}, u32[]{:S(2)}) collective-permute-start(bf16[2,64,640]{2,1,0:T(8,128)(2,1)S(1)} %get-tuple-element.37), channel_id=1, source_target_pairs={{0,1},{1,0},{2,3},{3,2},{4,5},{5,4},{6,7},{7,6},{8,9},{9,8},{10,11... | collective-permute-start | bytes 491528 | tf_op jit(solution)/shard_map/ppermute | solution.py:529
  29.0 16.9 %collective-permute-start.5 = (bf16[32,640]{1,0:T(8,128)(2,1)S(1)}, bf16[32,640]{1,0:T(8,128)(2,1)S(1)}, u32[]{:S(2)}, u32[]{:S(2)}) collective-permute-start(bf16[32,640]{1,0:T(8,128)(2,1)S(1)} %get-tuple-element.56), channel_id=1, source_target_pairs={{0,2},{1,3},{2,0},{3,1},{4,6},{5,7},{6,4},{7,5},{8,10},{9,11},{10,... | collective-permute-start | bytes 122888 | tf_op jit(solution)/shard_map/ppermute | solution.py:529
  31.9 7.6 %collective-permute-start.7 = (bf16[64,640]{1,0:T(8,128)(2,1)S(1)}, bf16[64,640]{1,0:T(8,128)(2,1)S(1)}, u32[]{:S(2)}, u32[]{:S(2)}) collective-permute-start(bf16[64,640]{1,0:T(8,128)(2,1)S(1)} %get-tuple-element.54), channel_id=1, source_target_pairs={{0,2},{1,3},{2,0},{3,1},{4,6},{5,7},{6,4},{7,5},{8,10},{9,11},{10,... | collective-permute-start | bytes 245768 | tf_op jit(solution)/shard_map/ppermute | solution.py:529
  32.1 10.5 %collective-permute-start.9 = (bf16[64,640]{1,0:T(8,128)(2,1)S(1)}, bf16[64,640]{1,0:T(8,128)(2,1)S(1)}, u32[]{:S(2)}, u32[]{:S(2)}) collective-permute-start(bf16[64,640]{1,0:T(8,128)(2,1)S(1)} %get-tuple-element.52), channel_id=1, source_target_pairs={{0,2},{1,3},{2,0},{3,1},{4,6},{5,7},{6,4},{7,5},{8,10},{9,11},{10,... | collective-permute-start | bytes 245768 | tf_op jit(solution)/shard_map/ppermute | solution.py:529
  42.7 15.9 %copy-start = (f32[2,2]{1,0:T(2,128)S(1)}, f32[2,2]{1,0:T(2,128)}, u32[]{:S(2)}) copy-start(f32[2,2]{1,0:T(2,128)} %refs_2_.1) | copy-start | bytes 52
  42.7 15.9 %copy-start.2 = (f32[2]{0:T(128)S(1)}, f32[2]{0:T(128)}, u32[]{:S(2)}) copy-start(f32[2]{0:T(128)} %refs_1_.1) | copy-start | bytes 28
  47.9 2.4 %collective-permute-start.10 = (f32[4,80,640]{2,1,0:T(8,128)S(1)}, f32[4,80,640]{2,1,0:T(8,128)S(1)}, u32[]{:S(2)}, u32[]{:S(2)}) collective-permute-start(f32[4,80,640]{2,1,0:T(8,128)S(1)} %get-tuple-element.39), channel_id=1, source_target_pairs={{0,4},{4,0},{8,12},{12,8},{16,20},{20,16},{24,28},{28,24},{1,5},{5... | collective-permute-start | bytes 2457608 | tf_op jit(solution)/shard_map/ppermute | solution.py:529
  50.4 6.7 %collective-permute-start.13 = (bf16[80,640]{1,0:T(8,128)(2,1)S(1)}, bf16[80,640]{1,0:T(8,128)(2,1)S(1)}, u32[]{:S(2)}, u32[]{:S(2)}) collective-permute-start(bf16[80,640]{1,0:T(8,128)(2,1)S(1)} %get-tuple-element.48), channel_id=1, source_target_pairs={{0,24},{4,28},{8,16},{12,20},{16,8},{20,12},{24,0},{28,4},{1,25},{... | collective-permute-start | bytes 307208 | tf_op jit(solution)/shard_map/ppermute | solution.py:529
  51.7 6.8 %collective-permute-start.12 = (bf16[80,640]{1,0:T(8,128)(2,1)S(1)}, bf16[80,640]{1,0:T(8,128)(2,1)S(1)}, u32[]{:S(2)}, u32[]{:S(2)}) collective-permute-start(bf16[80,640]{1,0:T(8,128)(2,1)S(1)} %get-tuple-element.49), channel_id=1, source_target_pairs={{0,16},{4,20},{8,24},{12,28},{16,0},{20,4},{24,8},{28,12},{1,17},{... | collective-permute-start | bytes 307208 | tf_op jit(solution)/shard_map/ppermute | solution.py:529
  52.7 5.9 %collective-permute-start.11 = (bf16[80,640]{1,0:T(8,128)(2,1)S(1)}, bf16[80,640]{1,0:T(8,128)(2,1)S(1)}, u32[]{:S(2)}, u32[]{:S(2)}) collective-permute-start(bf16[80,640]{1,0:T(8,128)(2,1)S(1)} %get-tuple-element.50), channel_id=1, source_target_pairs={{0,8},{4,12},{8,0},{12,4},{16,24},{20,28},{24,16},{28,20},{1,9},{5... | collective-permute-start | bytes 307208 | tf_op jit(solution)/shard_map/ppermute | solution.py:529
  75.4 8.9 %collective-permute-start.18 = (bf16[64,640]{1,0:T(8,128)(2,1)S(1)}, bf16[64,640]{1,0:T(8,128)(2,1)S(1)}, u32[]{:S(2)}, u32[]{:S(2)}) collective-permute-start(bf16[64,640]{1,0:T(8,128)(2,1)S(1)} %get-tuple-element.42.refs_3_), channel_id=1, source_target_pairs={{0,2},{1,3},{2,0},{3,1},{4,6},{5,7},{6,4},{7,5},{8,10},{9,11},{10,... | collective-permute-start | bytes 245768 | tf_op jit(solution)/shard_map/ppermute | solution.py:529
  79.2 9.3 %collective-permute-start.15 = (bf16[64,640]{1,0:T(8,128)(2,1)S(1)}, bf16[64,640]{1,0:T(8,128)(2,1)S(1)}, u32[]{:S(2)}, u32[]{:S(2)}) collective-permute-start(bf16[64,640]{1,0:T(8,128)(2,1)S(1)} %get-tuple-element.44), channel_id=1, source_target_pairs={{0,2},{1,3},{2,0},{3,1},{4,6},{5,7},{6,4},{7,5},{8,10},{9,11},{10,... | collective-permute-start | bytes 245768 | tf_op jit(solution)/shard_map/ppermute | solution.py:529
  82.2 6.3 %collective-permute-start.21 = (bf16[32,640]{1,0:T(8,128)(2,1)S(1)}, bf16[32,640]{1,0:T(8,128)(2,1)S(1)}, u32[]{:S(2)}, u32[]{:S(2)}) collective-permute-start(bf16[32,640]{1,0:T(8,128)(2,1)S(1)} %get-tuple-element.41.refs_3_), channel_id=1, source_target_pairs={{0,2},{1,3},{2,0},{3,1},{4,6},{5,7},{6,4},{7,5},{8,10},{9,11},{10,... | collective-permute-start | bytes 122888 | tf_op jit(solution)/shard_map/ppermute | solution.py:529
  82.3 8.3 %collective-permute-start.20 = (bf16[32,640]{1,0:T(8,128)(2,1)S(1)}, bf16[32,640]{1,0:T(8,128)(2,1)S(1)}, u32[]{:S(2)}, u32[]{:S(2)}) collective-permute-start(bf16[32,640]{1,0:T(8,128)(2,1)S(1)} %get-tuple-element.41.refs_3_), channel_id=1, source_target_pairs={{0,1},{1,0},{2,3},{3,2},{4,5},{5,4},{6,7},{7,6},{8,9},{9,8},{10,11... | collective-permute-start | bytes 122888 | tf_op jit(solution)/shard_map/ppermute | solution.py:529
  84.4 12.2 %collective-permute-start.17 = (bf16[64,640]{1,0:T(8,128)(2,1)S(1)}, bf16[64,640]{1,0:T(8,128)(2,1)S(1)}, u32[]{:S(2)}, u32[]{:S(2)}) collective-permute-start(bf16[64,640]{1,0:T(8,128)(2,1)S(1)} %get-tuple-element.42.refs_3_), channel_id=1, source_target_pairs={{0,1},{1,0},{2,3},{3,2},{4,5},{5,4},{6,7},{7,6},{8,9},{9,8},{10,11... | collective-permute-start | bytes 245768 | tf_op jit(solution)/shard_map/ppermute | solution.py:529
  84.4 12.2 %collective-permute-start.19 = (bf16[64,640]{1,0:T(8,128)(2,1)S(1)}, bf16[64,640]{1,0:T(8,128)(2,1)S(1)}, u32[]{:S(2)}, u32[]{:S(2)}) collective-permute-start(bf16[64,640]{1,0:T(8,128)(2,1)S(1)} %collective-permute-done.18.refs_2_), channel_id=1, source_target_pairs={{0,1},{1,0},{2,3},{3,2},{4,5},{5,4},{6,7},{7,6},{8,9},{9,8},{10,11... | collective-permute-start | bytes 245768 | tf_op jit(solution)/shard_map/ppermute | solution.py:529
  88.5 9.5 %collective-permute-start.14 = (bf16[64,640]{1,0:T(8,128)(2,1)S(1)}, bf16[64,640]{1,0:T(8,128)(2,1)S(1)}, u32[]{:S(2)}, u32[]{:S(2)}) collective-permute-start(bf16[64,640]{1,0:T(8,128)(2,1)S(1)} %get-tuple-element.44), channel_id=1, source_target_pairs={{0,1},{1,0},{2,3},{3,2},{4,5},{5,4},{6,7},{7,6},{8,9},{9,8},{10,11... | collective-permute-start | bytes 245768 | tf_op jit(solution)/shard_map/ppermute | solution.py:529
  88.5 9.6 %collective-permute-start.16 = (bf16[64,640]{1,0:T(8,128)(2,1)S(1)}, bf16[64,640]{1,0:T(8,128)(2,1)S(1)}, u32[]{:S(2)}, u32[]{:S(2)}) collective-permute-start(bf16[64,640]{1,0:T(8,128)(2,1)S(1)} %collective-permute-done.15.refs_2_), channel_id=1, source_target_pairs={{0,1},{1,0},{2,3},{3,2},{4,5},{5,4},{6,7},{7,6},{8,9},{9,8},{10,11... | collective-permute-start | bytes 245768 | tf_op jit(solution)/shard_map/ppermute | solution.py:529
  90.5 4.9 %collective-permute-start.22 = (bf16[32,640]{1,0:T(8,128)(2,1)S(1)}, bf16[32,640]{1,0:T(8,128)(2,1)S(1)}, u32[]{:S(2)}, u32[]{:S(2)}) collective-permute-start(bf16[32,640]{1,0:T(8,128)(2,1)S(1)} %collective-permute-done.21.refs_2_), channel_id=1, source_target_pairs={{0,1},{1,0},{2,3},{3,2},{4,5},{5,4},{6,7},{7,6},{8,9},{9,8},{10,11... | collective-permute-start | bytes 122888 | tf_op jit(solution)/shard_map/ppermute | solution.py:529

commit v4 on v3

--- a/solution.py
+++ b/solution.py
@@ -2,6 +2,7 @@
 
 import jax
 import jax.numpy as jnp
+import numpy as np
 from jax import lax
 from jax.experimental import pallas as pl
 from jax.experimental.pallas import tpu as pltpu
@@ -161,40 +162,28 @@
     return [(i, i ^ step) for i in range(count)]
 
 
-def load_kernel(fields_hbm, winds_hbm, fields_ref, winds_ref, *refs):
-    first_row, last_row, first_column, last_column, semaphores = refs
-    fields_copy = pltpu.make_async_copy(fields_hbm, fields_ref, semaphores.at[0])
-    winds_copy = pltpu.make_async_copy(winds_hbm, winds_ref, semaphores.at[1])
-    fields_copy.start()
-    winds_copy.start()
-    fields_copy.wait()
+def load_kernel(count_in, *refs):
+    sources, targets = refs[:count_in], refs[count_in : 2 * count_in]
+    first_row, last_row, first_column, last_column, semaphores = refs[2 * count_in :]
+    copies = [
+        pltpu.make_async_copy(source, target, semaphores.at[i])
+        for i, (source, target) in enumerate(zip(sources, targets))
+    ]
+    for copy in copies:
+        copy.start()
+    copies[0].wait()
+    fields_ref = targets[0]
     count, rows, columns = fields_ref.shape
     for p in range(count):
         first_row[p : p + 1, :] = fields_ref[p, 0:1, :]
         last_row[p : p + 1, :] = fields_ref[p, rows - 1 : rows, :]
         first_column[:, p : p + 1] = fields_ref[p, :, 0:1]
         last_column[:, p : p + 1] = fields_ref[p, :, columns - 1 : columns]
-    winds_copy.wait()
-
-
-def load_table_kernel(after_ref, table_hbm, table_ref, semaphores):
-    parts = semaphores.shape[0]
-    share = table_ref.shape[0] // parts
-    copies = [
-        pltpu.make_async_copy(
-            table_hbm.at[pl.ds(i * share, share)],
-            table_ref.at[pl.ds(i * share, share)],
-            semaphores.at[i],
-        )
-        for i in range(parts)
-    ]
-    for copy in copies:
-        copy.start()
-    for copy in copies:
+    for copy in copies[1:]:
         copy.wait()
 
 
-def advance(flags, fields_ref, wind_ref, step_ref, above, below, before, after, stepped_ref):
+def advance(place, lat_count, fields_ref, wind_ref, step_ref, above, below, before, after, stepped_ref):
     count, rows, columns = fields_ref.shape
     lane = lax.broadcasted_iota(jnp.int32, (rows, columns), 1)
     row = lax.broadcasted_iota(jnp.int32, (rows, columns), 0)
@@ -211,8 +200,8 @@
         )
         westward = jnp.where(lane == 0, before[:, p : p + 1], pltpu.roll(field, 1, 1))
         other = fields_ref[p ^ 1, rows - 1 : rows, :]
-        low_edge = jnp.where(flags[1] == 1, other, below[p : p + 1, :])
-        high_edge = jnp.where(flags[0] == 1, 0.0, above[p : p + 1, :])
+        low_edge = jnp.where(place[0] == lat_count - 1, other, below[p : p + 1, :])
+        high_edge = jnp.where(place[0] == 0, 0.0, above[p : p + 1, :])
         toward = jnp.where(row == rows - 1, low_edge, pltpu.roll(field, rows - 1, 0))
         poleward = jnp.where(row == 0, high_edge, pltpu.roll(field, 1, 0))
         tendency = wind_ref[h] * steps * (eastward - westward) + 0.25 * wind_ref[
@@ -221,17 +210,17 @@
         stepped_ref[p * rows : (p + 1) * rows, :] = field - tendency
 
 
-def table_rows(near, far, first, share, blocks, part):
-    per_block = near.shape[0] // blocks
-    half = far.shape[1] // 2
+def table_rows(place, turns, first, share, blocks, part):
+    per_block = turns.shape[0] // blocks
+    half = (turns.shape[1] - 2 * LANES) // 2
     out = []
     for k in range(blocks):
-        at = pl.ds(k * per_block + first, share)
-        near_cos, near_sin = near[at, :LANES], near[at, LANES:]
-        far_cos, far_sin = far[at, :half], far[at, half:]
+        at = pl.ds(pl.multiple_of((place[1] ^ k) * per_block + first, 32), share)
+        near_cos, near_sin = turns[at, :LANES], turns[at, LANES : 2 * LANES]
+        far = turns[at, 2 * LANES :]
         columns = []
         for j in range(half):
-            c, s = far_cos[:, j : j + 1], far_sin[:, j : j + 1]
+            c, s = far[:, j : j + 1], far[:, half + j : half + j + 1]
             if part:
                 columns.append(-(s * near_cos + c * near_sin))
             else:
@@ -240,11 +229,11 @@
     return jnp.concatenate(out, axis=0)
 
 
-def zonal_sums(blocks, share, first, stepped_ref, near, far, outs):
+def zonal_sums(place, blocks, share, first, stepped_ref, turns, outs):
     high, low = split_halves(stepped_ref[...])
     count = stepped_ref.shape[0]
     for part in range(2):
-        rows_high, rows_low = split_halves(table_rows(near, far, first, share, blocks, part))
+        rows_high, rows_low = split_halves(table_rows(place, turns, first, share, blocks, part))
         sums = dot_rows(rows_high, high) + (dot_rows(rows_high, low) + dot_rows(rows_low, high))
         lanes = slice(part * count, (part + 1) * count)
         own, pair = outs
@@ -254,11 +243,23 @@
 
 
 def forward_kernel(
-    blocks, sections, rows, degree_dev, first, last, waves_ref, place_ref, *refs
+    blocks, sections, rows, degree_dev, base, first, last, waves_ref, place_ref, *refs
 ):
     received = refs[:blocks]
     weight_ref, table_ref = refs[blocks : blocks + 2]
     rest = refs[blocks + 2 :]
+    copies = []
+    if not first:
+        table_hbm, *rest, table_ref, s0, s1, s2, semaphores = table_ref, *rest
+        rest = [*rest, s0, s1, s2]
+        copies = [
+            pltpu.make_async_copy(
+                table_hbm.at[pl.ds(i * GROUP, GROUP)],
+                table_ref.at[pl.ds(i * GROUP, GROUP)],
+                semaphores.at[i],
+            )
+            for i in range(semaphores.shape[0])
+        ]
     spread_ref, kept_ref, turned_ref = rest[-3:]
     step = pl.program_id(0)
     half = sections // 2
@@ -269,18 +270,24 @@
 
     @pl.when(step == 0)
     def _():
+        for copy in copies:
+            copy.start()
         total = received[0][...].astype(F32)
         for other in received[1:]:
             total = total + other[...].astype(F32)
-        total = total * weight_ref[...]
         for c in range(2):
             for level in range(levels):
                 for h in range(2):
                     at = ((c * levels + level) * 2 + h) * rows
-                    spread_ref[:, h * half + level * 2 + c, 0:rows] = total[:, at : at + rows]
-
+                    spread_ref[:, h * half + level * 2 + c, 0:rows] = (
+                        total[:, at : at + rows] * weight_ref[...]
+                    )
+
+    for i, copy in enumerate(copies[: share // group]):
+        pl.when(step == i)(copy.wait)
     degree = lax.broadcasted_iota(jnp.int32, (2 * half, columns), 1)
     row = lax.broadcasted_iota(jnp.int32, (2 * half, 1), 0)
+    mine = place_ref[1] * base + first
     for u in range(0, group, 2):
         sums = []
         for v in (u, u + 1):
@@ -291,7 +298,9 @@
         north = jnp.concatenate([sums[0][:half], sums[1][:half]], axis=0)
         south = jnp.concatenate([sums[0][half:], sums[1][half:]], axis=0)
         slot = step * group + u
-        past = degree - jnp.where(row < half, waves_ref[slot], waves_ref[slot + 1])
+        past = degree - jnp.where(
+            row < half, waves_ref[mine + slot], waves_ref[mine + slot + 1]
+        )
         combined = north + jnp.where(past & 1 == 0, south, -south)
         combined = jnp.where(past >= 0, combined, 0.0)
         at = pl.ds(pl.multiple_of(slot * half, 2 * half), 2 * half)
@@ -300,6 +309,8 @@
 
     @pl.when(step == pl.num_programs(0) - 1)
     def _():
+        for copy in copies[share // group :]:
+            copy.wait()
         target = turned_ref if last else rest[-4]
         for t in range(columns // LANES):
             tile = jnp.concatenate(
@@ -348,7 +359,7 @@
         at, slot = at + levels * wide, slot + share
 
 
-def inverse_kernel(sections, rows, first, waves_ref, joined_ref, table_ref, *refs):
+def inverse_kernel(sections, rows, base, first, waves_ref, place_ref, joined_ref, table_ref, *refs):
     own_ref, out_ref, kept_ref, spread_ref = refs
     step = pl.program_id(0)
     half = sections // 2
@@ -370,19 +381,20 @@
     degree = lax.broadcasted_iota(jnp.int32, (2 * half, columns), 1)
     row = lax.broadcasted_iota(jnp.int32, (2 * half, 1), 0)
     upper = row < half
+    mine = place_ref[1] * base + first
     for u in range(0, group, 2):
         slot = step * group + u
         at = pl.ds(pl.multiple_of(slot * half, 2 * half), 2 * half)
         values = jnp.concatenate(
             [kept_ref[t, at, :] for t in range(columns // LANES)], axis=1
         )
-        even = (degree - jnp.where(upper, waves_ref[slot], waves_ref[slot + 1])) & 1 == 0
+        even = (degree - jnp.where(upper, waves_ref[mine + slot], waves_ref[mine + slot + 1])) & 1 == 0
         evens = jnp.where(even, values, 0.0)
         odds = pltpu.roll(jnp.where(even, 0.0, values), half, 0)
         for v in range(2):
             both = jnp.where(upper, odds, evens) if v else jnp.where(upper, evens, odds)
             sums = dot_rows(both.astype(BF16), table_ref[first + slot + v])
-            factor = jnp.where(waves_ref[slot + v] == 0, 1.0, 2.0) / math.sqrt(M)
+            factor = jnp.where(waves_ref[mine + slot + v] == 0, 1.0, 2.0) / math.sqrt(M)
             sums = sums * factor
             swapped = pltpu.roll(sums, half, 0)
             less = sums - swapped if v else swapped - sums
@@ -399,10 +411,10 @@
                     out_ref[:, at : at + rows] = value.astype(out_ref.dtype)
 
 
-def zonal_values(blocks, share, first, near, far, received, total):
+def zonal_values(place, blocks, share, first, turns, received, total):
     for part in range(2):
         count = received[0].shape[1] // 2
-        rows_high, rows_low = split_halves(table_rows(near, far, first, share, blocks, part))
+        rows_high, rows_low = split_halves(table_rows(place, turns, first, share, blocks, part))
         lanes = slice(part * count, (part + 1) * count)
         own_high, own_low = split_halves(received[0][:, lanes])
         coefs = jnp.concatenate([own_high] + [other[:, lanes] for other in received[1:]], axis=0)
@@ -451,18 +463,21 @@
     fields = level_fields.reshape(planes, rows_half, lon_dev)
     winds = wind_field.reshape(2 * hemis, rows_half, lon_dev)
 
-    fields, winds, first_row, last_row, first_column, last_column = pl.pallas_call(
-        load_kernel,
-        out_shape=[pltpu.VMEM(fields.shape, F32), pltpu.VMEM(winds.shape, F32)]
-        + [like((planes, lon_dev), F32)] * 2
-        + [like((rows_half, planes), F32)] * 2,
-        in_specs=[HBM] * 2,
-        out_specs=[VMEM] * 6,
-        scratch_shapes=[pltpu.SemaphoreType.DMA((2,))],
-        compiler_params=grant(8),
-        cost_estimate=cost(1.5),
-        name="load",
-    )(*[pltpu.with_memory_space_constraint(value, pltpu.HBM) for value in (fields, winds)])
+    arrays = [fields, winds, zonal_step[None, :], quad_weight[None, :]]
+    fields, winds, step_row, weight_row, first_row, last_row, first_column, last_column = (
+        pl.pallas_call(
+            lambda *refs: load_kernel(len(arrays), *refs),
+            out_shape=[pltpu.VMEM(value.shape, F32) for value in arrays]
+            + [like((planes, lon_dev), F32)] * 2
+            + [like((rows_half, planes), F32)] * 2,
+            in_specs=[HBM] * len(arrays),
+            out_specs=[VMEM] * (4 + len(arrays)),
+            scratch_shapes=[pltpu.SemaphoreType.DMA((len(arrays),))],
+            compiler_params=grant(8),
+            cost_estimate=cost(1.5),
+            name="load",
+        )(*[pltpu.with_memory_space_constraint(value, pltpu.HBM) for value in arrays])
+    )
     up = [(i, (i + 1) % lat_count) for i in range(lat_count)]
     east = [(i, (i + 1) % lon_count) for i in range(lon_count)]
     down = [(j, i) for i, j in up]
@@ -472,58 +487,50 @@
     before = lax.ppermute(last_column, "lon", east)
     after = lax.ppermute(first_column, "lon", west)
 
-    order = [
-        lax.dynamic_slice_in_dim(wave_table, (lon_index ^ k) * slots_dev, slots_dev)
-        for k in range(lon_count)
-    ]
-    my_waves = order[0]
-    waves = jnp.concatenate(order)
-    near_angle = angle_table(waves, jnp.arange(LANES, dtype=jnp.int32))
-    near = jnp.concatenate([jnp.cos(near_angle), jnp.sin(near_angle)], axis=1)
-    far_angle = angle_table(
-        waves, lon_index * lon_dev + LANES * jnp.arange(lon_dev // LANES, dtype=jnp.int32)
-    )
-    far = jnp.concatenate([jnp.cos(far_angle), jnp.sin(far_angle)], axis=1) / math.sqrt(NLON)
-
-    flags = jnp.stack([lat_index == 0, lat_index == lat_count - 1]).astype(jnp.int32)
-    place = lat_index.astype(jnp.int32).reshape(1)
-    weight_row = jnp.tile(quad_weight, sections)[None, :]
+    tiles = lon_dev // LANES
+    tile_columns = lon_index * lon_dev + LANES * jnp.arange(tiles, dtype=jnp.int32)
+    near_columns = jnp.arange(LANES, dtype=jnp.int32)
+    at_columns = jnp.concatenate([near_columns, near_columns, tile_columns, tile_columns])
+    ahead = np.repeat([NLON // 4, 0, NLON // 4, 0], [LANES, LANES, tiles, tiles]).astype(np.int32)
+    scale = np.repeat([1.0, 1.0 / math.sqrt(NLON)], [2 * LANES, 2 * tiles]).astype(np.float32)
+    turned = (wave_table[:, None] * at_columns[None, :] + ahead[None, :]) % NLON
+    turns = jnp.sin(turned.astype(F32) * (2.0 * math.pi / NLON)) * scale[None, :]
+    place = jnp.stack([lat_index, lon_index]).astype(jnp.int32)
+    waves = pltpu.with_memory_space_constraint(wave_table, pltpu.HBM)
 
     def sums_shape(share):
         return [like((lon_count // 2, share, width), dtype) for dtype in (F32, BF16)]
 
-    def first_sums(flags_ref, fields_ref, winds_ref, step_ref, *refs):
-        edges, near_ref, far_ref, stepped_ref = refs[:4], *refs[4:7]
-        advance(flags_ref, fields_ref, winds_ref, step_ref, *edges, stepped_ref)
-        zonal_sums(lon_count, CUTS[0], 0, stepped_ref, near_ref, far_ref, refs[7:])
+    def first_sums(place_ref, fields_ref, winds_ref, step_ref, *refs):
+        edges, turns_ref, stepped_ref = refs[:4], refs[4], refs[5]
+        advance(place_ref, lat_count, fields_ref, winds_ref, step_ref, *edges, stepped_ref)
+        zonal_sums(place_ref, lon_count, CUTS[0], 0, stepped_ref, turns_ref, refs[6:])
 
     stepped, *pieces = pl.pallas_call(
         first_sums,
         out_shape=[like((grid_count, lon_dev), F32)] + sums_shape(CUTS[0]),
-        in_specs=[SMEM] + [VMEM] * 9,
+        in_specs=[SMEM] + [VMEM] * 8,
         out_specs=[VMEM] * 3,
         compiler_params=grant(20),
         cost_estimate=cost(3.0),
         name="advance_and_sums",
-    )(
-        flags, fields, winds, zonal_step[None, :], above, below, before, after, near, far
-    )
+    )(place, fields, winds, step_row, above, below, before, after, turns)
 
     def later_sums(chunk, first, after):
         share = CUTS[chunk]
 
-        def body(stepped_ref, near_ref, far_ref, after_ref, *outs):
-            zonal_sums(lon_count, share, first, stepped_ref, near_ref, far_ref, outs)
+        def body(place_ref, stepped_ref, turns_ref, after_ref, *outs):
+            zonal_sums(place_ref, lon_count, share, first, stepped_ref, turns_ref, outs)
 
         return pl.pallas_call(
             body,
             out_shape=sums_shape(share),
-            in_specs=[VMEM] * 4,
+            in_specs=[SMEM] + [VMEM] * 3,
             out_specs=[VMEM] * 2,
             compiler_params=grant(20),
             cost_estimate=cost(0.035 * share),
             name="sums",
-        )(stepped, near, far, after)
+        )(place, stepped, turns, after)
 
     def swap(value, axis, step):
         return lax.ppermute(value, axis, pairs(lax.axis_size(axis), step))
@@ -548,51 +555,51 @@
         pieces = later_sums(chunk, first, pieces[0])
         swapped.append(to_owners(*pieces))
         first += CUTS[chunk]
-    table = pl.pallas_call(
-        load_table_kernel,
-        out_shape=pltpu.VMEM(legendre.shape, BF16),
-        in_specs=[VMEM, HBM],
-        out_specs=VMEM,
-        scratch_shapes=[pltpu.SemaphoreType.DMA((4,))],
-        compiler_params=grant(8),
-        cost_estimate=cost(5.7),
-        name="load_table",
-    )(pieces[0], pltpu.with_memory_space_constraint(legendre, pltpu.HBM))
-
-
-    def forward(first, share, parts, earlier, last):
+
+    def forward(first, share, parts, table, earlier, last):
         if last:
             shape = (lat_count // 2, degree_dev, half * slots_dev)
             shapes = [like(shape, F32)] * 2
         else:
             shapes = [like((columns, half * share), F32)]
+        specs = [whole_block(shape.shape) for shape in shapes]
+        loads, table_spec = [], VMEM
+        if not first:
+            shapes = shapes + [pltpu.VMEM(legendre.shape, BF16)]
+            specs = specs + [VMEM]
+            loads, table_spec = [pltpu.SemaphoreType.DMA((slots_dev // GROUP,))], HBM
         return pl.pallas_call(
             lambda *refs: forward_kernel(
-                len(parts), sections, rows_half, degree_dev, first, last, *refs
+                len(parts), sections, rows_half, degree_dev, slots_dev, first, last, *refs
             ),
             out_shape=shapes,
             grid_spec=pltpu.PrefetchScalarGridSpec(
                 num_scalar_prefetch=2,
                 grid=(share // GROUP,),
                 in_specs=[whole_block((share, width))] * len(parts)
-                + [whole_block((1, width)), VMEM]
+                + [whole_block((1, rows_half)), table_spec]
                 + [whole_block(other.shape) for other in earlier],
-                out_specs=[whole_block(shape.shape) for shape in shapes],
+                out_specs=specs,
                 scratch_shapes=[
                     pltpu.VMEM((share, sections, LANES), F32),
                     pltpu.VMEM((columns // LANES, half * share, LANES), F32),
                     pltpu.VMEM((columns, half * share), F32),
-                ],
+                ]
+                + loads,
             ),
             compiler_params=grant(20),
             cost_estimate=cost(0.05 * share + 0.7),
             name="forward",
-        )(my_waves[first : first + share], place, *parts, weight_row, table, *earlier)
-
+        )(waves, place, *parts, weight_row, table, *earlier)
+
+    table = pltpu.with_memory_space_constraint(legendre, pltpu.HBM)
     earlier, first = [], 0
     for chunk, share in enumerate(CUTS):
         last = chunk == len(CUTS) - 1
-        earlier += forward(first, share, swapped[chunk], earlier, last)
+        outs = forward(first, share, swapped[chunk], table, earlier, last)
+        if not first:
+            *outs, table = outs
+        earlier += outs
         first += share
     own, other = earlier[-2:]
 
@@ -613,12 +620,14 @@
     joined = lax.all_gather(rounded, "lat", axis=0, tiled=True)
 
     def inverse(first, share, after):
-        count = 3 + len(after)
+        count = 4 + len(after)
         return pl.pallas_call(
-            lambda *refs: inverse_kernel(sections, rows_half, first, *refs[:3], *refs[count:]),
+            lambda *refs: inverse_kernel(
+                sections, rows_half, slots_dev, first, *refs[:4], *refs[count:]
+            ),
             out_shape=[like((share, width), F32), like((share, width), BF16)],
             grid_spec=pltpu.PrefetchScalarGridSpec(
-                num_scalar_prefetch=1,
+                num_scalar_prefetch=2,
                 grid=(share // GROUP,),
                 in_specs=[whole_block(joined.shape), VMEM] + [VMEM] * len(after),
                 out_specs=[whole_block((share, width))] * 2,
@@ -630,24 +639,24 @@
             compiler_params=grant(20),
             cost_estimate=cost(0.06 * share + 0.3),
             name="inverse",
-        )(my_waves[first : first + share], joined, table, *after)
+        )(waves, place, joined, table, *after)
 
     def values(first, share, parts, base):
-        def body(near_ref, far_ref, *refs):
+        def body(place_ref, turns_ref, *refs):
             start = refs[lon_count][...] if base else None
             refs[-1][...] = zonal_values(
-                lon_count, share, first, near_ref, far_ref, refs[:lon_count], start
+                place_ref, lon_count, share, first, turns_ref, refs[:lon_count], start
             )
 
         return pl.pallas_call(
             body,
             out_shape=like((grid_count, lon_dev), F32),
-            in_specs=[VMEM] * (2 + lon_count + len(base)),
+            in_specs=[SMEM] + [VMEM] * (1 + lon_count + len(base)),
             out_specs=VMEM,
             compiler_params=grant(24),
             cost_estimate=cost(0.025 * share),
             name="values",
-        )(near, far, *parts, *base)
+        )(place, turns, *parts, *base)
 
     base, first, coefs = [], slots_dev, []
     for chunk in reversed(range(len(CUTS))):

time: 101 us -> 107 us (1.059)
  waiting for transfers between devices: 17.5 us -> 23.5 us
  starting transfers between devices: 29.4 us -> 26 us
  Pallas kernels: 36.9 us -> 40 us
  other arithmetic: 1.96 us -> 4.9 us
  local copies, waits for them, and re-layouts: 3.55 us -> 1.01 us
    ppermute x19, waiting for transfers between devices: 17.5 us -> 23.5 us  [swap(): return lax.ppermute(value, axis, pairs(lax.axis_size(axis), step))]
    pallas_call x3, Pallas kernels: 8.3 us -> 13.8 us  [forward(): pl.pallas_call(lambda *refs: forward_kernel(len(parts), sections, rows_ha...]
    mul x0 -> x1, other arithmetic: none -> 4.55 us  [tiled(): jnp.sin(turned.astype(F32) * (2.0 * math.pi / NLON)) * scale[None, :]]
    pallas_call x7 -> x6, Pallas kernels: 19.9 us -> 15.7 us  [the longest x3 10.1 us: inverse(): pl.pallas_call(lambda *refs: inverse_kernel(sections, rows_half, slots_de...]
    ppermute x19, starting transfers between devices: 21.6 us -> 18.2 us  [swap(): return lax.ppermute(value, axis, pairs(lax.axis_size(axis), step))]
    pallas_call x3, Pallas kernels: 4.9 us -> 6.55 us  [values(): pl.pallas_call(body, out_shape=like((grid_count, lon_dev), F32), in_specs...]
    cos x2 -> x0, other arithmetic: 1.56 us -> none  [the longest x1 1.39 us: tiled(): near = jnp.concatenate([jnp.cos(near_angle), jnp.sin(near_angle)], axis=1)]
  transfers between devices with their start and end apart: 23 -> 23, of which waited for: 7 -> 10; matrix products, arithmetic and copies ran while one was open for 5% -> 5% of each run, Pallas kernels for 18% -> 18%
where the time goes in v4:
time: 107 us
  Pallas kernels  40 us (37%)
  starting transfers between devices  26 us (24%)
  waiting for transfers between devices  23.5 us (22%)
  blocking collectives  10.5 us (10%)
  other arithmetic  4.9 us (5%)
    ppermute x19, waiting for transfers between devices, swap(): return lax.ppermute(value, axis, pairs(lax.axis_size(axis), step))  23.5 us
    ppermute x19, starting transfers between devices, swap(): return lax.ppermute(value, axis, pairs(lax.axis_size(axis), step))  18.2 us
    pallas_call x3, Pallas kernels, forward(): pl.pallas_call(lambda *refs: forward_kernel(len(parts), sections, rows_ha...  13.8 us
    all_gather x1, blocking collectives, tiled(): joined = lax.all_gather(rounded, 'lat', axis=0, tiled=True)  10.5 us
    pallas_call x3, Pallas kernels, inverse(): pl.pallas_call(lambda *refs: inverse_kernel(sections, rows_half, slots_de...  10.1 us
    pallas_call x3, Pallas kernels, values(): pl.pallas_call(body, out_shape=like((grid_count, lon_dev), F32), in_specs...  6.55 us
    mul x1, other arithmetic, tiled(): jnp.sin(turned.astype(F32) * (2.0 * math.pi / NLON)) * scale[None, :]  4.55 us
    pallas_call x2, Pallas kernels, later_sums(): pl.pallas_call(body, out_shape=sums_shape(share), in_specs=[SMEM] + [VMEM...  4.23 us
  transfers between devices with their start and end apart: 23, of which 10 were waited for; matrix products, arithmetic and copies ran while one was open for 5% of the time, Pallas kernels for 18%

profile of v4, /device:TPU:0, one launch (start us, length us, event | category | flops | bytes accessed | tf_op | source)
XLA Modules:
  0.0 106.8 jit_solution(3485432981647157105)
XLA Ops:
  2.6 2.9 %collective-permute-start.1 = (f32[4,640]{1,0:T(4,128)S(1)}, f32[4,640]{1,0:T(4,128)S(1)}, u32[]{:S(2)}, u32[]{:S(2)}) collective-permute-start(f32[4,640]{1,0:T(4,128)S(1)} %get-tuple-element.33), channel_id=1, source_target_pairs={{4,0},{8,4},{12,8},{16,12},{20,16},{24,20},{28,24},{0,28},{5,1},{9... | collective-permute-start | bytes 30728 | tf_op jit(solution)/shard_map/ppermute | solution.py:486
  5.6 2.3 %collective-permute-start.2 = (f32[80,4]{1,0:T(8,128)S(1)}, f32[80,4]{1,0:T(8,128)S(1)}, u32[]{:S(2)}, u32[]{:S(2)}) collective-permute-start(f32[80,4]{1,0:T(8,128)S(1)} %get-tuple-element.34), channel_id=1, source_target_pairs={{0,1},{1,2},{2,3},{3,0},{4,5},{5,6},{6,7},{7,4},{8,9},{9,10},{10,1... | collective-permute-start | bytes 3848 | tf_op jit(solution)/shard_map/ppermute | solution.py:487
  7.8 2.0 %collective-permute-start.3 = (f32[80,4]{1,0:T(8,128)S(1)}, f32[80,4]{1,0:T(8,128)S(1)}, u32[]{:S(2)}, u32[]{:S(2)}) collective-permute-start(f32[80,4]{1,0:T(8,128)S(1)} %get-tuple-element.35), channel_id=1, source_target_pairs={{1,0},{2,1},{3,2},{0,3},{5,4},{6,5},{7,6},{4,7},{9,8},{10,9},{11,1... | collective-permute-start | bytes 3848 | tf_op jit(solution)/shard_map/ppermute | solution.py:488
  9.9 4.5 %fusion.3.refs_4_.turns_ref = f32[640,266]{1,0:T(8,128)S(1)} fusion(f32[266]{0:T(512)} %constant.34, s32[266]{0:T(512)} %constant.33, s32[266]{0:T(512)S(1)} %pad_add_fusion, s32[640]{0:T(1024)} %refs_0_.11), kind=kLoop, calls=%fused_computation.4 | loop fusion | flops 1872640 | bytes 686712 | tf_op jit(solution)/shard_map/mul | solution.py:497
  14.6 3.1 %advance_and_sums.1 = (f32[320,640]{1,0:T(8,128)S(1)}, f32[2,64,640]{2,1,0:T(8,128)S(1)}, bf16[2,64,640]{2,1,0:T(8,128)(2,1)S(1)}) custom-call(s32[2]{0:T(128)S(1)} %pad_add_fusion.1.place_ref.refs_1_.refs_0_, f32[4,80,640]{2,1,0:T(8,128)S(1)} %get-tuple-element.29.fields_ref, f32[4,80,640]{2,1,0:T(8,128)S(1)} %get-tuple-element.30.winds_ref, ...), custom_call_target="tpu_custom_call" | custom-call | bytes 9900000 | tf_op jit(solution)/shard_map/advance_and_sums/pallas_call | solution.py:509
  17.7 2.4 %sums.2 = (f32[2,64,640]{2,1,0:T(8,128)S(1)}, bf16[2,64,640]{2,1,0:T(8,128)(2,1)S(1)}) custom-call(s32[2]{0:T(128)S(1)} %pad_add_fusion.1.place_ref.refs_1_.refs_0_, f32[320,640]{1,0:T(8,128)S(1)} %get-tuple-element.36.stepped_ref, f32[640,266]{1,0:T(8,128)S(1)} %fusion.3.refs_4_.turns_ref, f32[2,64,640]{2,1,0:T(8,128)S(1)} %get-tuple-element.37.after_ref), custom_call_target="tpu_custom_call" | custom-call | bytes 7392000 | tf_op jit(solution)/shard_map/sums/pallas_call | solution.py:525
  20.1 1.8 %sums.3 = (f32[2,32,640]{2,1,0:T(8,128)S(1)}, bf16[2,32,640]{2,1,0:T(8,128)(2,1)S(1)}) custom-call(s32[2]{0:T(128)S(1)} %pad_add_fusion.1.place_ref.refs_1_.refs_0_, f32[320,640]{1,0:T(8,128)S(1)} %get-tuple-element.36.stepped_ref, f32[640,266]{1,0:T(8,128)S(1)} %fusion.3.refs_4_.turns_ref, f32[2,64,640]{2,1,0:T(8,128)S(1)} %get-tuple-element.38.after_ref), custom_call_target="tpu_custom_call" | custom-call | bytes 3696000 | tf_op jit(solution)/shard_map/sums/pallas_call | solution.py:525
  22.0 2.0 %collective-permute-start.6 = (bf16[2,64,640]{2,1,0:T(8,128)(2,1)S(1)}, bf16[2,64,640]{2,1,0:T(8,128)(2,1)S(1)}, u32[]{:S(2)}, u32[]{:S(2)}) collective-permute-start(bf16[2,64,640]{2,1,0:T(8,128)(2,1)S(1)} %get-tuple-element.42), channel_id=1, source_target_pairs={{0,1},{1,0},{2,3},{3,2},{4,5},{5,4},{6,7},{7,6},{8,9},{9,8},{10,11... | collective-permute-start | bytes 491528 | tf_op jit(solution)/shard_map/ppermute | solution.py:536
  24.1 3.2 %collective-permute-done.4 = bf16[2,32,640]{2,1,0:T(8,128)(2,1)S(1)} collective-permute-done((bf16[2,32,640]{2,1,0:T(8,128)(2,1)S(1)}, bf16[2,32,640]{2,1,0:T(8,128)(2,1)S(1)}, u32[]{:S(2)}, u32[]{:S(2)}) %collective-permute-start.4) | collective-permute-done | bytes 81952 | tf_op jit(solution)/shard_map/ppermute | solution.py:536
  28.4 3.2 %collective-permute-done.6 = bf16[2,64,640]{2,1,0:T(8,128)(2,1)S(1)} collective-permute-done((bf16[2,64,640]{2,1,0:T(8,128)(2,1)S(1)}, bf16[2,64,640]{2,1,0:T(8,128)(2,1)S(1)}, u32[]{:S(2)}, u32[]{:S(2)}) %collective-permute-start.6) | collective-permute-done | bytes 163872 | tf_op jit(solution)/shard_map/ppermute | solution.py:536
  31.9 1.9 %collective-permute-done.8 = bf16[2,64,640]{2,1,0:T(8,128)(2,1)S(1)} collective-permute-done((bf16[2,64,640]{2,1,0:T(8,128)(2,1)S(1)}, bf16[2,64,640]{2,1,0:T(8,128)(2,1)S(1)}, u32[]{:S(2)}, u32[]{:S(2)}) %collective-permute-start.8) | collective-permute-done | bytes 163872 | tf_op jit(solution)/shard_map/ppermute | solution.py:536
  34.8 3.1 %collective-permute-done.7.refs_4_ = bf16[64,640]{1,0:T(8,128)(2,1)S(1)} collective-permute-done((bf16[64,640]{1,0:T(8,128)(2,1)S(1)}, bf16[64,640]{1,0:T(8,128)(2,1)S(1)}, u32[]{:S(2)}, u32[]{:S(2)}) %collective-permute-start.7) | collective-permute-done | bytes 81952 | tf_op jit(solution)/shard_map/ppermute | solution.py:536
  37.9 7.3 %forward.3 = (f32[640,256]{1,0:T(8,128)S(1)}, bf16[160,80,640]{2,1,0:T(8,128)(2,1)S(1)}) custom-call(s32[640]{0:T(1024)} %refs_0_.11, s32[2]{0:T(128)S(1)} %pad_add_fusion.1.place_ref.refs_1_.refs_0_, f32[64,640]{1,0:T(8,128)S(1)} %get-tuple-element.63.refs_2_, bf16[64,640]{1,0:T(8,128)(2,1)S(1)} %slice_bitcast_fusion.3.refs_3_, ...), custom_call_target="tpu_custom_call" | custom-call | bytes 12870000 | tf_op jit(solution)/shard_map/forward/pallas_call | solution.py:571
  45.3 3.9 %forward.4.refs_8_ = f32[640,256]{1,0:T(8,128)S(1)} custom-call(s32[640]{0:T(1024)} %refs_0_.11, s32[2]{0:T(128)S(1)} %pad_add_fusion.1.place_ref.refs_1_.refs_0_, f32[64,640]{1,0:T(8,128)S(1)} %get-tuple-element.61.refs_2_, bf16[64,640]{1,0:T(8,128)(2,1)S(1)} %slice_bitcast_fusion.2.refs_3_, bf16[64,640]{1,0:T(8,128)(2,1)S(1)} %collective-permute-done.9.refs_4_, ...), custom_call_target="tpu_custom_call" | custom-call | bytes 12870000 | tf_op jit(solution)/shard_map/forward/pallas_call | solution.py:571
  49.3 2.5 %forward.5 = (f32[4,80,640]{2,1,0:T(8,128)S(1)}, f32[4,80,640]{2,1,0:T(8,128)S(1)}) custom-call(s32[640]{0:T(1024)} %refs_0_.11, s32[2]{0:T(128)S(1)} %pad_add_fusion.1.place_ref.refs_1_.refs_0_, f32[32,640]{1,0:T(8,128)S(1)} %get-tuple-element.65.refs_2_, bf16[32,640]{1,0:T(8,128)(2,1)S(1)} %slice_bitcast_fusion.5.refs_3_, ...), custom_call_target="tpu_custom_call" | custom-call | bytes 7589999 | tf_op jit(solution)/shard_map/forward/pallas_call | solution.py:571
  51.9 2.3 %collective-permute-done.10 = f32[4,80,640]{2,1,0:T(8,128)S(1)} collective-permute-done((f32[4,80,640]{2,1,0:T(8,128)S(1)}, f32[4,80,640]{2,1,0:T(8,128)S(1)}, u32[]{:S(2)}, u32[]{:S(2)}) %collective-permute-start.10) | collective-permute-done | bytes 819232 | tf_op jit(solution)/shard_map/ppermute | solution.py:536
  54.3 1.5 %collective-permute-start.13 = (bf16[80,640]{1,0:T(8,128)(2,1)S(1)}, bf16[80,640]{1,0:T(8,128)(2,1)S(1)}, u32[]{:S(2)}, u32[]{:S(2)}) collective-permute-start(bf16[80,640]{1,0:T(8,128)(2,1)S(1)} %get-tuple-element.56), channel_id=1, source_target_pairs={{0,24},{4,28},{8,16},{12,20},{16,8},{20,12},{24,0},{28,4},{1,25},{... | collective-permute-start | bytes 307208 | tf_op jit(solution)/shard_map/ppermute | solution.py:536
  55.8 1.5 %collective-permute-start.12 = (bf16[80,640]{1,0:T(8,128)(2,1)S(1)}, bf16[80,640]{1,0:T(8,128)(2,1)S(1)}, u32[]{:S(2)}, u32[]{:S(2)}) collective-permute-start(bf16[80,640]{1,0:T(8,128)(2,1)S(1)} %get-tuple-element.57), channel_id=1, source_target_pairs={{0,16},{4,20},{8,24},{12,28},{16,0},{20,4},{24,8},{28,12},{1,17},{... | collective-permute-start | bytes 307208 | tf_op jit(solution)/shard_map/ppermute | solution.py:536
  57.9 3.1 %collective-permute-done.13.refs_6_ = bf16[80,640]{1,0:T(8,128)(2,1)S(1)} collective-permute-done((bf16[80,640]{1,0:T(8,128)(2,1)S(1)}, bf16[80,640]{1,0:T(8,128)(2,1)S(1)}, u32[]{:S(2)}, u32[]{:S(2)}) %collective-permute-start.13) | collective-permute-done | bytes 102432 | tf_op jit(solution)/shard_map/ppermute | solution.py:536
  63.3 10.5 %all_gather.3.refs_2_ = bf16[640,640]{1,0:T(8,128)(2,1)S(1)} all-gather(bf16[80,640]{1,0:T(8,128)(2,1)S(1)} %get-tuple-element.48), channel_id=1, replica_groups=mesh['lat'=8,'lon'=4] {'lat'}, dimensions={0}, use_global_device_ids=true | all-gather | bytes 921600 | tf_op jit(solution)/shard_map/all_gather | solution.py:620
  73.8 2.3 %inverse.3 = (f32[32,640]{1,0:T(8,128)S(1)}, bf16[32,640]{1,0:T(8,128)(2,1)S(1)}) custom-call(s32[640]{0:T(1024)} %refs_0_.11, s32[2]{0:T(128)S(1)} %pad_add_fusion.1.place_ref.refs_1_.refs_0_, bf16[640,640]{1,0:T(8,128)(2,1)S(1)} %all_gather.3.refs_2_, bf16[160,80,640]{2,1,0:T(8,128)(2,1)S(1)} %get-tuple-element.43.refs_6_.refs_3_), custom_call_target="tpu_custom_call" | custom-call | bytes 7325999 | tf_op jit(solution)/shard_map/inverse/pallas_call | solution.py:624
  76.1 3.9 %inverse.4 = (f32[64,640]{1,0:T(8,128)S(1)}, bf16[64,640]{1,0:T(8,128)(2,1)S(1)}) custom-call(s32[640]{0:T(1024)} %refs_0_.11, s32[2]{0:T(128)S(1)} %pad_add_fusion.1.place_ref.refs_1_.refs_0_, bf16[640,640]{1,0:T(8,128)(2,1)S(1)} %all_gather.3.refs_2_, bf16[160,80,640]{2,1,0:T(8,128)(2,1)S(1)} %get-tuple-element.43.refs_6_.refs_3_, ...), custom_call_target="tpu_custom_call" | custom-call | bytes 13661999 | tf_op jit(solution)/shard_map/inverse/pallas_call | solution.py:624
  80.1 3.9 %inverse.5 = (f32[64,640]{1,0:T(8,128)S(1)}, bf16[64,640]{1,0:T(8,128)(2,1)S(1)}) custom-call(s32[640]{0:T(1024)} %refs_0_.11, s32[2]{0:T(128)S(1)} %pad_add_fusion.1.place_ref.refs_1_.refs_0_, bf16[640,640]{1,0:T(8,128)(2,1)S(1)} %all_gather.3.refs_2_, bf16[160,80,640]{2,1,0:T(8,128)(2,1)S(1)} %get-tuple-element.43.refs_6_.refs_3_, ...), custom_call_target="tpu_custom_call" | custom-call | bytes 13661999 | tf_op jit(solution)/shard_map/inverse/pallas_call | solution.py:624
  83.9 3.0 %collective-permute-start.15 = (bf16[64,640]{1,0:T(8,128)(2,1)S(1)}, bf16[64,640]{1,0:T(8,128)(2,1)S(1)}, u32[]{:S(2)}, u32[]{:S(2)}) collective-permute-start(bf16[64,640]{1,0:T(8,128)(2,1)S(1)} %get-tuple-element.52), channel_id=1, source_target_pairs={{0,2},{1,3},{2,0},{3,1},{4,6},{5,7},{6,4},{7,5},{8,10},{9,11},{10,... | collective-permute-start | bytes 245768 | tf_op jit(solution)/shard_map/ppermute | solution.py:536
  87.0 2.5 %collective-permute-start.20 = (bf16[32,640]{1,0:T(8,128)(2,1)S(1)}, bf16[32,640]{1,0:T(8,128)(2,1)S(1)}, u32[]{:S(2)}, u32[]{:S(2)}) collective-permute-start(bf16[32,640]{1,0:T(8,128)(2,1)S(1)} %get-tuple-element.49.refs_4_), channel_id=1, source_target_pairs={{0,1},{1,0},{2,3},{3,2},{4,5},{5,4},{6,7},{7,6},{8,9},{9,8},{10,11... | collective-permute-start | bytes 122888 | tf_op jit(solution)/shard_map/ppermute | solution.py:536
  89.6 2.0 %collective-permute-start.19 = (bf16[64,640]{1,0:T(8,128)(2,1)S(1)}, bf16[64,640]{1,0:T(8,128)(2,1)S(1)}, u32[]{:S(2)}, u32[]{:S(2)}) collective-permute-start(bf16[64,640]{1,0:T(8,128)(2,1)S(1)} %collective-permute-done.18.refs_2_), channel_id=1, source_target_pairs={{0,1},{1,0},{2,3},{3,2},{4,5},{5,4},{6,7},{7,6},{8,9},{9,8},{10,11... | collective-permute-start | bytes 245768 | tf_op jit(solution)/shard_map/ppermute | solution.py:536
  91.6 1.7 %collective-permute-done.21.refs_2_ = bf16[32,640]{1,0:T(8,128)(2,1)S(1)} collective-permute-done((bf16[32,640]{1,0:T(8,128)(2,1)S(1)}, bf16[32,640]{1,0:T(8,128)(2,1)S(1)}, u32[]{:S(2)}, u32[]{:S(2)}) %collective-permute-start.21) | collective-permute-done | bytes 40992 | tf_op jit(solution)/shard_map/ppermute | solution.py:536
  93.7 1.6 %collective-permute-start.16 = (bf16[64,640]{1,0:T(8,128)(2,1)S(1)}, bf16[64,640]{1,0:T(8,128)(2,1)S(1)}, u32[]{:S(2)}, u32[]{:S(2)}) collective-permute-start(bf16[64,640]{1,0:T(8,128)(2,1)S(1)} %collective-permute-done.15.refs_2_), channel_id=1, source_target_pairs={{0,1},{1,0},{2,3},{3,2},{4,5},{5,4},{6,7},{7,6},{8,9},{9,8},{10,11... | collective-permute-start | bytes 245768 | tf_op jit(solution)/shard_map/ppermute | solution.py:536
  96.7 3.5 %collective-permute-done.22.refs_3_ = bf16[32,640]{1,0:T(8,128)(2,1)S(1)} collective-permute-done((bf16[32,640]{1,0:T(8,128)(2,1)S(1)}, bf16[32,640]{1,0:T(8,128)(2,1)S(1)}, u32[]{:S(2)}, u32[]{:S(2)}) %collective-permute-start.22) | collective-permute-done | bytes 40992 | tf_op jit(solution)/shard_map/ppermute | solution.py:536
  100.2 1.6 %values.3.refs_4_ = f32[320,640]{1,0:T(8,128)S(1)} custom-call(s32[2]{0:T(128)S(1)} %pad_add_fusion.1.place_ref.refs_1_.refs_0_, f32[640,266]{1,0:T(8,128)S(1)} %fusion.3.refs_4_.turns_ref, f32[32,640]{1,0:T(8,128)S(1)} %get-tuple-element.54.refs_0_, bf16[32,640]{1,0:T(8,128)(2,1)S(1)} %collective-permute-done.20.refs_1_, ...), custom_call_target="tpu_custom_call" | custom-call | bytes 2640000 | tf_op jit(solution)/shard_map/values/pallas_call | solution.py:651
  101.9 2.0 %values.4.refs_4_ = f32[320,640]{1,0:T(8,128)S(1)} custom-call(s32[2]{0:T(128)S(1)} %pad_add_fusion.1.place_ref.refs_1_.refs_0_, f32[640,266]{1,0:T(8,128)S(1)} %fusion.3.refs_4_.turns_ref, f32[64,640]{1,0:T(8,128)S(1)} %get-tuple-element.53.refs_0_, bf16[64,640]{1,0:T(8,128)(2,1)S(1)} %collective-permute-done.17.refs_1_, ...), custom_call_target="tpu_custom_call" | custom-call | bytes 5280000 | tf_op jit(solution)/shard_map/values/pallas_call | solution.py:651
  103.9 2.9 %values.5 = f32[320,640]{1,0:T(8,128)} custom-call(s32[2]{0:T(128)S(1)} %pad_add_fusion.1.place_ref.refs_1_.refs_0_, f32[640,266]{1,0:T(8,128)S(1)} %fusion.3.refs_4_.turns_ref, f32[64,640]{1,0:T(8,128)S(1)} %get-tuple-element.51.refs_0_, bf16[64,640]{1,0:T(8,128)(2,1)S(1)} %collective-permute-done.14.refs_1_, ...), custom_call_target="tpu_custom_call" | custom-call | bytes 5280000 | tf_op jit(solution)/shard_map/values/pallas_call | solution.py:651
  (46 shorter events, 9.8 us)
Async XLA Ops:
  2.1 12.5 %collective-permute-start = (f32[4,640]{1,0:T(4,128)S(1)}, f32[4,640]{1,0:T(4,128)S(1)}, u32[]{:S(2)}, u32[]{:S(2)}) collective-permute-start(f32[4,640]{1,0:T(4,128)S(1)} %get-tuple-element.32), channel_id=1, source_target_pairs={{0,4},{4,8},{8,12},{12,16},{16,20},{20,24},{24,28},{28,0},{1,5},{5... | collective-permute-start | bytes 30728 | tf_op jit(solution)/shard_map/ppermute | solution.py:485
  2.6 12.0 %collective-permute-start.1 = (f32[4,640]{1,0:T(4,128)S(1)}, f32[4,640]{1,0:T(4,128)S(1)}, u32[]{:S(2)}, u32[]{:S(2)}) collective-permute-start(f32[4,640]{1,0:T(4,128)S(1)} %get-tuple-element.33), channel_id=1, source_target_pairs={{4,0},{8,4},{12,8},{16,12},{20,16},{24,20},{28,24},{0,28},{5,1},{9... | collective-permute-start | bytes 30728 | tf_op jit(solution)/shard_map/ppermute | solution.py:486
  5.6 9.0 %collective-permute-start.2 = (f32[80,4]{1,0:T(8,128)S(1)}, f32[80,4]{1,0:T(8,128)S(1)}, u32[]{:S(2)}, u32[]{:S(2)}) collective-permute-start(f32[80,4]{1,0:T(8,128)S(1)} %get-tuple-element.34), channel_id=1, source_target_pairs={{0,1},{1,2},{2,3},{3,0},{4,5},{5,6},{6,7},{7,4},{8,9},{9,10},{10,1... | collective-permute-start | bytes 3848 | tf_op jit(solution)/shard_map/ppermute | solution.py:487
  7.8 6.8 %collective-permute-start.3 = (f32[80,4]{1,0:T(8,128)S(1)}, f32[80,4]{1,0:T(8,128)S(1)}, u32[]{:S(2)}, u32[]{:S(2)}) collective-permute-start(f32[80,4]{1,0:T(8,128)S(1)} %get-tuple-element.35), channel_id=1, source_target_pairs={{1,0},{2,1},{3,2},{0,3},{5,4},{6,5},{7,6},{4,7},{9,8},{10,9},{11,1... | collective-permute-start | bytes 3848 | tf_op jit(solution)/shard_map/ppermute | solution.py:488
  21.9 5.4 %collective-permute-start.4 = (bf16[2,32,640]{2,1,0:T(8,128)(2,1)S(1)}, bf16[2,32,640]{2,1,0:T(8,128)(2,1)S(1)}, u32[]{:S(2)}, u32[]{:S(2)}) collective-permute-start(bf16[2,32,640]{2,1,0:T(8,128)(2,1)S(1)} %get-tuple-element.40), channel_id=1, source_target_pairs={{0,1},{1,0},{2,3},{3,2},{4,5},{5,4},{6,7},{7,6},{8,9},{9,8},{10,11... | collective-permute-start | bytes 245768 | tf_op jit(solution)/shard_map/ppermute | solution.py:536
  22.0 9.6 %collective-permute-start.6 = (bf16[2,64,640]{2,1,0:T(8,128)(2,1)S(1)}, bf16[2,64,640]{2,1,0:T(8,128)(2,1)S(1)}, u32[]{:S(2)}, u32[]{:S(2)}) collective-permute-start(bf16[2,64,640]{2,1,0:T(8,128)(2,1)S(1)} %get-tuple-element.42), channel_id=1, source_target_pairs={{0,1},{1,0},{2,3},{3,2},{4,5},{5,4},{6,7},{7,6},{8,9},{9,8},{10,11... | collective-permute-start | bytes 491528 | tf_op jit(solution)/shard_map/ppermute | solution.py:536
  24.0 9.8 %collective-permute-start.8 = (bf16[2,64,640]{2,1,0:T(8,128)(2,1)S(1)}, bf16[2,64,640]{2,1,0:T(8,128)(2,1)S(1)}, u32[]{:S(2)}, u32[]{:S(2)}) collective-permute-start(bf16[2,64,640]{2,1,0:T(8,128)(2,1)S(1)} %get-tuple-element.45), channel_id=1, source_target_pairs={{0,1},{1,0},{2,3},{3,2},{4,5},{5,4},{6,7},{7,6},{8,9},{9,8},{10,11... | collective-permute-start | bytes 491528 | tf_op jit(solution)/shard_map/ppermute | solution.py:536
  27.3 21.9 %collective-permute-start.5 = (bf16[32,640]{1,0:T(8,128)(2,1)S(1)}, bf16[32,640]{1,0:T(8,128)(2,1)S(1)}, u32[]{:S(2)}, u32[]{:S(2)}) collective-permute-start(bf16[32,640]{1,0:T(8,128)(2,1)S(1)} %get-tuple-element.64), channel_id=1, source_target_pairs={{0,2},{1,3},{2,0},{3,1},{4,6},{5,7},{6,4},{7,5},{8,10},{9,11},{10,... | collective-permute-start | bytes 122888 | tf_op jit(solution)/shard_map/ppermute | solution.py:536
  31.7 6.3 %collective-permute-start.7 = (bf16[64,640]{1,0:T(8,128)(2,1)S(1)}, bf16[64,640]{1,0:T(8,128)(2,1)S(1)}, u32[]{:S(2)}, u32[]{:S(2)}) collective-permute-start(bf16[64,640]{1,0:T(8,128)(2,1)S(1)} %get-tuple-element.62), channel_id=1, source_target_pairs={{0,2},{1,3},{2,0},{3,1},{4,6},{5,7},{6,4},{7,5},{8,10},{9,11},{10,... | collective-permute-start | bytes 245768 | tf_op jit(solution)/shard_map/ppermute | solution.py:536
  33.9 11.4 %collective-permute-start.9 = (bf16[64,640]{1,0:T(8,128)(2,1)S(1)}, bf16[64,640]{1,0:T(8,128)(2,1)S(1)}, u32[]{:S(2)}, u32[]{:S(2)}) collective-permute-start(bf16[64,640]{1,0:T(8,128)(2,1)S(1)} %get-tuple-element.60), channel_id=1, source_target_pairs={{0,2},{1,3},{2,0},{3,1},{4,6},{5,7},{6,4},{7,5},{8,10},{9,11},{10,... | collective-permute-start | bytes 245768 | tf_op jit(solution)/shard_map/ppermute | solution.py:536
  45.3 17.2 %copy-start = (f32[2,2]{1,0:T(2,128)S(1)}, f32[2,2]{1,0:T(2,128)}, u32[]{:S(2)}) copy-start(f32[2,2]{1,0:T(2,128)} %refs_2_.1) | copy-start | bytes 52
  45.3 17.2 %copy-start.1 = (f32[2]{0:T(128)S(1)}, f32[2]{0:T(128)}, u32[]{:S(2)}) copy-start(f32[2]{0:T(128)} %refs_1_.1) | copy-start | bytes 28
  51.8 2.4 %collective-permute-start.10 = (f32[4,80,640]{2,1,0:T(8,128)S(1)}, f32[4,80,640]{2,1,0:T(8,128)S(1)}, u32[]{:S(2)}, u32[]{:S(2)}) collective-permute-start(f32[4,80,640]{2,1,0:T(8,128)S(1)} %get-tuple-element.47), channel_id=1, source_target_pairs={{0,4},{4,0},{8,12},{12,8},{16,20},{20,16},{24,28},{28,24},{1,5},{5... | collective-permute-start | bytes 2457608 | tf_op jit(solution)/shard_map/ppermute | solution.py:536
  54.3 6.6 %collective-permute-start.13 = (bf16[80,640]{1,0:T(8,128)(2,1)S(1)}, bf16[80,640]{1,0:T(8,128)(2,1)S(1)}, u32[]{:S(2)}, u32[]{:S(2)}) collective-permute-start(bf16[80,640]{1,0:T(8,128)(2,1)S(1)} %get-tuple-element.56), channel_id=1, source_target_pairs={{0,24},{4,28},{8,16},{12,20},{16,8},{20,12},{24,0},{28,4},{1,25},{... | collective-permute-start | bytes 307208 | tf_op jit(solution)/shard_map/ppermute | solution.py:536
  55.8 6.6 %collective-permute-start.12 = (bf16[80,640]{1,0:T(8,128)(2,1)S(1)}, bf16[80,640]{1,0:T(8,128)(2,1)S(1)}, u32[]{:S(2)}, u32[]{:S(2)}) collective-permute-start(bf16[80,640]{1,0:T(8,128)(2,1)S(1)} %get-tuple-element.57), channel_id=1, source_target_pairs={{0,16},{4,20},{8,24},{12,28},{16,0},{20,4},{24,8},{28,12},{1,17},{... | collective-permute-start | bytes 307208 | tf_op jit(solution)/shard_map/ppermute | solution.py:536
  57.3 5.1 %collective-permute-start.11 = (bf16[80,640]{1,0:T(8,128)(2,1)S(1)}, bf16[80,640]{1,0:T(8,128)(2,1)S(1)}, u32[]{:S(2)}, u32[]{:S(2)}) collective-permute-start(bf16[80,640]{1,0:T(8,128)(2,1)S(1)} %get-tuple-element.58), channel_id=1, source_target_pairs={{0,8},{4,12},{8,0},{12,4},{16,24},{20,28},{24,16},{28,20},{1,9},{5... | collective-permute-start | bytes 307208 | tf_op jit(solution)/shard_map/ppermute | solution.py:536
  80.0 9.6 %collective-permute-start.18 = (bf16[64,640]{1,0:T(8,128)(2,1)S(1)}, bf16[64,640]{1,0:T(8,128)(2,1)S(1)}, u32[]{:S(2)}, u32[]{:S(2)}) collective-permute-start(bf16[64,640]{1,0:T(8,128)(2,1)S(1)} %get-tuple-element.50.refs_4_), channel_id=1, source_target_pairs={{0,2},{1,3},{2,0},{3,1},{4,6},{5,7},{6,4},{7,5},{8,10},{9,11},{10,... | collective-permute-start | bytes 245768 | tf_op jit(solution)/shard_map/ppermute | solution.py:536
  83.9 9.7 %collective-permute-start.15 = (bf16[64,640]{1,0:T(8,128)(2,1)S(1)}, bf16[64,640]{1,0:T(8,128)(2,1)S(1)}, u32[]{:S(2)}, u32[]{:S(2)}) collective-permute-start(bf16[64,640]{1,0:T(8,128)(2,1)S(1)} %get-tuple-element.52), channel_id=1, source_target_pairs={{0,2},{1,3},{2,0},{3,1},{4,6},{5,7},{6,4},{7,5},{8,10},{9,11},{10,... | collective-permute-start | bytes 245768 | tf_op jit(solution)/shard_map/ppermute | solution.py:536
  86.9 6.3 %collective-permute-start.21 = (bf16[32,640]{1,0:T(8,128)(2,1)S(1)}, bf16[32,640]{1,0:T(8,128)(2,1)S(1)}, u32[]{:S(2)}, u32[]{:S(2)}) collective-permute-start(bf16[32,640]{1,0:T(8,128)(2,1)S(1)} %get-tuple-element.49.refs_4_), channel_id=1, source_target_pairs={{0,2},{1,3},{2,0},{3,1},{4,6},{5,7},{6,4},{7,5},{8,10},{9,11},{10,... | collective-permute-start | bytes 122888 | tf_op jit(solution)/shard_map/ppermute | solution.py:536
  87.0 8.3 %collective-permute-start.20 = (bf16[32,640]{1,0:T(8,128)(2,1)S(1)}, bf16[32,640]{1,0:T(8,128)(2,1)S(1)}, u32[]{:S(2)}, u32[]{:S(2)}) collective-permute-start(bf16[32,640]{1,0:T(8,128)(2,1)S(1)} %get-tuple-element.49.refs_4_), channel_id=1, source_target_pairs={{0,1},{1,0},{2,3},{3,2},{4,5},{5,4},{6,7},{7,6},{8,9},{9,8},{10,11... | collective-permute-start | bytes 122888 | tf_op jit(solution)/shard_map/ppermute | solution.py:536
  89.5 12.3 %collective-permute-start.17 = (bf16[64,640]{1,0:T(8,128)(2,1)S(1)}, bf16[64,640]{1,0:T(8,128)(2,1)S(1)}, u32[]{:S(2)}, u32[]{:S(2)}) collective-permute-start(bf16[64,640]{1,0:T(8,128)(2,1)S(1)} %get-tuple-element.50.refs_4_), channel_id=1, source_target_pairs={{0,1},{1,0},{2,3},{3,2},{4,5},{5,4},{6,7},{7,6},{8,9},{9,8},{10,11... | collective-permute-start | bytes 245768 | tf_op jit(solution)/shard_map/ppermute | solution.py:536
  89.6 12.3 %collective-permute-start.19 = (bf16[64,640]{1,0:T(8,128)(2,1)S(1)}, bf16[64,640]{1,0:T(8,128)(2,1)S(1)}, u32[]{:S(2)}, u32[]{:S(2)}) collective-permute-start(bf16[64,640]{1,0:T(8,128)(2,1)S(1)} %collective-permute-done.18.refs_2_), channel_id=1, source_target_pairs={{0,1},{1,0},{2,3},{3,2},{4,5},{5,4},{6,7},{7,6},{8,9},{9,8},{10,11... | collective-permute-start | bytes 245768 | tf_op jit(solution)/shard_map/ppermute | solution.py:536
  93.2 10.7 %collective-permute-start.14 = (bf16[64,640]{1,0:T(8,128)(2,1)S(1)}, bf16[64,640]{1,0:T(8,128)(2,1)S(1)}, u32[]{:S(2)}, u32[]{:S(2)}) collective-permute-start(bf16[64,640]{1,0:T(8,128)(2,1)S(1)} %get-tuple-element.52), channel_id=1, source_target_pairs={{0,1},{1,0},{2,3},{3,2},{4,5},{5,4},{6,7},{7,6},{8,9},{9,8},{10,11... | collective-permute-start | bytes 245768 | tf_op jit(solution)/shard_map/ppermute | solution.py:536
  93.7 10.2 %collective-permute-start.16 = (bf16[64,640]{1,0:T(8,128)(2,1)S(1)}, bf16[64,640]{1,0:T(8,128)(2,1)S(1)}, u32[]{:S(2)}, u32[]{:S(2)}) collective-permute-start(bf16[64,640]{1,0:T(8,128)(2,1)S(1)} %collective-permute-done.15.refs_2_), channel_id=1, source_target_pairs={{0,1},{1,0},{2,3},{3,2},{4,5},{5,4},{6,7},{7,6},{8,9},{9,8},{10,11... | collective-permute-start | bytes 245768 | tf_op jit(solution)/shard_map/ppermute | solution.py:536
  95.3 4.9 %collective-permute-start.22 = (bf16[32,640]{1,0:T(8,128)(2,1)S(1)}, bf16[32,640]{1,0:T(8,128)(2,1)S(1)}, u32[]{:S(2)}, u32[]{:S(2)}) collective-permute-start(bf16[32,640]{1,0:T(8,128)(2,1)S(1)} %collective-permute-done.21.refs_2_), channel_id=1, source_target_pairs={{0,1},{1,0},{2,3},{3,2},{4,5},{5,4},{6,7},{7,6},{8,9},{9,8},{10,11... | collective-permute-start | bytes 122888 | tf_op jit(solution)/shard_map/ppermute | solution.py:536
